TPU v7x, 128 devices: a whole 4x4x4 slice. The times are simulated.
128 devices in a mesh: req: 8 (over y, core), tok: 16 (over x, z).
Axes of the slice: x: 4, y: 4, z: 4, core: 2. Of those that a mesh axis runs over, the one named last changes fastest.
Arguments:
- layer_input: bfloat16 [16384, 2048], P(('req', 'tok')), may hold values from -12 to 12
- q_in: bfloat16 [16384, 2048], P(('req', 'tok')), may hold values from -10 to 10
- k_in: bfloat16 [16384, 2048], P(('req', 'tok')), may hold values from -10 to 10
- v_in: bfloat16 [16384, 2048], P(('req', 'tok')), may hold values from -6 to 6
- segment_ids: int32 [8, 2048], P('req'), may hold values from 0 to 3, never falling along the last dimension, each value on 1 to 1024 neighbouring positions
- lambda_parts: float32 [4, 128], replicated, may hold values from -0.8 to 0.8
- out_weight: bfloat16 [2048, 2048], replicated, may hold values from -0.125 to 0.125
- ffn_gain: float32 [2048], replicated, may hold values from 0.1 to 1.9
- gate_weight: bfloat16 [2048, 5632], P(None, 'req'), may hold values from -0.125 to 0.125
- up_weight: bfloat16 [2048, 5632], P(None, 'req'), may hold values from -0.125 to 0.125
- down_weight: bfloat16 [5632, 2048], P('req'), may hold values from -0.078125 to 0.078125
- next_gain: float32 [2048], replicated, may hold values from 0.1 to 1.9
- qkv_weight: bfloat16 [2048, 6144], P(None, 'req'), may hold values from -0.125 to 0.125
- page_owner: int32 [8, 256], P('req'), may hold values from 0 to 15, as said below
- page_slot: int32 [8, 256], P('req'), may hold values from 0 to 15, as said below
Outputs:
- layer_output: bfloat16 [16384, 2048], P(('req', 'tok'))
- q_next: bfloat16 [16384, 2048], P(('req', 'tok'))
- page_cache: bfloat16 [2048, 8, 4096], P(('req', 'tok'))
Inputs may be any that keep to these rules, and one draw needn't show every extreme that they name: `segment_ids`: segment numbers never fall along a group; each of the 4 prompts of a group has 1 to 1024 tokens, one exactly 1024. `page_owner`: the 16 pages of each device name every device of its request group as owner exactly once. `page_slot`: within a request group every pair of owner and slot is named by exactly one page.
All inputs are finite; a program needn't handle non-finite values.
Results may differ from a plain program's by a relative error of at most 0.017.
Values may be sent and summed in bfloat16 or wider, within the bound.
A program may use at most 192 MiB of HBM per device.

v0:
```python
import math

import jax
import jax.numpy as jnp
from jax import lax
from jax.sharding import PartitionSpec as P

HEADS = 8
PAGE = 8


NEG_FILL = -1e30
LAMBDA_INIT = 0.2
EPSILON = 1e-05


def rms_rows(values):
    return values * lax.rsqrt(jnp.mean(values * values, axis=-1, keepdims=True) + EPSILON)


def lambda_value(lambda_parts):
    first_term = jnp.exp(jnp.sum(lambda_parts[0] * lambda_parts[1]))
    second_term = jnp.exp(jnp.sum(lambda_parts[2] * lambda_parts[3]))
    return first_term - second_term + LAMBDA_INIT


def body(
    layer_input,
    q_in,
    k_in,
    v_in,
    segment_ids,
    lambda_parts,
    out_weight,
    ffn_gain,
    gate_weight,
    up_weight,
    down_weight,
    next_gain,
    qkv_weight,
    page_owner,
    page_slot,
):
    row_count = q_in.shape[0]
    feat_width = q_in.shape[1]
    head_dim = feat_width // (2 * HEADS)
    peer_count = lax.axis_size("tok")
    tok_place = lax.axis_index("tok")
    seg_row = segment_ids[0]
    first_row = tok_place * row_count
    query_places = first_row + jnp.arange(row_count)
    query_segs = lax.dynamic_slice_in_dim(seg_row, first_row, row_count)
    lambda_mix = lambda_value(lambda_parts)
    score_scale = 1.0 / math.sqrt(head_dim)
    query_split = q_in.reshape(row_count, HEADS, 2, head_dim)
    run_max = jnp.full((HEADS, 2, row_count), NEG_FILL, jnp.float32)
    key_rows = lax.all_gather(k_in, "tok", axis=0, tiled=True)
    value_rows = lax.all_gather(v_in, "tok", axis=0, tiled=True)
    piece_len = key_rows.shape[0]
    key_split = key_rows.reshape(piece_len, HEADS, 2, head_dim)
    value_split = value_rows.reshape(piece_len, HEADS, 2 * head_dim)
    key_places = jnp.arange(piece_len)
    visible = (seg_row[None, :] == query_segs[:, None]) & (
        key_places[None, :] <= query_places[:, None]
    )
    scores = (
        jnp.einsum("qhmd,khmd->hmqk", query_split, key_split, preferred_element_type=jnp.float32)
        * score_scale
    )
    scores = jnp.where(visible, scores, NEG_FILL)
    new_max = jnp.maximum(run_max, jnp.max(scores, axis=-1))
    weights = jnp.where(visible, jnp.exp(scores - new_max[..., None]), 0.0)
    totals = jnp.sum(weights, axis=-1)
    weighted = jnp.einsum(
        "hmqk,khe->hmqe",
        weights.astype(jnp.bfloat16),
        value_split,
        preferred_element_type=jnp.float32,
    )
    run_max, totals, weighted = (new_max, totals, weighted)
    map_outputs = weighted / totals[..., None]
    difference = map_outputs[:, 0] - lambda_mix * map_outputs[:, 1]
    head_outputs = rms_rows(difference) * (1.0 - LAMBDA_INIT)
    attention = (
        jnp.transpose(head_outputs, (1, 0, 2)).reshape(row_count, feat_width).astype(jnp.bfloat16)
    )
    residual_mid = (
        layer_input.astype(jnp.float32)
        + jnp.dot(attention, out_weight, preferred_element_type=jnp.float32)
    ).astype(jnp.bfloat16)
    gathered = lax.all_gather(residual_mid, "req", axis=0, tiled=True)
    normed = (rms_rows(gathered.astype(jnp.float32)) * ffn_gain).astype(jnp.bfloat16)
    gate_proj = jnp.dot(normed, gate_weight, preferred_element_type=jnp.float32)
    up_proj = jnp.dot(normed, up_weight, preferred_element_type=jnp.float32)
    hidden = (jax.nn.silu(gate_proj) * up_proj).astype(jnp.bfloat16)
    ffn_own = lax.psum_scatter(
        jnp.dot(hidden, down_weight, preferred_element_type=jnp.float32).astype(jnp.bfloat16),
        "req",
        scatter_dimension=0,
        tiled=True,
    ).astype(jnp.float32)
    layer_output = (residual_mid.astype(jnp.float32) + ffn_own).astype(jnp.bfloat16)
    next_normed = (rms_rows(layer_output.astype(jnp.float32)) * next_gain).astype(jnp.bfloat16)
    projected_cols = jnp.dot(
        lax.all_gather(next_normed, "req", axis=0, tiled=True),
        qkv_weight,
        preferred_element_type=jnp.float32,
    ).astype(jnp.bfloat16)
    projected = lax.all_to_all(projected_cols, "req", split_axis=0, concat_axis=1, tiled=True)
    q_next = projected[:, :feat_width]
    pages_dev = row_count // PAGE
    per_owner = pages_dev // peer_count
    key_values = projected[:, feat_width:].reshape(pages_dev, PAGE, 2 * feat_width)
    owner_all = page_owner[0].reshape(peer_count, pages_dev)
    slot_all = page_slot[0].reshape(peer_count, pages_dev)
    page_numbers = jnp.arange(pages_dev, dtype=jnp.int32)
    my_owners = lax.dynamic_index_in_dim(owner_all, tok_place, 0, keepdims=False)
    send_order = jnp.argsort(my_owners * pages_dev + page_numbers)
    outgoing = key_values[send_order].reshape(peer_count, per_owner, PAGE, 2 * feat_width)
    incoming = lax.all_to_all(outgoing, "tok", split_axis=0, concat_axis=0, tiled=True)
    rank_keys = jnp.where(
        owner_all == tok_place, page_numbers[None, :], pages_dev + page_numbers[None, :]
    )
    chosen_pages = jnp.argsort(rank_keys, axis=1)[:, :per_owner]
    slot_list = jnp.take_along_axis(slot_all, chosen_pages, axis=1).reshape(pages_dev)
    page_cache = (
        jnp.zeros((pages_dev, PAGE, 2 * feat_width), jnp.bfloat16)
        .at[slot_list]
        .set(incoming.reshape(pages_dev, PAGE, 2 * feat_width))
    )
    return (layer_output, q_next, page_cache)


def solution(mesh):
    in_specs = (
        P(("req", "tok"), None),
        P(("req", "tok"), None),
        P(("req", "tok"), None),
        P(("req", "tok"), None),
        P("req", None),
        P(),
        P(),
        P(),
        P(None, "req"),
        P(None, "req"),
        P("req", None),
        P(),
        P(None, "req"),
        P("req", None),
        P("req", None),
    )
    out_specs = (P(("req", "tok"), None), P(("req", "tok"), None), P(("req", "tok"), None, None))
    return jax.shard_map(body, mesh=mesh, in_specs=in_specs, out_specs=out_specs, check_vma=False)
```

profile of v0, /device:TPU:0, one launch (start us, length us, event | category | flops | bytes accessed | tf_op | source)
XLA Modules:
  0.0 395.1 jit_solution(589856986905657744)
XLA Ops:
  7.2 2.2 copy.35
  9.5 2.0 copy.38
  11.6 2.2 reshape.96
  16.2 75.5 %all-gather.5.cloned.1.call-done = bf16[2048,2048]{0,1:T(8,128)(2,1)} async-done(((bf16[128,2048]{0,1:T(8,128)(2,1)}), bf16[2048,2048]{0,1:T(8,128)(2,1)}) %all-gather.5.cloned.1.call-update) | async-done | bytes 8388624 | tf_op jit(solution)/shard_map/all_gather | solution.py:57
  91.7 6.6 %fusion = (f32[8,2,128]{2,1,0:T(2,128)S(1)}, f32[8,2,128,2048]{3,2,1,0:T(8,128)S(1)}) fusion(pred[128,2048]{1,0:T(8,128)(4,1)S(1)} %fusion.24, bf16[2048,8,2,128]{0,3,2,1:T(8,128)(2,1)} %bitcast.49, bf16[128,8,2,128]{3,2,1,0:T(2,128)(2,1)} %reshape.96), kind=kOutput, calls=%fused_computation.5 | convolution fusion | flops 1086322688 | bytes 25960448 | tf_op jit(solution)/shard_map/qhmd,khmd->hmqk/dot_general | solution.py:67
  98.4 5.9 %copy-done.1 = f32[8,2,128,2048]{3,2,1,0:T(8,128)} copy-done((f32[8,2,128,2048]{3,2,1,0:T(8,128)}, f32[8,2,128,2048]{3,2,1,0:T(8,128)S(1)}, u32[]{:S(2)}) %copy-start.1) | copy-done | bytes 16777240
  104.3 5.0 %fusion.1 = f32[8,2,128]{2,1,0:T(2,128)S(1)} fusion(f32[8,2,128,2048]{3,2,1,0:T(8,128)S(1)} %get-tuple-element.12, f32[8,2,128]{2,1,0:T(2,128)S(1)} %broadcast_maximum_fusion, pred[128,2048]{1,0:T(8,128)(4,1)S(1)} %fusion.24), kind=kLoop, calls=%fused_computation.6 | loop fusion | flops 20969472 | bytes 17055744 | tf_op jit(solution)/shard_map/reduce_sum | solution.py:73
  109.3 63.0 %all-gather.7.cloned.1.call-done = bf16[2048,2048]{0,1:T(8,128)(2,1)} async-done(((bf16[128,2048]{0,1:T(8,128)(2,1)}), bf16[2048,2048]{0,1:T(8,128)(2,1)}) %all-gather.7.cloned.1.call-update) | async-done | bytes 8388624 | tf_op jit(solution)/shard_map/all_gather | solution.py:58
  172.3 12.6 %broadcast_divide_fusion = f32[8,2,128,256]{3,2,1,0:T(8,128)S(1)} fusion(f32[8,2,128]{2,1,0:T(2,128)S(1)} %fusion.1, bf16[2048,8,256,1]{0,2,3,1:T(8,128)(2,1)} %bitcast.56, f32[8,2,128,2048]{3,2,1,0:T(8,128)} %copy-done.1, f32[8,2,128]{2,1,0:T(2,128)S(1)} %broadcast_maximum_fusion, pred[128,2048]{1,0:T(8,128)(4,1)S(1)} %fusion.24), kind=kOutput, calls=%fused_computation.37 | convolution fusion | flops 2168979456 | bytes 27541504 | tf_op jit(solution)/shard_map/hmqk,khe->hmqe/dot_general | solution.py:74
  185.1 1.1 fusion.25
  186.2 2.0 copy.40
  188.3 5.7 %fusion.13 = bf16[128,2048]{1,0:T(8,128)(2,1)} fusion(bf16[128,2048]{0,1:T(8,128)(2,1)} %bitcast.53, bf16[2048,2048]{1,0:T(8,128)(2,1)} %param.21, bf16[128,2048]{1,0:T(8,128)(2,1)} %param.15), kind=kOutput, calls=%fused_computation.22 | convolution fusion | flops 1074528256 | bytes 9961472 | tf_op jit(solution)/shard_map/dot_general | solution.py:89
  194.2 31.3 %all-gather.9.cloned.1.call-done = bf16[1024,2048]{1,0:T(8,128)(2,1)} async-done(((bf16[128,2048]{1,0:T(8,128)(2,1)}), bf16[1024,2048]{1,0:T(8,128)(2,1)}) %all-gather.9.cloned.1.call-update) | async-done | bytes 4194320 | tf_op jit(solution)/shard_map/all_gather | solution.py:91
  225.5 3.2 fusion.3
  228.9 6.7 %fusion.15 = f32[1024,704]{0,1:T(8,128)} fusion(bf16[2048,704]{0,1:T(8,128)(2,1)} %param.23, bf16[1024,2048]{1,0:T(8,128)(2,1)S(1)} %copy-done.3, f32[2048]{0:T(1024)S(1)} %copy-done.10, f32[1024]{0:T(1024)S(1)} %add_rsqrt_fusion), kind=kOutput, calls=%fused_computation.26 | convolution fusion | flops 2961178624 | bytes 9973760 | tf_op jit(solution)/shard_map/dot_general | solution.py:93
  235.7 12.4 %convolution_convert_fusion = bf16[1024,2048]{1,0:T(8,128)(2,1)} fusion(bf16[704,2048]{1,0:T(8,128)(2,1)} %param.25, f32[1024,704]{0,1:T(8,128)} %fusion.15, bf16[2048,704]{0,1:T(8,128)(2,1)} %param.24, bf16[1024,2048]{1,0:T(8,128)(2,1)} %all-gather.9.cloned.1.call-done, f32[2048]{0:T(1024)S(1)} %copy-done.10, f32[1024]{0:T(1024)S(1)} %add_rsqrt_fusion), kind=kOutput, calls=%fused_computation.19 | convolution fusion | flops 5920391168 | bytes 17051648 | tf_op jit(solution)/shard_map/dot_general | solution.py:97
  248.1 37.9 %reduce-scatter.2.cloned.1.call-done = bf16[128,2048]{1,0:T(8,128)(2,1)} async-done(((bf16[1024,2048]{1,0:T(8,128)(2,1)}), bf16[128,2048]{1,0:T(8,128)(2,1)}) %reduce-scatter.2.cloned.1.call-update) | async-done | bytes 524304 | tf_op jit(solution)/shard_map/reduce_scatter | solution.py:96
  286.0 1.5 fusion.19
  289.3 31.2 %all-gather.11.cloned.1.call-done = bf16[1024,2048]{1,0:T(8,128)(2,1)} async-done(((bf16[128,2048]{1,0:T(8,128)(2,1)}), bf16[1024,2048]{1,0:T(8,128)(2,1)}) %all-gather.11.cloned.1.call-update) | async-done | bytes 4194320 | tf_op jit(solution)/shard_map/all_gather | solution.py:105
  320.4 6.8 %convolution_convert_fusion.1 = bf16[1024,768]{1,0:T(8,128)(2,1)} fusion(bf16[1024,2048]{1,0:T(8,128)(2,1)} %all-gather.11.cloned.1.call-done, bf16[2048,768]{1,0:T(8,128)(2,1)S(1)} %copy-done), kind=kOutput, calls=%fused_computation.23 | convolution fusion | flops 3222011904 | bytes 8912896 | tf_op jit(solution)/shard_map/dot_general | solution.py:104
  327.2 4.3 %all-to-all-start = ((bf16[8,128,768]{2,1,0:T(8,128)(2,1)}), bf16[8,128,768]{2,1,0:T(8,128)(2,1)}, u32[]{:S(2)}, u32[]{:S(2)}) async-start(bf16[8,128,768]{2,1,0:T(8,128)(2,1)} %bitcast.54), calls=%async_computation.1 | async-start | bytes 3145728 | tf_op jit(solution)/shard_map/all_to_all | solution.py:109
  333.6 1.2 sort.35
  334.9 18.2 %all-to-all-done = bf16[8,128,768]{2,1,0:T(8,128)(2,1)} async-done(((bf16[8,128,768]{2,1,0:T(8,128)(2,1)}), bf16[8,128,768]{2,1,0:T(8,128)(2,1)}, u32[]{:S(2)}, u32[]{:S(2)}) %all-to-all-start) | async-done | bytes 1572896 | tf_op jit(solution)/shard_map/all_to_all | solution.py:109
  353.1 1.6 copy.47
  354.7 1.1 copy-done.2
  355.8 1.0 slice_bitcast_fusion
  356.9 2.8 gather_fusion
  359.7 7.0 %all-to-all-start.1 = ((bf16[16,1,8,4096]{3,2,1,0:T(8,128)(2,1)}), bf16[16,1,8,4096]{3,2,1,0:T(8,128)(2,1)}, u32[]{:S(2)}, u32[]{:S(2)}) async-start(bf16[16,1,8,4096]{3,2,1,0:T(8,128)(2,1)} %bitcast.52), calls=%async_computation.2 | async-start | bytes 2097152 | tf_op jit(solution)/shard_map/all_to_all | solution.py:120
  368.2 1.9 slice.42
  370.1 14.1 %all-to-all-done.1 = bf16[16,1,8,4096]{3,2,1,0:T(8,128)(2,1)} async-done(((bf16[16,1,8,4096]{3,2,1,0:T(8,128)(2,1)}), bf16[16,1,8,4096]{3,2,1,0:T(8,128)(2,1)}, u32[]{:S(2)}, u32[]{:S(2)}) %all-to-all-start.1) | async-done | bytes 1048608 | tf_op jit(solution)/shard_map/all_to_all | solution.py:120
  384.1 1.1 broadcast_in_dim.54
  385.2 3.4 scatter_fusion
  (60 shorter events, 7.4 us)
Async XLA Ops:
  7.2 313.3 %copy-start = (bf16[2048,768]{1,0:T(8,128)(2,1)S(1)}, bf16[2048,768]{1,0:T(8,128)(2,1)}, u32[]{:S(2)}) copy-start(bf16[2048,768]{1,0:T(8,128)(2,1)} %param.27) | copy-start | bytes 9437188
  7.2 6.7 %copy-start.7 = (f32[4,128]{1,0:T(4,128)S(1)}, f32[4,128]{1,0:T(4,128)}, u32[]{:S(2)}) copy-start(f32[4,128]{1,0:T(4,128)} %param.20) | copy-start | bytes 6148
  7.2 8.6 %copy-start.6 = (s32[1,2048]{1,0:T(1,128)S(1)}, s32[1,2048]{1,0:T(1,128)}, u32[]{:S(2)}) copy-start(s32[1,2048]{1,0:T(1,128)} %param.19) | copy-start | bytes 24580
  7.2 84.5 %all-gather.5.cloned.1.call-start = ((), (), s32[]{:S(2)}) async-start(), calls=%async_computation.3 | async-start | bytes 8912896 | tf_op jit(solution)/shard_map/all_gather | solution.py:57
  9.5 162.8 %all-gather.7.cloned.1.call-start = ((), (), s32[]{:S(2)}) async-start(), calls=%async_computation.4 | async-start | bytes 8912896 | tf_op jit(solution)/shard_map/all_gather | solution.py:58
  11.6 213.9 %all-gather.9.cloned.1.call-start = ((), (), s32[]{:S(2)}) async-start(), calls=%async_computation.5 | async-start | bytes 4718592 | tf_op jit(solution)/shard_map/all_gather | solution.py:91
  98.4 5.9 %copy-start.1 = (f32[8,2,128,2048]{3,2,1,0:T(8,128)}, f32[8,2,128,2048]{3,2,1,0:T(8,128)S(1)}, u32[]{:S(2)}) copy-start(f32[8,2,128,2048]{3,2,1,0:T(8,128)S(1)} %get-tuple-element.12) | copy-start | bytes 50331652
  193.9 34.8 %copy-start.10 = (f32[2048]{0:T(1024)S(1)}, f32[2048]{0:T(1024)}, u32[]{:S(2)}) copy-start(f32[2048]{0:T(1024)} %param.22) | copy-start | bytes 24580
  193.9 92.0 %reduce-scatter.2.cloned.1.call-start = ((), (), s32[]{:S(2)}) async-start(), calls=%async_computation.6 | async-start | bytes 4718592 | tf_op jit(solution)/shard_map/reduce_scatter | solution.py:96
  225.5 3.4 copy-start.3
  248.1 40.2 %copy-start.5 = (f32[2048]{0:T(1024)S(1)}, f32[2048]{0:T(1024)}, u32[]{:S(2)}) copy-start(f32[2048]{0:T(1024)} %param.26) | copy-start | bytes 24580
  248.1 72.4 %all-gather.11.cloned.1.call-start = ((), (), s32[]{:S(2)}) async-start(), calls=%async_computation.7 | async-start | bytes 4718592 | tf_op jit(solution)/shard_map/all_gather | solution.py:105
  287.5 0.8 copy-start.4
  289.3 42.8 %copy-start.8 = (s32[1,256]{1,0:T(1,128)S(1)}, s32[1,256]{1,0:T(1,128)}, u32[]{:S(2)}) copy-start(s32[1,256]{1,0:T(1,128)} %param.28) | copy-start | bytes 3076
  289.3 43.6 %copy-start.9 = (s32[1,256]{1,0:T(1,128)S(1)}, s32[1,256]{1,0:T(1,128)}, u32[]{:S(2)}) copy-start(s32[1,256]{1,0:T(1,128)} %param.29) | copy-start | bytes 3076
  327.2 25.9 %all-to-all-start = ((bf16[8,128,768]{2,1,0:T(8,128)(2,1)}), bf16[8,128,768]{2,1,0:T(8,128)(2,1)}, u32[]{:S(2)}, u32[]{:S(2)}) async-start(bf16[8,128,768]{2,1,0:T(8,128)(2,1)} %bitcast.54), calls=%async_computation.1 | async-start | bytes 3145728 | tf_op jit(solution)/shard_map/all_to_all | solution.py:109
  354.7 1.2 copy-start.2
  359.7 24.4 %all-to-all-start.1 = ((bf16[16,1,8,4096]{3,2,1,0:T(8,128)(2,1)}), bf16[16,1,8,4096]{3,2,1,0:T(8,128)(2,1)}, u32[]{:S(2)}, u32[]{:S(2)}) async-start(bf16[16,1,8,4096]{3,2,1,0:T(8,128)(2,1)} %bitcast.52), calls=%async_computation.2 | async-start | bytes 2097152 | tf_op jit(solution)/shard_map/all_to_all | solution.py:120
Sparse Core Ops, SparseCore 0:
  10.7 80.9 all-gather.4
  94.4 77.8 all-gather.6
  194.1 31.3 all-gather.8
  248.2 37.7 reduce-scatter.1
  289.4 31.0 all-gather.10
where the time goes:
time: 396 us; the launch traced here: 395 us
  waiting for transfers between devices  271 us (68%)
  matrix products  50.8 us (13%)
  local copies, waits for them, and re-layouts  29.8 us (8%)
  other arithmetic  16.5 us (4%)
  between operations  15.3 us (4%)
  starting transfers between devices  11.7 us (3%)
    all_gather x1, waiting for transfers between devices, body(): key_rows = lax.all_gather(k_in, 'tok', axis=0, tiled=True)  75.5 us
    all_gather x1, waiting for transfers between devices, body(): value_rows = lax.all_gather(v_in, 'tok', axis=0, tiled=True)  63 us
    reduce_scatter x1, waiting for transfers between devices, body(): lax.psum_scatter(jnp.dot(hidden, down_weight, preferred_element_type=jnp....  37.9 us
    all_gather x1, waiting for transfers between devices, body(): gathered = lax.all_gather(residual_mid, 'req', axis=0, tiled=True)  31.3 us
    all_gather x1, waiting for transfers between devices, body(): lax.all_gather(next_normed, 'req', axis=0, tiled=True)  31.2 us
    all_to_all x1, waiting for transfers between devices, body(): lax.all_to_all(projected_cols, 'req', split_axis=0, concat_axis=1, tiled=...  18.2 us
    all_to_all x1, waiting for transfers between devices, body(): lax.all_to_all(outgoing, 'tok', split_axis=0, concat_axis=0, tiled=True)  14.1 us
    unnamed x26, local copies, waits for them, and re-layouts  12.8 us
  transfers between devices with their start and end apart: 7, of which 7 were waited for; matrix products, arithmetic and copies ran while one was open for 6% of the time, Pallas kernels for 0%

commit v1 on v0

--- a/solution.py
+++ b/solution.py
@@ -12,6 +12,7 @@
 NEG_FILL = -1e30
 LAMBDA_INIT = 0.2
 EPSILON = 1e-05
+MAX_SEG = 1024
 
 
 def rms_rows(values):
@@ -54,14 +55,25 @@
     score_scale = 1.0 / math.sqrt(head_dim)
     query_split = q_in.reshape(row_count, HEADS, 2, head_dim)
     run_max = jnp.full((HEADS, 2, row_count), NEG_FILL, jnp.float32)
-    key_rows = lax.all_gather(k_in, "tok", axis=0, tiled=True)
-    value_rows = lax.all_gather(v_in, "tok", axis=0, tiled=True)
-    piece_len = key_rows.shape[0]
+    back = -(-(MAX_SEG - 1) // row_count)
+    own_kv = jnp.concatenate([k_in, v_in], axis=1)
+    pieces = []
+    for shift in range(back, 0, -1):
+        pairs = [(src_i, src_i + shift) for src_i in range(peer_count - shift)]
+        pieces.append(lax.ppermute(own_kv, "tok", perm=pairs))
+    pieces.append(own_kv)
+    window = jnp.concatenate(pieces, axis=0)
+    piece_len = window.shape[0]
+    key_rows = window[:, :feat_width]
+    value_rows = window[:, feat_width:]
     key_split = key_rows.reshape(piece_len, HEADS, 2, head_dim)
     value_split = value_rows.reshape(piece_len, HEADS, 2 * head_dim)
-    key_places = jnp.arange(piece_len)
-    visible = (seg_row[None, :] == query_segs[:, None]) & (
-        key_places[None, :] <= query_places[:, None]
+    key_places = (tok_place - back) * row_count + jnp.arange(piece_len)
+    key_segs = jnp.take(seg_row, jnp.clip(key_places, 0, seg_row.shape[0] - 1))
+    visible = (
+        (key_places[None, :] >= 0)
+        & (key_segs[None, :] == query_segs[:, None])
+        & (key_places[None, :] <= query_places[:, None])
     )
     scores = (
         jnp.einsum("qhmd,khmd->hmqk", query_split, key_split, preferred_element_type=jnp.float32)

time: 396 us -> 438 us (1.11)
  starting transfers between devices: 11.7 us -> 44.4 us
  local copies, waits for them, and re-layouts: 29.8 us -> 53.4 us
  waiting for transfers between devices: 271 us -> 263 us
  matrix products: 50.8 us -> 43.6 us
    all_gather x2 -> x0, waiting for transfers between devices: 138 us -> none  [the longest x1 75.5 us: body(): key_rows = lax.all_gather(k_in, 'tok', axis=0, tiled=True)]
    all_gather x1, waiting for transfers between devices: 31.3 us -> 97.9 us  [body(): gathered = lax.all_gather(residual_mid, 'req', axis=0, tiled=True)]
    ppermute x0 -> x8, waiting for transfers between devices: none -> 63.6 us  [body(): pieces.append(lax.ppermute(own_kv, 'tok', perm=pairs))]
    ppermute x0 -> x8, starting transfers between devices: none -> 32.8 us  [body(): pieces.append(lax.ppermute(own_kv, 'tok', perm=pairs))]
    unnamed x26 -> x38, local copies, waits for them, and re-layouts: 12.8 us -> 23.2 us
    slice x0 -> x1, local copies, waits for them, and re-layouts: none -> 6.77 us  [body(): value_rows = window[:, feat_width:]]
    gather x0 -> x1, local copies, waits for them, and re-layouts: none -> 6.48 us  [body(): key_segs = jnp.take(seg_row, jnp.clip(key_places, 0, seg_row.shape[0] - 1))]
  transfers between devices with their start and end apart: 7 -> 13, of which waited for: 7 -> 9; matrix products, arithmetic and copies ran while one was open for 6% -> 7% of each run, Pallas kernels for 0% -> 0%
where the time goes in v1:
time: 438 us; the launch traced here: 437 us
  waiting for transfers between devices  263 us (60%)
  local copies, waits for them, and re-layouts  53.4 us (12%)
  starting transfers between devices  44.4 us (10%)
  matrix products  43.6 us (10%)
  other arithmetic  17.7 us (4%)
  between operations  15.4 us (4%)
    all_gather x1, waiting for transfers between devices, body(): gathered = lax.all_gather(residual_mid, 'req', axis=0, tiled=True)  97.9 us
    ppermute x8, waiting for transfers between devices, body(): pieces.append(lax.ppermute(own_kv, 'tok', perm=pairs))  63.6 us
    reduce_scatter x1, waiting for transfers between devices, body(): lax.psum_scatter(jnp.dot(hidden, down_weight, preferred_element_type=jnp....  37.9 us
    ppermute x8, starting transfers between devices, body(): pieces.append(lax.ppermute(own_kv, 'tok', perm=pairs))  32.8 us
    all_gather x1, waiting for transfers between devices, body(): lax.all_gather(next_normed, 'req', axis=0, tiled=True)  31.2 us
    unnamed x38, local copies, waits for them, and re-layouts  23.2 us
    all_to_all x1, waiting for transfers between devices, body(): lax.all_to_all(projected_cols, 'req', split_axis=0, concat_axis=1, tiled=...  18.2 us
    all_to_all x1, waiting for transfers between devices, body(): lax.all_to_all(outgoing, 'tok', split_axis=0, concat_axis=0, tiled=True)  14.1 us
  transfers between devices with their start and end apart: 13, of which 9 were waited for; matrix products, arithmetic and copies ran while one was open for 7% of the time, Pallas kernels for 0%

profile of v1, /device:TPU:0, one launch (start us, length us, event | category | flops | bytes accessed | tf_op | source)
XLA Modules:
  0.0 437.3 jit_solution(304008285303600586)
XLA Ops:
  13.7 6.0 %collective-permute-start = (bf16[128,4096]{0,1:T(8,128)(2,1)}, bf16[128,4096]{0,1:T(8,128)(2,1)}, u32[]{:S(2)}, u32[]{:S(2)}) collective-permute-start(bf16[128,4096]{0,1:T(8,128)(2,1)} %pad_maximum_fusion), channel_id=1, source_target_pairs={{0,8},{1,9},{2,10},{3,11},{4,12},{5,13},{6,14},{7,15},{16,24},{17,... | collective-permute-start | bytes 3145736 | tf_op jit(solution)/shard_map/ppermute | solution.py:63
  19.7 7.0 %collective-permute-start.1 = (bf16[128,4096]{0,1:T(8,128)(2,1)}, bf16[128,4096]{0,1:T(8,128)(2,1)}, u32[]{:S(2)}, u32[]{:S(2)}) collective-permute-start(bf16[128,4096]{0,1:T(8,128)(2,1)} %pad_maximum_fusion), channel_id=1, source_target_pairs={{0,7},{1,8},{2,9},{3,10},{4,11},{5,12},{6,13},{7,14},{8,15},{16,23... | collective-permute-start | bytes 3145736 | tf_op jit(solution)/shard_map/ppermute | solution.py:63
  33.6 6.5 %gather_fusion = s32[1152]{0:T(1024)S(1)} fusion(s32[2048]{0:T(1024)S(1)} %bitcast.62, s32[2048]{0:T(1024)S(1)} %pad_clamp_fusion), kind=kCustom, calls=%fused_computation | custom fusion | bytes 13824 | tf_op jit(solution)/shard_map/jit(_take)/gather | solution.py:72
  45.4 3.2 collective-permute-start.5
  48.6 2.4 constant_dynamic-update-slice_fusion.8
  51.0 14.2 %collective-permute-done.1 = bf16[128,4096]{0,1:T(8,128)(2,1)} collective-permute-done((bf16[128,4096]{0,1:T(8,128)(2,1)}, bf16[128,4096]{0,1:T(8,128)(2,1)}, u32[]{:S(2)}, u32[]{:S(2)}) %collective-permute-start.1) | collective-permute-done | bytes 1048608 | tf_op jit(solution)/shard_map/ppermute | solution.py:63
  65.1 5.8 %collective-permute-start.6 = (bf16[128,4096]{0,1:T(8,128)(2,1)}, bf16[128,4096]{0,1:T(8,128)(2,1)S(1)}, u32[]{:S(2)}, u32[]{:S(2)}) collective-permute-start(bf16[128,4096]{0,1:T(8,128)(2,1)} %pad_maximum_fusion), channel_id=1, source_target_pairs={{0,2},{1,3},{2,4},{3,5},{4,6},{5,7},{6,8},{7,9},{8,10},{9,11},{10,... | collective-permute-start | bytes 3145736 | tf_op jit(solution)/shard_map/ppermute | solution.py:63
  70.9 2.3 constant_dynamic-update-slice_fusion.7
  73.3 14.4 %collective-permute-done.2 = bf16[128,4096]{0,1:T(8,128)(2,1)} collective-permute-done((bf16[128,4096]{0,1:T(8,128)(2,1)}, bf16[128,4096]{0,1:T(8,128)(2,1)}, u32[]{:S(2)}, u32[]{:S(2)}) %collective-permute-start.2) | collective-permute-done | bytes 1048608 | tf_op jit(solution)/shard_map/ppermute | solution.py:63
  87.6 4.0 collective-permute-start.7
  91.7 2.4 constant_dynamic-update-slice_fusion.6
  94.0 16.1 %collective-permute-done.3 = bf16[128,4096]{0,1:T(8,128)(2,1)} collective-permute-done((bf16[128,4096]{0,1:T(8,128)(2,1)}, bf16[128,4096]{0,1:T(8,128)(2,1)}, u32[]{:S(2)}, u32[]{:S(2)}) %collective-permute-start.3) | collective-permute-done | bytes 1048608 | tf_op jit(solution)/shard_map/ppermute | solution.py:63
  110.1 2.4 constant_dynamic-update-slice_fusion.5
  112.5 19.0 %collective-permute-done.4 = bf16[128,4096]{0,1:T(8,128)(2,1)} collective-permute-done((bf16[128,4096]{0,1:T(8,128)(2,1)}, bf16[128,4096]{0,1:T(8,128)(2,1)}, u32[]{:S(2)}, u32[]{:S(2)}) %collective-permute-start.4) | collective-permute-done | bytes 1048608 | tf_op jit(solution)/shard_map/ppermute | solution.py:63
  131.4 2.4 constant_dynamic-update-slice_fusion.4
  138.3 6.8 %fusion.37 = (bf16[1152,2048]{0,1:T(8,128)(2,1)}, bf16[1152,2048]{0,1:T(8,128)(2,1)S(1)}) fusion(bf16[1152,4096]{0,1:T(8,128)(2,1)} %constant_dynamic-update-slice_fusion), kind=kLoop, calls=%fused_computation.84 | loop fusion | bytes 18874368 | tf_op jit(solution)/shard_map/slice | solution.py:68
  145.1 2.5 fusion.3
  151.2 8.3 %broadcast_divide_fusion = f32[8,2,128,256]{3,2,1,0:T(8,128)S(1)} fusion(f32[8,2,128]{2,1,0:T(2,128)S(1)} %fusion.4, bf16[1152,8,256,1]{0,2,3,1:T(8,128)(2,1)} %bitcast.66, f32[8,2,1152,128]{3,2,1,0:T(8,128)} %copy-done.2, f32[8,2,128]{2,1,0:T(2,128)S(1)} %broadcast_maximum_fusion, pred[128,1152]{0,1:T(8,128)(4,1)S(1)} %compare_and_fusion), kind=kOutput, calls=%fused_computation.39 | convolution fusion | flops 1220280320 | bytes 16416768 | tf_op jit(solution)/shard_map/hmqk,khe->hmqe/dot_general | solution.py:86
  162.9 5.7 %fusion.13 = bf16[128,2048]{1,0:T(8,128)(2,1)} fusion(bf16[128,2048]{0,1:T(8,128)(2,1)} %bitcast.68, bf16[2048,2048]{1,0:T(8,128)(2,1)} %param.21, bf16[128,2048]{1,0:T(8,128)(2,1)} %param.15), kind=kOutput, calls=%fused_computation.23 | convolution fusion | flops 1074528256 | bytes 9961472 | tf_op jit(solution)/shard_map/dot_general | solution.py:101
  168.8 97.9 %all-gather.3.cloned.1.call-done = bf16[1024,2048]{1,0:T(8,128)(2,1)} async-done(((bf16[128,2048]{1,0:T(8,128)(2,1)}), bf16[1024,2048]{1,0:T(8,128)(2,1)}) %all-gather.3.cloned.1.call-update) | async-done | bytes 4194320 | tf_op jit(solution)/shard_map/all_gather | solution.py:103
  266.7 3.1 fusion
  269.8 8.0 %fusion.15 = f32[1024,704]{0,1:T(8,128)} fusion(bf16[2048,704]{0,1:T(8,128)(2,1)} %param.23, bf16[1024,2048]{1,0:T(8,128)(2,1)} %all-gather.3.cloned.1.call-done, f32[2048]{0:T(1024)S(1)} %copy-done.12, f32[1024]{0:T(1024)S(1)} %add_rsqrt_fusion), kind=kOutput, calls=%fused_computation.27 | convolution fusion | flops 2961178624 | bytes 9973760 | tf_op jit(solution)/shard_map/dot_general | solution.py:105
  277.8 12.4 %convolution_convert_fusion = bf16[1024,2048]{1,0:T(8,128)(2,1)} fusion(bf16[704,2048]{1,0:T(8,128)(2,1)} %param.25, f32[1024,704]{0,1:T(8,128)} %fusion.15, bf16[2048,704]{0,1:T(8,128)(2,1)} %param.24, bf16[1024,2048]{1,0:T(8,128)(2,1)} %all-gather.3.cloned.1.call-done, f32[2048]{0:T(1024)S(1)} %copy-done.12, f32[1024]{0:T(1024)S(1)} %add_rsqrt_fusion), kind=kOutput, calls=%fused_computation.20 | convolution fusion | flops 5920391168 | bytes 17051648 | tf_op jit(solution)/shard_map/dot_general | solution.py:109
  290.3 37.9 %reduce-scatter.2.cloned.1.call-done = bf16[128,2048]{1,0:T(8,128)(2,1)} async-done(((bf16[1024,2048]{1,0:T(8,128)(2,1)}), bf16[128,2048]{1,0:T(8,128)(2,1)}) %reduce-scatter.2.cloned.1.call-update) | async-done | bytes 524304 | tf_op jit(solution)/shard_map/reduce_scatter | solution.py:108
  331.4 31.2 %all-gather.5.cloned.1.call-done = bf16[1024,2048]{1,0:T(8,128)(2,1)} async-done(((bf16[128,2048]{1,0:T(8,128)(2,1)}), bf16[1024,2048]{1,0:T(8,128)(2,1)}) %all-gather.5.cloned.1.call-update) | async-done | bytes 4194320 | tf_op jit(solution)/shard_map/all_gather | solution.py:117
  362.6 6.8 %convolution_convert_fusion.1 = bf16[1024,768]{1,0:T(8,128)(2,1)} fusion(bf16[1024,2048]{1,0:T(8,128)(2,1)} %all-gather.5.cloned.1.call-done, bf16[2048,768]{1,0:T(8,128)(2,1)S(1)} %copy-done), kind=kOutput, calls=%fused_computation.24 | convolution fusion | flops 3222011904 | bytes 8912896 | tf_op jit(solution)/shard_map/dot_general | solution.py:116
  369.4 4.3 all-to-all-start
  377.0 18.2 %all-to-all-done = bf16[8,128,768]{2,1,0:T(8,128)(2,1)} async-done(((bf16[8,128,768]{2,1,0:T(8,128)(2,1)}), bf16[8,128,768]{2,1,0:T(8,128)(2,1)}, u32[]{:S(2)}, u32[]{:S(2)}) %all-to-all-start) | async-done | bytes 1572896 | tf_op jit(solution)/shard_map/all_to_all | solution.py:121
  399.0 2.8 gather_fusion.1
  401.8 7.0 %all-to-all-start.1 = ((bf16[16,1,8,4096]{3,2,1,0:T(8,128)(2,1)}), bf16[16,1,8,4096]{3,2,1,0:T(8,128)(2,1)}, u32[]{:S(2)}, u32[]{:S(2)}) async-start(bf16[16,1,8,4096]{3,2,1,0:T(8,128)(2,1)} %bitcast.67), calls=%async_computation.2 | async-start | bytes 2097152 | tf_op jit(solution)/shard_map/all_to_all | solution.py:132
  412.2 14.1 %all-to-all-done.1 = bf16[16,1,8,4096]{3,2,1,0:T(8,128)(2,1)} async-done(((bf16[16,1,8,4096]{3,2,1,0:T(8,128)(2,1)}), bf16[16,1,8,4096]{3,2,1,0:T(8,128)(2,1)}, u32[]{:S(2)}, u32[]{:S(2)}) %all-to-all-start.1) | async-done | bytes 1048608 | tf_op jit(solution)/shard_map/all_to_all | solution.py:132
  427.4 3.4 scatter_fusion
  (90 shorter events, 43.9 us)
Async XLA Ops:
  7.2 355.4 %copy-start = (bf16[2048,768]{1,0:T(8,128)(2,1)S(1)}, bf16[2048,768]{1,0:T(8,128)(2,1)}, u32[]{:S(2)}) copy-start(bf16[2048,768]{1,0:T(8,128)(2,1)} %param.27) | copy-start | bytes 9437188
  7.2 26.4 %copy-start.1 = (s32[1,2048]{1,0:T(1,128)S(1)}, s32[1,2048]{1,0:T(1,128)}, u32[]{:S(2)}) copy-start(s32[1,2048]{1,0:T(1,128)} %param.19) | copy-start | bytes 24580
  7.2 259.5 %all-gather.3.cloned.1.call-start = ((), (), s32[]{:S(2)}) async-start(), calls=%async_computation.3 | async-start | bytes 4718592 | tf_op jit(solution)/shard_map/all_gather | solution.py:103
  13.7 31.7 %collective-permute-start = (bf16[128,4096]{0,1:T(8,128)(2,1)}, bf16[128,4096]{0,1:T(8,128)(2,1)}, u32[]{:S(2)}, u32[]{:S(2)}) collective-permute-start(bf16[128,4096]{0,1:T(8,128)(2,1)} %pad_maximum_fusion), channel_id=1, source_target_pairs={{0,8},{1,9},{2,10},{3,11},{4,12},{5,13},{6,14},{7,15},{16,24},{17,... | collective-permute-start | bytes 3145736 | tf_op jit(solution)/shard_map/ppermute | solution.py:63
  19.7 45.4 %collective-permute-start.1 = (bf16[128,4096]{0,1:T(8,128)(2,1)}, bf16[128,4096]{0,1:T(8,128)(2,1)}, u32[]{:S(2)}, u32[]{:S(2)}) collective-permute-start(bf16[128,4096]{0,1:T(8,128)(2,1)} %pad_maximum_fusion), channel_id=1, source_target_pairs={{0,7},{1,8},{2,9},{3,10},{4,11},{5,12},{6,13},{7,14},{8,15},{16,23... | collective-permute-start | bytes 3145736 | tf_op jit(solution)/shard_map/ppermute | solution.py:63
  26.7 60.9 %collective-permute-start.2 = (bf16[128,4096]{0,1:T(8,128)(2,1)}, bf16[128,4096]{0,1:T(8,128)(2,1)}, u32[]{:S(2)}, u32[]{:S(2)}) collective-permute-start(bf16[128,4096]{0,1:T(8,128)(2,1)} %pad_maximum_fusion), channel_id=1, source_target_pairs={{0,6},{1,7},{2,8},{3,9},{4,10},{5,11},{6,12},{7,13},{8,14},{9,15},... | collective-permute-start | bytes 3145736 | tf_op jit(solution)/shard_map/ppermute | solution.py:63
  29.0 81.2 %collective-permute-start.3 = (bf16[128,4096]{0,1:T(8,128)(2,1)}, bf16[128,4096]{0,1:T(8,128)(2,1)}, u32[]{:S(2)}, u32[]{:S(2)}) collective-permute-start(bf16[128,4096]{0,1:T(8,128)(2,1)} %pad_maximum_fusion), channel_id=1, source_target_pairs={{0,5},{1,6},{2,7},{3,8},{4,9},{5,10},{6,11},{7,12},{8,13},{9,14},{... | collective-permute-start | bytes 3145736 | tf_op jit(solution)/shard_map/ppermute | solution.py:63
  31.2 100.2 %collective-permute-start.4 = (bf16[128,4096]{0,1:T(8,128)(2,1)}, bf16[128,4096]{0,1:T(8,128)(2,1)}, u32[]{:S(2)}, u32[]{:S(2)}) collective-permute-start(bf16[128,4096]{0,1:T(8,128)(2,1)} %pad_maximum_fusion), channel_id=1, source_target_pairs={{0,4},{1,5},{2,6},{3,7},{4,8},{5,9},{6,10},{7,11},{8,12},{9,13},{1... | collective-permute-start | bytes 3145736 | tf_op jit(solution)/shard_map/ppermute | solution.py:63
  33.6 9.8 %copy-start.9 = (f32[4,128]{1,0:T(4,128)S(1)}, f32[4,128]{1,0:T(4,128)}, u32[]{:S(2)}) copy-start(f32[4,128]{1,0:T(4,128)} %param.20) | copy-start | bytes 6148
  45.4 88.4 %collective-permute-start.5 = (bf16[128,4096]{0,1:T(8,128)(2,1)}, bf16[128,4096]{0,1:T(8,128)(2,1)S(1)}, u32[]{:S(2)}, u32[]{:S(2)}) collective-permute-start(bf16[128,4096]{0,1:T(8,128)(2,1)} %pad_maximum_fusion), channel_id=1, source_target_pairs={{0,3},{1,4},{2,5},{3,6},{4,7},{5,8},{6,9},{7,10},{8,11},{9,12},{10... | collective-permute-start | bytes 3145736 | tf_op jit(solution)/shard_map/ppermute | solution.py:63
  65.1 69.8 %collective-permute-start.6 = (bf16[128,4096]{0,1:T(8,128)(2,1)}, bf16[128,4096]{0,1:T(8,128)(2,1)S(1)}, u32[]{:S(2)}, u32[]{:S(2)}) collective-permute-start(bf16[128,4096]{0,1:T(8,128)(2,1)} %pad_maximum_fusion), channel_id=1, source_target_pairs={{0,2},{1,3},{2,4},{3,5},{4,6},{5,7},{6,8},{7,9},{8,10},{9,11},{10,... | collective-permute-start | bytes 3145736 | tf_op jit(solution)/shard_map/ppermute | solution.py:63
  87.6 48.4 %collective-permute-start.7 = (bf16[128,4096]{0,1:T(8,128)(2,1)}, bf16[128,4096]{0,1:T(8,128)(2,1)S(1)}, u32[]{:S(2)}, u32[]{:S(2)}) collective-permute-start(bf16[128,4096]{0,1:T(8,128)(2,1)} %pad_maximum_fusion), channel_id=1, source_target_pairs={{0,1},{1,2},{2,3},{3,4},{4,5},{5,6},{6,7},{7,8},{8,9},{9,10},{10,1... | collective-permute-start | bytes 3145736 | tf_op jit(solution)/shard_map/ppermute | solution.py:63
  112.5 24.7 %copy-start.4 = (bf16[128,2048]{0,1:T(8,128)(2,1)S(1)}, bf16[128,2048]{0,1:T(8,128)(2,1)}, u32[]{:S(2)}) copy-start(bf16[128,2048]{0,1:T(8,128)(2,1)} %copy.38) | copy-start | bytes 1572868
  112.5 24.7 %copy-start.5 = (bf16[128,2048]{0,1:T(8,128)(2,1)S(1)}, bf16[128,2048]{0,1:T(8,128)(2,1)}, u32[]{:S(2)}) copy-start(bf16[128,2048]{0,1:T(8,128)(2,1)} %copy.39) | copy-start | bytes 1572868
  138.3 6.8 %copy-start.6 = (bf16[128,8,2,128]{3,2,1,0:T(2,128)(2,1)S(1)}, bf16[128,8,2,128]{3,2,1,0:T(2,128)(2,1)}, u32[]{:S(2)}) copy-start(bf16[128,8,2,128]{3,2,1,0:T(2,128)(2,1)} %reshape.141) | copy-start | bytes 1572868
  147.6 3.6 copy-start.2
  168.5 101.3 %copy-start.12 = (f32[2048]{0:T(1024)S(1)}, f32[2048]{0:T(1024)}, u32[]{:S(2)}) copy-start(f32[2048]{0:T(1024)} %param.22) | copy-start | bytes 24580
  168.5 159.6 %reduce-scatter.2.cloned.1.call-start = ((), (), s32[]{:S(2)}) async-start(), calls=%async_computation.4 | async-start | bytes 4718592 | tf_op jit(solution)/shard_map/reduce_scatter | solution.py:108
  290.2 40.2 %copy-start.8 = (f32[2048]{0:T(1024)S(1)}, f32[2048]{0:T(1024)}, u32[]{:S(2)}) copy-start(f32[2048]{0:T(1024)} %param.26) | copy-start | bytes 24580
  290.2 72.4 %all-gather.5.cloned.1.call-start = ((), (), s32[]{:S(2)}) async-start(), calls=%async_computation.5 | async-start | bytes 4718592 | tf_op jit(solution)/shard_map/all_gather | solution.py:117
  329.6 0.8 copy-start.7
  331.4 42.8 %copy-start.10 = (s32[1,256]{1,0:T(1,128)S(1)}, s32[1,256]{1,0:T(1,128)}, u32[]{:S(2)}) copy-start(s32[1,256]{1,0:T(1,128)} %param.28) | copy-start | bytes 3076
  331.4 43.6 %copy-start.11 = (s32[1,256]{1,0:T(1,128)S(1)}, s32[1,256]{1,0:T(1,128)}, u32[]{:S(2)}) copy-start(s32[1,256]{1,0:T(1,128)} %param.29) | copy-start | bytes 3076
  369.4 25.9 %all-to-all-start = ((bf16[8,128,768]{2,1,0:T(8,128)(2,1)}), bf16[8,128,768]{2,1,0:T(8,128)(2,1)}, u32[]{:S(2)}, u32[]{:S(2)}) async-start(bf16[8,128,768]{2,1,0:T(8,128)(2,1)} %bitcast.69), calls=%async_computation.1 | async-start | bytes 3145728 | tf_op jit(solution)/shard_map/all_to_all | solution.py:121
  396.8 1.2 copy-start.3
  401.8 24.4 %all-to-all-start.1 = ((bf16[16,1,8,4096]{3,2,1,0:T(8,128)(2,1)}), bf16[16,1,8,4096]{3,2,1,0:T(8,128)(2,1)}, u32[]{:S(2)}, u32[]{:S(2)}) async-start(bf16[16,1,8,4096]{3,2,1,0:T(8,128)(2,1)} %bitcast.67), calls=%async_computation.2 | async-start | bytes 2097152 | tf_op jit(solution)/shard_map/all_to_all | solution.py:132
Sparse Core Ops, SparseCore 0:
  168.7 98.0 all-gather.2
  290.4 37.7 reduce-scatter.1
  331.5 31.0 all-gather.4

commit v2 on v1

--- a/solution.py
+++ b/solution.py
@@ -3,6 +3,7 @@
 import jax
 import jax.numpy as jnp
 from jax import lax
+from jax.sharding import Mesh
 from jax.sharding import PartitionSpec as P
 
 HEADS = 8
@@ -13,6 +14,8 @@
 LAMBDA_INIT = 0.2
 EPSILON = 1e-05
 MAX_SEG = 1024
+TOK = ("tx", "tz")
+REQ = ("ry", "rc")
 
 
 def rms_rows(values):
@@ -23,6 +26,11 @@
     first_term = jnp.exp(jnp.sum(lambda_parts[0] * lambda_parts[1]))
     second_term = jnp.exp(jnp.sum(lambda_parts[2] * lambda_parts[3]))
     return first_term - second_term + LAMBDA_INIT
+
+
+def gather_rows(rows):
+    across = lax.all_gather(rows, "ry", axis=0, tiled=True)
+    return lax.all_gather(across, "rc", axis=0, tiled=True)
 
 
 def body(
@@ -45,8 +53,8 @@
     row_count = q_in.shape[0]
     feat_width = q_in.shape[1]
     head_dim = feat_width // (2 * HEADS)
-    peer_count = lax.axis_size("tok")
-    tok_place = lax.axis_index("tok")
+    peer_count = lax.axis_size(TOK)
+    tok_place = lax.axis_index(TOK)
     seg_row = segment_ids[0]
     first_row = tok_place * row_count
     query_places = first_row + jnp.arange(row_count)
@@ -57,12 +65,11 @@
     run_max = jnp.full((HEADS, 2, row_count), NEG_FILL, jnp.float32)
     back = -(-(MAX_SEG - 1) // row_count)
     own_kv = jnp.concatenate([k_in, v_in], axis=1)
-    pieces = []
-    for shift in range(back, 0, -1):
-        pairs = [(src_i, src_i + shift) for src_i in range(peer_count - shift)]
-        pieces.append(lax.ppermute(own_kv, "tok", perm=pairs))
-    pieces.append(own_kv)
-    window = jnp.concatenate(pieces, axis=0)
+    all_kv = lax.all_gather(own_kv, TOK, axis=0, tiled=True)
+    padded_kv = jnp.concatenate(
+        [jnp.zeros((back * row_count, 2 * feat_width), all_kv.dtype), all_kv], axis=0
+    )
+    window = lax.dynamic_slice_in_dim(padded_kv, first_row, (back + 1) * row_count, 0)
     piece_len = window.shape[0]
     key_rows = window[:, :feat_width]
     value_rows = window[:, feat_width:]
@@ -100,25 +107,28 @@
         layer_input.astype(jnp.float32)
         + jnp.dot(attention, out_weight, preferred_element_type=jnp.float32)
     ).astype(jnp.bfloat16)
-    gathered = lax.all_gather(residual_mid, "req", axis=0, tiled=True)
+    gathered = gather_rows(residual_mid)
     normed = (rms_rows(gathered.astype(jnp.float32)) * ffn_gain).astype(jnp.bfloat16)
     gate_proj = jnp.dot(normed, gate_weight, preferred_element_type=jnp.float32)
     up_proj = jnp.dot(normed, up_weight, preferred_element_type=jnp.float32)
     hidden = (jax.nn.silu(gate_proj) * up_proj).astype(jnp.bfloat16)
-    ffn_own = lax.psum_scatter(
-        jnp.dot(hidden, down_weight, preferred_element_type=jnp.float32).astype(jnp.bfloat16),
-        "req",
-        scatter_dimension=0,
-        tiled=True,
-    ).astype(jnp.float32)
+    partial = jnp.dot(hidden, down_weight, preferred_element_type=jnp.float32).astype(jnp.bfloat16)
+    partial = lax.psum_scatter(partial, "rc", scatter_dimension=0, tiled=True)
+    ffn_own = lax.psum_scatter(partial, "ry", scatter_dimension=0, tiled=True).astype(jnp.float32)
     layer_output = (residual_mid.astype(jnp.float32) + ffn_own).astype(jnp.bfloat16)
     next_normed = (rms_rows(layer_output.astype(jnp.float32)) * next_gain).astype(jnp.bfloat16)
     projected_cols = jnp.dot(
-        lax.all_gather(next_normed, "req", axis=0, tiled=True),
+        gather_rows(next_normed),
         qkv_weight,
         preferred_element_type=jnp.float32,
     ).astype(jnp.bfloat16)
-    projected = lax.all_to_all(projected_cols, "req", split_axis=0, concat_axis=1, tiled=True)
+    n_rc = lax.axis_size("rc")
+    n_ry = lax.axis_size("ry")
+    col_w = projected_cols.shape[1]
+    blocks = projected_cols.reshape(n_rc, n_ry, row_count, col_w)
+    blocks = lax.all_to_all(blocks, "rc", 0, 0, tiled=True)
+    blocks = lax.all_to_all(blocks, "ry", 1, 1, tiled=True)
+    projected = jnp.transpose(blocks, (2, 1, 0, 3)).reshape(row_count, n_ry * n_rc * col_w)
     q_next = projected[:, :feat_width]
     pages_dev = row_count // PAGE
     per_owner = pages_dev // peer_count
@@ -129,7 +139,7 @@
     my_owners = lax.dynamic_index_in_dim(owner_all, tok_place, 0, keepdims=False)
     send_order = jnp.argsort(my_owners * pages_dev + page_numbers)
     outgoing = key_values[send_order].reshape(peer_count, per_owner, PAGE, 2 * feat_width)
-    incoming = lax.all_to_all(outgoing, "tok", split_axis=0, concat_axis=0, tiled=True)
+    incoming = lax.all_to_all(outgoing, TOK, split_axis=0, concat_axis=0, tiled=True)
     rank_keys = jnp.where(
         owner_all == tok_place, page_numbers[None, :], pages_dev + page_numbers[None, :]
     )
@@ -144,22 +154,29 @@
 
 
 def solution(mesh):
+    n_req, n_tok = mesh.devices.shape
+    cores = 2
+    lanes = 4
+    fine = Mesh(
+        mesh.devices.reshape(n_req // cores, cores, n_tok // lanes, lanes), ("ry", "rc", "tx", "tz")
+    )
+    rows = P(REQ + TOK, None)
     in_specs = (
-        P(("req", "tok"), None),
-        P(("req", "tok"), None),
-        P(("req", "tok"), None),
-        P(("req", "tok"), None),
-        P("req", None),
+        rows,
+        rows,
+        rows,
+        rows,
+        P(REQ, None),
         P(),
         P(),
         P(),
-        P(None, "req"),
-        P(None, "req"),
-        P("req", None),
+        P(None, REQ),
+        P(None, REQ),
+        P(REQ, None),
         P(),
-        P(None, "req"),
-        P("req", None),
-        P("req", None),
+        P(None, REQ),
+        P(REQ, None),
+        P(REQ, None),
     )
-    out_specs = (P(("req", "tok"), None), P(("req", "tok"), None), P(("req", "tok"), None, None))
-    return jax.shard_map(body, mesh=mesh, in_specs=in_specs, out_specs=out_specs, check_vma=False)
+    out_specs = (rows, rows, P(REQ + TOK, None, None))
+    return jax.shard_map(body, mesh=fine, in_specs=in_specs, out_specs=out_specs, check_vma=False)

time: 438 us -> 425 us (0.970)
  starting transfers between devices: 44.4 us -> 11.9 us
  waiting for transfers between devices: 263 us -> 290 us
  local copies, waits for them, and re-layouts: 53.4 us -> 43.3 us
  blocking collectives: 0 us -> 5 us
    all_gather x2 -> x5, waiting for transfers between devices: 129 us -> 211 us  [the longest x1 112 us: body(): all_kv = lax.all_gather(own_kv, TOK, axis=0, tiled=True)]
    ppermute x8 -> x0, waiting for transfers between devices: 63.6 us -> none  [body(): pieces.append(lax.ppermute(own_kv, 'tok', perm=pairs))]
    ppermute x8 -> x0, starting transfers between devices: 32.8 us -> none  [body(): pieces.append(lax.ppermute(own_kv, 'tok', perm=pairs))]
    unnamed x38 -> x27, local copies, waits for them, and re-layouts: 23.2 us -> 9.14 us
    reduce_scatter x1 -> x2, waiting for transfers between devices: 37.9 us -> 49.7 us  [the longest x1 33.4 us: body(): lax.psum_scatter(partial, 'ry', scatter_dimension=0, tiled=True)]
    all_to_all x0 -> x1, blocking collectives: none -> 5 us  [body(): blocks = lax.all_to_all(blocks, 'rc', 0, 0, tiled=True)]
    slice x0 -> x2, local copies, waits for them, and re-layouts: none -> 4.52 us  [body(): projected[:, feat_width:].reshape(pages_dev, PAGE, 2 * feat_width)]
  transfers between devices with their start and end apart: 13 -> 9, of which waited for: 9 -> 9; matrix products, arithmetic and copies ran while one was open for 7% -> 5% of each run, Pallas kernels for 0% -> 0%
where the time goes in v2:
time: 425 us; the launch traced here: 424 us
  waiting for transfers between devices  290 us (68%)
  local copies, waits for them, and re-layouts  43.3 us (10%)
  matrix products  41.1 us (10%)
  other arithmetic  16.7 us (4%)
  between operations  15.7 us (4%)
  starting transfers between devices  11.9 us (3%)
  blocking collectives  5 us (1%)
    all_gather x1, waiting for transfers between devices, body(): all_kv = lax.all_gather(own_kv, TOK, axis=0, tiled=True)  112 us
    all_gather x2, waiting for transfers between devices, gather_rows(): across = lax.all_gather(rows, 'ry', axis=0, tiled=True)  63.4 us
    all_gather x2, waiting for transfers between devices, gather_rows(): return lax.all_gather(across, 'rc', axis=0, tiled=True)  35.8 us
    reduce_scatter x1, waiting for transfers between devices, body(): lax.psum_scatter(partial, 'ry', scatter_dimension=0, tiled=True)  33.4 us
    all_to_all x1, waiting for transfers between devices, body(): blocks = lax.all_to_all(blocks, 'ry', 1, 1, tiled=True)  17.9 us
    reduce_scatter x1, waiting for transfers between devices, body(): partial = lax.psum_scatter(partial, 'rc', scatter_dimension=0, tiled=True)  16.3 us
    dot_general x1, matrix products, body(): jnp.dot(hidden, down_weight, preferred_element_type=jnp.float32)  12.5 us
    all_to_all x1, waiting for transfers between devices, body(): lax.all_to_all(outgoing, TOK, split_axis=0, concat_axis=0, tiled=True)  11.5 us
  transfers between devices with their start and end apart: 9, of which 9 were waited for; matrix products, arithmetic and copies ran while one was open for 5% of the time, Pallas kernels for 0%

profile of v2, /device:TPU:0, one launch (start us, length us, event | category | flops | bytes accessed | tf_op | source)
XLA Modules:
  0.0 424.2 jit_solution(14550294573071543669)
XLA Ops:
  7.2 2.2 copy.71
  11.5 2.2 pad_maximum_fusion
  13.8 2.2 reshape.144
  18.0 6.5 %gather_fusion = s32[1152]{0:T(1024)S(1)} fusion(s32[2048]{0:T(1024)S(1)} %bitcast.65, s32[2048]{0:T(1024)S(1)} %pad_clamp_fusion), kind=kCustom, calls=%fused_computation | custom fusion | bytes 13824 | tf_op jit(solution)/shard_map/jit(_take)/gather | solution.py:79
  25.6 112.0 %all-gather.6.cloned.1.call-done = bf16[2048,4096]{0,1:T(8,128)(2,1)} async-done(((bf16[128,4096]{0,1:T(8,128)(2,1)}), bf16[2048,4096]{0,1:T(8,128)(2,1)}) %all-gather.6.cloned.1.call-update) | async-done | bytes 16777232 | tf_op jit(solution)/shard_map/all_gather | solution.py:68
  137.5 5.1 %pad_dynamic-slice_fusion.1 = (bf16[1152,2048]{0,1:T(8,128)(2,1)}, bf16[1152,2048]{0,1:T(8,128)(2,1)S(1)}) fusion(s32[]{:T(128)S(6)} %select_n.70, s32[]{:T(128)S(6)} %add.187, bf16[2048,4096]{0,1:T(8,128)(2,1)} %all-gather.6.cloned.1.call-done), kind=kLoop, calls=%fused_computation.5 | loop fusion | bytes 26214408 | tf_op jit(solution)/shard_map/slice | solution.py:75
  142.6 2.5 fusion.3
  145.1 2.3 fusion.4
  148.7 8.3 %broadcast_divide_fusion = f32[8,2,128,256]{3,2,1,0:T(8,128)S(1)} fusion(f32[8,2,128]{2,1,0:T(2,128)S(1)} %fusion.4, bf16[1152,8,256,1]{0,2,3,1:T(8,128)(2,1)} %bitcast.69, f32[8,2,1152,128]{3,2,1,0:T(8,128)} %copy-done.2, f32[8,2,128]{2,1,0:T(2,128)S(1)} %broadcast_maximum_fusion, pred[128,1152]{0,1:T(8,128)(4,1)S(1)} %compare_and_fusion), kind=kOutput, calls=%fused_computation.40 | convolution fusion | flops 1220280320 | bytes 16416768 | tf_op jit(solution)/shard_map/hmqk,khe->hmqe/dot_general | solution.py:93
  158.3 2.0 copy.77
  160.3 5.7 %fusion.13 = bf16[128,2048]{1,0:T(8,128)(2,1)} fusion(bf16[128,2048]{0,1:T(8,128)(2,1)} %bitcast.72, bf16[2048,2048]{1,0:T(8,128)(2,1)} %param.21, bf16[128,2048]{1,0:T(8,128)(2,1)} %param.15), kind=kOutput, calls=%fused_computation.25 | convolution fusion | flops 1074528256 | bytes 9961472 | tf_op jit(solution)/shard_map/dot_general | solution.py:108
  166.1 32.8 %all-gather.8.cloned.1.call-done = bf16[512,2048]{1,0:T(8,128)(2,1)} async-done(((bf16[128,2048]{1,0:T(8,128)(2,1)}), bf16[512,2048]{1,0:T(8,128)(2,1)}) %all-gather.8.cloned.1.call-update) | async-done | bytes 2097168 | tf_op jit(solution)/shard_map/all_gather | solution.py:32
  199.1 17.8 %all-gather.10.cloned.1.call-done = bf16[1024,2048]{1,0:T(8,128)(2,1)} async-done(((bf16[512,2048]{1,0:T(8,128)(2,1)}), bf16[1024,2048]{1,0:T(8,128)(2,1)}) %all-gather.10.cloned.1.call-update) | async-done | bytes 4194320 | tf_op jit(solution)/shard_map/all_gather | solution.py:33
  216.9 3.2 fusion
  220.3 6.7 %fusion.15 = f32[1024,704]{0,1:T(8,128)} fusion(bf16[2048,704]{0,1:T(8,128)(2,1)} %param.23, bf16[1024,2048]{1,0:T(8,128)(2,1)S(1)} %copy-done.3, f32[2048]{0:T(1024)S(1)} %copy-done.10, f32[1024]{0:T(1024)S(1)} %add_rsqrt_fusion), kind=kOutput, calls=%fused_computation.29 | convolution fusion | flops 2961178624 | bytes 9973760 | tf_op jit(solution)/shard_map/dot_general | solution.py:112
  227.0 12.5 %convolution_convert_fusion = bf16[1024,2048]{1,0:T(8,128)(2,1)} fusion(bf16[704,2048]{1,0:T(8,128)(2,1)} %param.25, f32[1024,704]{0,1:T(8,128)} %fusion.15, bf16[2048,704]{0,1:T(8,128)(2,1)} %param.24, bf16[1024,2048]{1,0:T(8,128)(2,1)} %all-gather.10.cloned.1.call-done, f32[2048]{0:T(1024)S(1)} %copy-done.10, f32[1024]{0:T(1024)S(1)} %add_rsqrt_fusion), kind=kOutput, calls=%fused_computation.22 | convolution fusion | flops 5920391168 | bytes 17051648 | tf_op jit(solution)/shard_map/dot_general | solution.py:115
  239.6 16.3 %reduce-scatter.3.cloned.1.call-done = bf16[512,2048]{1,0:T(8,128)(2,1)} async-done(((bf16[1024,2048]{1,0:T(8,128)(2,1)}), bf16[512,2048]{1,0:T(8,128)(2,1)}) %reduce-scatter.3.cloned.1.call-update) | async-done | bytes 2097168 | tf_op jit(solution)/shard_map/reduce_scatter | solution.py:116
  255.9 33.4 %reduce-scatter.5.cloned.1.call-done = bf16[128,2048]{1,0:T(8,128)(2,1)} async-done(((bf16[512,2048]{1,0:T(8,128)(2,1)}), bf16[128,2048]{1,0:T(8,128)(2,1)}) %reduce-scatter.5.cloned.1.call-update) | async-done | bytes 524304 | tf_op jit(solution)/shard_map/reduce_scatter | solution.py:117
  292.7 30.7 %all-gather.12.cloned.1.call-done = bf16[512,2048]{1,0:T(8,128)(2,1)} async-done(((bf16[128,2048]{1,0:T(8,128)(2,1)}), bf16[512,2048]{1,0:T(8,128)(2,1)}) %all-gather.12.cloned.1.call-update) | async-done | bytes 2097168 | tf_op jit(solution)/shard_map/all_gather | solution.py:32
  323.4 18.0 %all-gather.14.cloned.1.call-done = bf16[1024,2048]{1,0:T(8,128)(2,1)} async-done(((bf16[512,2048]{1,0:T(8,128)(2,1)}), bf16[1024,2048]{1,0:T(8,128)(2,1)}) %all-gather.14.cloned.1.call-update) | async-done | bytes 4194320 | tf_op jit(solution)/shard_map/all_gather | solution.py:33
  341.4 5.6 %convolution_convert_fusion.1 = bf16[1024,768]{1,0:T(8,128)(2,1)S(1)} fusion(bf16[1024,2048]{1,0:T(8,128)(2,1)} %all-gather.14.cloned.1.call-done, bf16[2048,768]{1,0:T(8,128)(2,1)S(1)} %copy-done), kind=kOutput, calls=%fused_computation.26 | convolution fusion | flops 3222011904 | bytes 8912896 | tf_op jit(solution)/shard_map/dot_general | solution.py:120
  347.0 5.0 %all_to_all.15 = bf16[2,4,128,768]{3,2,1,0:T(8,128)(2,1)S(1)} all-to-all(bf16[2,4,128,768]{3,2,1,0:T(8,128)(2,1)S(1)} %bitcast.73), channel_id=1, replica_groups=mesh['ry'=4,'rc'=2,'tx'=4,'tz'=4] {'rc'}, dimensions={0} | all-to-all | bytes 3145728 | tf_op jit(solution)/shard_map/all_to_all | solution.py:129
  353.3 4.4 %all-to-all-start.1 = ((bf16[2,4,128,768]{3,2,0,1:T(8,128)(2,1)}), bf16[2,4,128,768]{3,2,0,1:T(8,128)(2,1)}, u32[]{:S(2)}, u32[]{:S(2)}) async-start(bf16[2,4,128,768]{3,2,0,1:T(8,128)(2,1)} %copy.78), calls=%async_computation.3 | async-start | bytes 3145728 | tf_op jit(solution)/shard_map/all_to_all | solution.py:130
  361.0 17.9 %all-to-all-done.1 = bf16[2,4,128,768]{3,2,0,1:T(8,128)(2,1)} async-done(((bf16[2,4,128,768]{3,2,0,1:T(8,128)(2,1)}), bf16[2,4,128,768]{3,2,0,1:T(8,128)(2,1)}, u32[]{:S(2)}, u32[]{:S(2)}) %all-to-all-start.1) | async-done | bytes 1572896 | tf_op jit(solution)/shard_map/all_to_all | solution.py:130
  379.0 2.6 copy.79
  381.6 2.3 slice.53
  383.8 2.3 copy.81
  386.1 2.8 gather_fusion.1
  388.9 7.1 %all-to-all-start.2 = ((bf16[16,1,8,4096]{3,2,1,0:T(8,128)(2,1)}), bf16[16,1,8,4096]{3,2,1,0:T(8,128)(2,1)}, u32[]{:S(2)}, u32[]{:S(2)}) async-start(bf16[16,1,8,4096]{3,2,1,0:T(8,128)(2,1)} %bitcast.70), calls=%async_computation.4 | async-start | bytes 2097152 | tf_op jit(solution)/shard_map/all_to_all | solution.py:142
  399.4 2.0 copy.83
  401.4 11.5 %all-to-all-done.2 = bf16[16,1,8,4096]{3,2,1,0:T(8,128)(2,1)} async-done(((bf16[16,1,8,4096]{3,2,1,0:T(8,128)(2,1)}), bf16[16,1,8,4096]{3,2,1,0:T(8,128)(2,1)}, u32[]{:S(2)}, u32[]{:S(2)}) %all-to-all-start.2) | async-done | bytes 1048608 | tf_op jit(solution)/shard_map/all_to_all | solution.py:142
  414.0 3.4 scatter_fusion
  (77 shorter events, 19.5 us)
Async XLA Ops:
  7.2 334.2 %copy-start = (bf16[2048,768]{1,0:T(8,128)(2,1)S(1)}, bf16[2048,768]{1,0:T(8,128)(2,1)}, u32[]{:S(2)}) copy-start(bf16[2048,768]{1,0:T(8,128)(2,1)} %param.27) | copy-start | bytes 9437188
  7.2 8.8 %copy-start.7 = (f32[4,128]{1,0:T(4,128)S(1)}, f32[4,128]{1,0:T(4,128)}, u32[]{:S(2)}) copy-start(f32[4,128]{1,0:T(4,128)} %param.20) | copy-start | bytes 6148
  7.2 10.8 %copy-start.1 = (s32[1,2048]{1,0:T(1,128)S(1)}, s32[1,2048]{1,0:T(1,128)}, u32[]{:S(2)}) copy-start(s32[1,2048]{1,0:T(1,128)} %param.19) | copy-start | bytes 24580
  7.2 130.3 %all-gather.6.cloned.1.call-start = ((), (), s32[]{:S(2)}) async-start(), calls=%async_computation.5 | async-start | bytes 17825792 | tf_op jit(solution)/shard_map/all_gather | solution.py:68
  13.7 185.1 %all-gather.8.cloned.1.call-start = ((), (), s32[]{:S(2)}) async-start(), calls=%async_computation.6 | async-start | bytes 2621440 | tf_op jit(solution)/shard_map/all_gather | solution.py:32
  137.5 5.1 %copy-start.4 = (bf16[128,8,2,128]{3,2,1,0:T(2,128)(2,1)S(1)}, bf16[128,8,2,128]{3,2,1,0:T(2,128)(2,1)}, u32[]{:S(2)}) copy-start(bf16[128,8,2,128]{3,2,1,0:T(2,128)(2,1)} %reshape.144) | copy-start | bytes 1572868
  145.1 3.6 copy-start.2
  166.0 54.1 %copy-start.10 = (f32[2048]{0:T(1024)S(1)}, f32[2048]{0:T(1024)}, u32[]{:S(2)}) copy-start(f32[2048]{0:T(1024)} %param.22) | copy-start | bytes 24580
  166.0 50.9 %all-gather.10.cloned.1.call-start = ((), (), s32[]{:S(2)}) async-start(), calls=%async_computation.7 | async-start | bytes 6291456 | tf_op jit(solution)/shard_map/all_gather | solution.py:33
  198.9 57.0 %reduce-scatter.3.cloned.1.call-start = ((), (), s32[]{:S(2)}) async-start(), calls=%async_computation.8 | async-start | bytes 6291456 | tf_op jit(solution)/shard_map/reduce_scatter | solution.py:116
  216.9 3.4 copy-start.3
  239.5 52.1 %copy-start.6 = (f32[2048]{0:T(1024)S(1)}, f32[2048]{0:T(1024)}, u32[]{:S(2)}) copy-start(f32[2048]{0:T(1024)} %param.26) | copy-start | bytes 24580
  239.5 49.8 %reduce-scatter.5.cloned.1.call-start = ((), (), s32[]{:S(2)}) async-start(), calls=%async_computation.9 | async-start | bytes 2621440 | tf_op jit(solution)/shard_map/reduce_scatter | solution.py:117
  255.9 67.5 %all-gather.12.cloned.1.call-start = ((), (), s32[]{:S(2)}) async-start(), calls=%async_computation.10 | async-start | bytes 2621440 | tf_op jit(solution)/shard_map/all_gather | solution.py:32
  290.8 0.8 copy-start.5
  292.6 48.7 %all-gather.14.cloned.1.call-start = ((), (), s32[]{:S(2)}) async-start(), calls=%async_computation.11 | async-start | bytes 6291456 | tf_op jit(solution)/shard_map/all_gather | solution.py:33
  347.0 11.2 %copy-start.8 = (s32[1,256]{1,0:T(1,128)S(1)}, s32[1,256]{1,0:T(1,128)}, u32[]{:S(2)}) copy-start(s32[1,256]{1,0:T(1,128)} %param.28) | copy-start | bytes 3076
  347.0 12.0 %copy-start.9 = (s32[1,256]{1,0:T(1,128)S(1)}, s32[1,256]{1,0:T(1,128)}, u32[]{:S(2)}) copy-start(s32[1,256]{1,0:T(1,128)} %param.29) | copy-start | bytes 3076
  353.3 25.7 %all-to-all-start.1 = ((bf16[2,4,128,768]{3,2,0,1:T(8,128)(2,1)}), bf16[2,4,128,768]{3,2,0,1:T(8,128)(2,1)}, u32[]{:S(2)}, u32[]{:S(2)}) async-start(bf16[2,4,128,768]{3,2,0,1:T(8,128)(2,1)} %copy.78), calls=%async_computation.3 | async-start | bytes 3145728 | tf_op jit(solution)/shard_map/all_to_all | solution.py:130
  388.9 24.1 %all-to-all-start.2 = ((bf16[16,1,8,4096]{3,2,1,0:T(8,128)(2,1)}), bf16[16,1,8,4096]{3,2,1,0:T(8,128)(2,1)}, u32[]{:S(2)}, u32[]{:S(2)}) async-start(bf16[16,1,8,4096]{3,2,1,0:T(8,128)(2,1)} %bitcast.70), calls=%async_computation.4 | async-start | bytes 2097152 | tf_op jit(solution)/shard_map/all_to_all | solution.py:142
Sparse Core Ops, SparseCore 0:
  13.9 123.6 all-gather.5
  166.1 32.6 all-gather.7
  200.5 16.3 all-gather.9
  239.6 16.1 reduce-scatter.2
  258.2 31.0 reduce-scatter.4
  292.7 30.5 all-gather.11
  325.0 16.3 all-gather.13

commit v3 on v1

--- a/solution.py
+++ b/solution.py
@@ -57,12 +57,11 @@
     run_max = jnp.full((HEADS, 2, row_count), NEG_FILL, jnp.float32)
     back = -(-(MAX_SEG - 1) // row_count)
     own_kv = jnp.concatenate([k_in, v_in], axis=1)
-    pieces = []
-    for shift in range(back, 0, -1):
-        pairs = [(src_i, src_i + shift) for src_i in range(peer_count - shift)]
-        pieces.append(lax.ppermute(own_kv, "tok", perm=pairs))
-    pieces.append(own_kv)
-    window = jnp.concatenate(pieces, axis=0)
+    all_kv = lax.all_gather(own_kv, "tok", axis=0, tiled=True)
+    padded_kv = jnp.concatenate(
+        [jnp.zeros((back * row_count, 2 * feat_width), all_kv.dtype), all_kv], axis=0
+    )
+    window = lax.dynamic_slice_in_dim(padded_kv, first_row, (back + 1) * row_count, 0)
     piece_len = window.shape[0]
     key_rows = window[:, :feat_width]
     value_rows = window[:, feat_width:]

time: 438 us -> 370 us (0.84)
  starting transfers between devices: 44.4 us -> 11.6 us
  local copies, waits for them, and re-layouts: 53.4 us -> 36.7 us
  waiting for transfers between devices: 263 us -> 247 us
    all_gather x0 -> x1, waiting for transfers between devices: none -> 112 us  [body(): all_kv = lax.all_gather(own_kv, 'tok', axis=0, tiled=True)]
    all_gather x1, waiting for transfers between devices: 97.9 us -> 33.9 us  [body(): gathered = lax.all_gather(residual_mid, 'req', axis=0, tiled=True)]
    ppermute x8 -> x0, waiting for transfers between devices: 63.6 us -> none  [body(): pieces.append(lax.ppermute(own_kv, 'tok', perm=pairs))]
    ppermute x8 -> x0, starting transfers between devices: 32.8 us -> none  [body(): pieces.append(lax.ppermute(own_kv, 'tok', perm=pairs))]
    unnamed x38 -> x28, local copies, waits for them, and re-layouts: 23.2 us -> 8.25 us
  transfers between devices with their start and end apart: 13 -> 6, of which waited for: 9 -> 6; matrix products, arithmetic and copies ran while one was open for 7% -> 5% of each run, Pallas kernels for 0% -> 0%
where the time goes in v3:
time: 370 us
  waiting for transfers between devices  247 us (67%)
  matrix products  42.3 us (11%)
  local copies, waits for them, and re-layouts  36.7 us (10%)
  other arithmetic  16.7 us (5%)
  between operations  15.3 us (4%)
  starting transfers between devices  11.6 us (3%)
    all_gather x1, waiting for transfers between devices, body(): all_kv = lax.all_gather(own_kv, 'tok', axis=0, tiled=True)  112 us
    reduce_scatter x1, waiting for transfers between devices, body(): lax.psum_scatter(jnp.dot(hidden, down_weight, preferred_element_type=jnp....  37.9 us
    all_gather x1, waiting for transfers between devices, body(): gathered = lax.all_gather(residual_mid, 'req', axis=0, tiled=True)  33.9 us
    all_gather x1, waiting for transfers between devices, body(): lax.all_gather(next_normed, 'req', axis=0, tiled=True)  31.2 us
    all_to_all x1, waiting for transfers between devices, body(): lax.all_to_all(projected_cols, 'req', split_axis=0, concat_axis=1, tiled=...  18.2 us
    all_to_all x1, waiting for transfers between devices, body(): lax.all_to_all(outgoing, 'tok', split_axis=0, concat_axis=0, tiled=True)  14.1 us
    dot_general x1, matrix products, body(): jnp.dot(hidden, down_weight, preferred_element_type=jnp.float32)  12.4 us
    dot_general x1, matrix products, body(): jnp.einsum('hmqk,khe->hmqe', weights.astype(jnp.bfloat16), value_split, p...  8.27 us
  transfers between devices with their start and end apart: 6, of which 6 were waited for; matrix products, arithmetic and copies ran while one was open for 5% of the time, Pallas kernels for 0%

profile of v3, /device:TPU:0, one launch (start us, length us, event | category | flops | bytes accessed | tf_op | source)
XLA Modules:
  0.0 369.7 jit_solution(3113207393178205079)
XLA Ops:
  7.2 2.2 copy.38
  9.4 2.0 copy.39
  11.5 2.2 pad_maximum_fusion
  13.8 2.2 reshape.141
  18.0 6.5 %gather_fusion = s32[1152]{0:T(1024)S(1)} fusion(s32[2048]{0:T(1024)S(1)} %bitcast.64, s32[2048]{0:T(1024)S(1)} %pad_clamp_fusion), kind=kCustom, calls=%fused_computation | custom fusion | bytes 13824 | tf_op jit(solution)/shard_map/jit(_take)/gather | solution.py:71
  25.6 112.0 %all-gather.4.cloned.1.call-done = bf16[2048,4096]{0,1:T(8,128)(2,1)} async-done(((bf16[128,4096]{0,1:T(8,128)(2,1)}), bf16[2048,4096]{0,1:T(8,128)(2,1)}) %all-gather.4.cloned.1.call-update) | async-done | bytes 16777232 | tf_op jit(solution)/shard_map/all_gather | solution.py:60
  137.5 5.1 %pad_dynamic-slice_fusion.1 = (bf16[1152,2048]{0,1:T(8,128)(2,1)}, bf16[1152,2048]{0,1:T(8,128)(2,1)S(1)}) fusion(s32[]{:T(128)S(6)} %select_n.70, s32[]{:T(128)S(6)} %add.181, bf16[2048,4096]{0,1:T(8,128)(2,1)} %all-gather.4.cloned.1.call-done), kind=kLoop, calls=%fused_computation.5 | loop fusion | bytes 26214408 | tf_op jit(solution)/shard_map/slice | solution.py:67
  142.6 2.5 fusion.3
  145.1 2.3 fusion.4
  147.4 1.3 copy-done.2
  148.7 8.3 %broadcast_divide_fusion = f32[8,2,128,256]{3,2,1,0:T(8,128)S(1)} fusion(f32[8,2,128]{2,1,0:T(2,128)S(1)} %fusion.4, bf16[1152,8,256,1]{0,2,3,1:T(8,128)(2,1)} %bitcast.68, f32[8,2,1152,128]{3,2,1,0:T(8,128)} %copy-done.2, f32[8,2,128]{2,1,0:T(2,128)S(1)} %broadcast_maximum_fusion, pred[128,1152]{0,1:T(8,128)(4,1)S(1)} %compare_and_fusion), kind=kOutput, calls=%fused_computation.41 | convolution fusion | flops 1220280320 | bytes 16416768 | tf_op jit(solution)/shard_map/hmqk,khe->hmqe/dot_general | solution.py:85
  157.2 1.1 fusion.26
  158.3 2.0 copy.44
  160.3 5.7 %fusion.13 = bf16[128,2048]{1,0:T(8,128)(2,1)} fusion(bf16[128,2048]{0,1:T(8,128)(2,1)} %bitcast.70, bf16[2048,2048]{1,0:T(8,128)(2,1)} %param.21, bf16[128,2048]{1,0:T(8,128)(2,1)} %param.15), kind=kOutput, calls=%fused_computation.25 | convolution fusion | flops 1074528256 | bytes 9961472 | tf_op jit(solution)/shard_map/dot_general | solution.py:100
  166.3 33.9 %all-gather.6.cloned.1.call-done = bf16[1024,2048]{1,0:T(8,128)(2,1)} async-done(((bf16[128,2048]{1,0:T(8,128)(2,1)}), bf16[1024,2048]{1,0:T(8,128)(2,1)}) %all-gather.6.cloned.1.call-update) | async-done | bytes 4194320 | tf_op jit(solution)/shard_map/all_gather | solution.py:102
  200.1 3.2 fusion
  203.6 6.7 %fusion.15 = f32[1024,704]{0,1:T(8,128)} fusion(bf16[2048,704]{0,1:T(8,128)(2,1)} %param.23, bf16[1024,2048]{1,0:T(8,128)(2,1)S(1)} %copy-done.4, f32[2048]{0:T(1024)S(1)} %copy-done.11, f32[1024]{0:T(1024)S(1)} %add_rsqrt_fusion), kind=kOutput, calls=%fused_computation.29 | convolution fusion | flops 2961178624 | bytes 9973760 | tf_op jit(solution)/shard_map/dot_general | solution.py:104
  210.3 12.4 %convolution_convert_fusion = bf16[1024,2048]{1,0:T(8,128)(2,1)} fusion(bf16[704,2048]{1,0:T(8,128)(2,1)} %param.25, f32[1024,704]{0,1:T(8,128)} %fusion.15, bf16[2048,704]{0,1:T(8,128)(2,1)} %param.24, bf16[1024,2048]{1,0:T(8,128)(2,1)} %all-gather.6.cloned.1.call-done, f32[2048]{0:T(1024)S(1)} %copy-done.11, f32[1024]{0:T(1024)S(1)} %add_rsqrt_fusion), kind=kOutput, calls=%fused_computation.22 | convolution fusion | flops 5920391168 | bytes 17051648 | tf_op jit(solution)/shard_map/dot_general | solution.py:108
  222.8 37.9 %reduce-scatter.2.cloned.1.call-done = bf16[128,2048]{1,0:T(8,128)(2,1)} async-done(((bf16[1024,2048]{1,0:T(8,128)(2,1)}), bf16[128,2048]{1,0:T(8,128)(2,1)}) %reduce-scatter.2.cloned.1.call-update) | async-done | bytes 524304 | tf_op jit(solution)/shard_map/reduce_scatter | solution.py:107
  260.6 1.5 fusion.19
  263.9 31.2 %all-gather.8.cloned.1.call-done = bf16[1024,2048]{1,0:T(8,128)(2,1)} async-done(((bf16[128,2048]{1,0:T(8,128)(2,1)}), bf16[1024,2048]{1,0:T(8,128)(2,1)}) %all-gather.8.cloned.1.call-update) | async-done | bytes 4194320 | tf_op jit(solution)/shard_map/all_gather | solution.py:116
  295.1 6.8 %convolution_convert_fusion.1 = bf16[1024,768]{1,0:T(8,128)(2,1)} fusion(bf16[1024,2048]{1,0:T(8,128)(2,1)} %all-gather.8.cloned.1.call-done, bf16[2048,768]{1,0:T(8,128)(2,1)S(1)} %copy-done), kind=kOutput, calls=%fused_computation.26 | convolution fusion | flops 3222011904 | bytes 8912896 | tf_op jit(solution)/shard_map/dot_general | solution.py:115
  301.8 4.3 %all-to-all-start = ((bf16[8,128,768]{2,1,0:T(8,128)(2,1)}), bf16[8,128,768]{2,1,0:T(8,128)(2,1)}, u32[]{:S(2)}, u32[]{:S(2)}) async-start(bf16[8,128,768]{2,1,0:T(8,128)(2,1)} %bitcast.71), calls=%async_computation.1 | async-start | bytes 3145728 | tf_op jit(solution)/shard_map/all_to_all | solution.py:120
  308.2 1.2 sort.35
  309.5 18.2 %all-to-all-done = bf16[8,128,768]{2,1,0:T(8,128)(2,1)} async-done(((bf16[8,128,768]{2,1,0:T(8,128)(2,1)}), bf16[8,128,768]{2,1,0:T(8,128)(2,1)}, u32[]{:S(2)}, u32[]{:S(2)}) %all-to-all-start) | async-done | bytes 1572896 | tf_op jit(solution)/shard_map/all_to_all | solution.py:120
  327.7 1.6 copy.52
  329.3 1.1 copy-done.3
  331.5 2.8 gather_fusion.1
  334.3 7.0 %all-to-all-start.1 = ((bf16[16,1,8,4096]{3,2,1,0:T(8,128)(2,1)}), bf16[16,1,8,4096]{3,2,1,0:T(8,128)(2,1)}, u32[]{:S(2)}, u32[]{:S(2)}) async-start(bf16[16,1,8,4096]{3,2,1,0:T(8,128)(2,1)} %bitcast.69), calls=%async_computation.2 | async-start | bytes 2097152 | tf_op jit(solution)/shard_map/all_to_all | solution.py:131
  342.8 1.9 slice.52
  344.7 14.1 %all-to-all-done.1 = bf16[16,1,8,4096]{3,2,1,0:T(8,128)(2,1)} async-done(((bf16[16,1,8,4096]{3,2,1,0:T(8,128)(2,1)}), bf16[16,1,8,4096]{3,2,1,0:T(8,128)(2,1)}, u32[]{:S(2)}, u32[]{:S(2)}) %all-to-all-start.1) | async-done | bytes 1048608 | tf_op jit(solution)/shard_map/all_to_all | solution.py:131
  359.8 3.4 scatter_fusion
  (66 shorter events, 10.1 us)
Async XLA Ops:
  7.2 287.9 %copy-start = (bf16[2048,768]{1,0:T(8,128)(2,1)S(1)}, bf16[2048,768]{1,0:T(8,128)(2,1)}, u32[]{:S(2)}) copy-start(bf16[2048,768]{1,0:T(8,128)(2,1)} %param.27) | copy-start | bytes 9437188
  7.2 8.8 %copy-start.8 = (f32[4,128]{1,0:T(4,128)S(1)}, f32[4,128]{1,0:T(4,128)}, u32[]{:S(2)}) copy-start(f32[4,128]{1,0:T(4,128)} %param.20) | copy-start | bytes 6148
  7.2 10.8 %copy-start.1 = (s32[1,2048]{1,0:T(1,128)S(1)}, s32[1,2048]{1,0:T(1,128)}, u32[]{:S(2)}) copy-start(s32[1,2048]{1,0:T(1,128)} %param.19) | copy-start | bytes 24580
  7.2 130.3 %all-gather.4.cloned.1.call-start = ((), (), s32[]{:S(2)}) async-start(), calls=%async_computation.3 | async-start | bytes 17825792 | tf_op jit(solution)/shard_map/all_gather | solution.py:60
  13.7 186.4 %all-gather.6.cloned.1.call-start = ((), (), s32[]{:S(2)}) async-start(), calls=%async_computation.4 | async-start | bytes 4718592 | tf_op jit(solution)/shard_map/all_gather | solution.py:102
  137.5 5.1 %copy-start.5 = (bf16[128,8,2,128]{3,2,1,0:T(2,128)(2,1)S(1)}, bf16[128,8,2,128]{3,2,1,0:T(2,128)(2,1)}, u32[]{:S(2)}) copy-start(bf16[128,8,2,128]{3,2,1,0:T(2,128)(2,1)} %reshape.141) | copy-start | bytes 1572868
  145.1 3.6 copy-start.2
  166.0 37.4 %copy-start.11 = (f32[2048]{0:T(1024)S(1)}, f32[2048]{0:T(1024)}, u32[]{:S(2)}) copy-start(f32[2048]{0:T(1024)} %param.22) | copy-start | bytes 24580
  166.0 94.6 %reduce-scatter.2.cloned.1.call-start = ((), (), s32[]{:S(2)}) async-start(), calls=%async_computation.5 | async-start | bytes 4718592 | tf_op jit(solution)/shard_map/reduce_scatter | solution.py:107
  200.1 3.4 copy-start.4
  222.7 40.2 %copy-start.7 = (f32[2048]{0:T(1024)S(1)}, f32[2048]{0:T(1024)}, u32[]{:S(2)}) copy-start(f32[2048]{0:T(1024)} %param.26) | copy-start | bytes 24580
  222.7 72.4 %all-gather.8.cloned.1.call-start = ((), (), s32[]{:S(2)}) async-start(), calls=%async_computation.6 | async-start | bytes 4718592 | tf_op jit(solution)/shard_map/all_gather | solution.py:116
  262.1 0.8 copy-start.6
  263.9 42.8 %copy-start.9 = (s32[1,256]{1,0:T(1,128)S(1)}, s32[1,256]{1,0:T(1,128)}, u32[]{:S(2)}) copy-start(s32[1,256]{1,0:T(1,128)} %param.28) | copy-start | bytes 3076
  263.9 43.6 %copy-start.10 = (s32[1,256]{1,0:T(1,128)S(1)}, s32[1,256]{1,0:T(1,128)}, u32[]{:S(2)}) copy-start(s32[1,256]{1,0:T(1,128)} %param.29) | copy-start | bytes 3076
  301.8 25.9 %all-to-all-start = ((bf16[8,128,768]{2,1,0:T(8,128)(2,1)}), bf16[8,128,768]{2,1,0:T(8,128)(2,1)}, u32[]{:S(2)}, u32[]{:S(2)}) async-start(bf16[8,128,768]{2,1,0:T(8,128)(2,1)} %bitcast.71), calls=%async_computation.1 | async-start | bytes 3145728 | tf_op jit(solution)/shard_map/all_to_all | solution.py:120
  329.3 1.2 copy-start.3
  334.3 24.4 %all-to-all-start.1 = ((bf16[16,1,8,4096]{3,2,1,0:T(8,128)(2,1)}), bf16[16,1,8,4096]{3,2,1,0:T(8,128)(2,1)}, u32[]{:S(2)}, u32[]{:S(2)}) async-start(bf16[16,1,8,4096]{3,2,1,0:T(8,128)(2,1)} %bitcast.69), calls=%async_computation.2 | async-start | bytes 2097152 | tf_op jit(solution)/shard_map/all_to_all | solution.py:131
Sparse Core Ops, SparseCore 0:
  13.9 123.6 all-gather.3
  166.1 33.9 all-gather.5
  222.8 37.7 reduce-scatter.1
  264.0 31.0 all-gather.7

commit v4 on v3

--- a/solution.py
+++ b/solution.py
@@ -104,16 +104,15 @@
     gate_proj = jnp.dot(normed, gate_weight, preferred_element_type=jnp.float32)
     up_proj = jnp.dot(normed, up_weight, preferred_element_type=jnp.float32)
     hidden = (jax.nn.silu(gate_proj) * up_proj).astype(jnp.bfloat16)
-    ffn_own = lax.psum_scatter(
-        jnp.dot(hidden, down_weight, preferred_element_type=jnp.float32).astype(jnp.bfloat16),
-        "req",
-        scatter_dimension=0,
-        tiled=True,
+    ffn_all = lax.psum(
+        jnp.dot(hidden, down_weight, preferred_element_type=jnp.float32).astype(jnp.bfloat16), "req"
     ).astype(jnp.float32)
-    layer_output = (residual_mid.astype(jnp.float32) + ffn_own).astype(jnp.bfloat16)
-    next_normed = (rms_rows(layer_output.astype(jnp.float32)) * next_gain).astype(jnp.bfloat16)
+    output_all = (gathered.astype(jnp.float32) + ffn_all).astype(jnp.bfloat16)
+    req_place = lax.axis_index("req")
+    layer_output = lax.dynamic_slice_in_dim(output_all, req_place * row_count, row_count, 0)
+    next_normed = (rms_rows(output_all.astype(jnp.float32)) * next_gain).astype(jnp.bfloat16)
     projected_cols = jnp.dot(
-        lax.all_gather(next_normed, "req", axis=0, tiled=True),
+        next_normed,
         qkv_weight,
         preferred_element_type=jnp.float32,
     ).astype(jnp.bfloat16)

time: 370 us -> 374 us (1.011)
    psum x0 -> x1, waiting for transfers between devices: none -> 72.6 us  [body(): lax.psum(jnp.dot(hidden, down_weight, preferred_element_type=jnp.float32)...]
    reduce_scatter x1 -> x0, waiting for transfers between devices: 37.9 us -> none  [body(): lax.psum_scatter(jnp.dot(hidden, down_weight, preferred_element_type=jnp....]
    all_gather x1 -> x0, waiting for transfers between devices: 31.2 us -> none  [body(): lax.all_gather(next_normed, 'req', axis=0, tiled=True)]
    reduce_sum x3, other arithmetic: 4.9 us -> 8.9 us  [rms_rows(): jnp.mean(values * values, axis=-1, keepdims=True) + EPSILON]
  transfers between devices with their start and end apart: 6 -> 5, of which waited for: 6 -> 5; matrix products, arithmetic and copies ran while one was open for 5% -> 5% of each run, Pallas kernels for 0% -> 0%
where the time goes in v4:
time: 374 us
  waiting for transfers between devices  249 us (67%)
  matrix products  40.3 us (11%)
  local copies, waits for them, and re-layouts  37.8 us (10%)
  other arithmetic  19.7 us (5%)
  between operations  15.3 us (4%)
  starting transfers between devices  11.6 us (3%)
    all_gather x1, waiting for transfers between devices, body(): all_kv = lax.all_gather(own_kv, 'tok', axis=0, tiled=True)  112 us
    psum x1, waiting for transfers between devices, body(): lax.psum(jnp.dot(hidden, down_weight, preferred_element_type=jnp.float32)...  72.6 us
    all_gather x1, waiting for transfers between devices, body(): gathered = lax.all_gather(residual_mid, 'req', axis=0, tiled=True)  33.9 us
    all_to_all x1, waiting for transfers between devices, body(): lax.all_to_all(projected_cols, 'req', split_axis=0, concat_axis=1, tiled=...  17.4 us
    all_to_all x1, waiting for transfers between devices, body(): lax.all_to_all(outgoing, 'tok', split_axis=0, concat_axis=0, tiled=True)  13 us
    dot_general x1, matrix products, body(): jnp.dot(hidden, down_weight, preferred_element_type=jnp.float32)  12.4 us
    reduce_sum x3, other arithmetic, rms_rows(): jnp.mean(values * values, axis=-1, keepdims=True) + EPSILON  8.9 us
    dot_general x1, matrix products, body(): jnp.einsum('hmqk,khe->hmqe', weights.astype(jnp.bfloat16), value_split, p...  8.27 us
  transfers between devices with their start and end apart: 5, of which 5 were waited for; matrix products, arithmetic and copies ran while one was open for 5% of the time, Pallas kernels for 0%

profile of v4, /device:TPU:0, one launch (start us, length us, event | category | flops | bytes accessed | tf_op | source)
XLA Modules:
  0.0 373.5 jit_solution(1170883260938946228)
XLA Ops:
  7.2 2.2 copy.38
  9.4 2.0 copy.39
  11.5 2.2 pad_maximum_fusion
  13.8 2.2 reshape.141
  18.0 6.5 %gather_fusion = s32[1152]{0:T(1024)S(1)} fusion(s32[2048]{0:T(1024)S(1)} %bitcast.63, s32[2048]{0:T(1024)S(1)} %pad_clamp_fusion), kind=kCustom, calls=%fused_computation | custom fusion | bytes 13824 | tf_op jit(solution)/shard_map/jit(_take)/gather | solution.py:71
  25.6 112.0 %all-gather.3.cloned.1.call-done = bf16[2048,4096]{0,1:T(8,128)(2,1)} async-done(((bf16[128,4096]{0,1:T(8,128)(2,1)}), bf16[2048,4096]{0,1:T(8,128)(2,1)}) %all-gather.3.cloned.1.call-update) | async-done | bytes 16777232 | tf_op jit(solution)/shard_map/all_gather | solution.py:60
  137.5 5.1 %pad_dynamic-slice_fusion.1 = (bf16[1152,2048]{0,1:T(8,128)(2,1)}, bf16[1152,2048]{0,1:T(8,128)(2,1)S(1)}) fusion(s32[]{:T(128)S(6)} %select_n.73, s32[]{:T(128)S(6)} %add.177, bf16[2048,4096]{0,1:T(8,128)(2,1)} %all-gather.3.cloned.1.call-done), kind=kLoop, calls=%fused_computation.5 | loop fusion | bytes 26214408 | tf_op jit(solution)/shard_map/slice | solution.py:67
  142.6 2.5 fusion.7
  145.1 2.3 fusion.8
  147.4 1.3 copy-done.2
  148.7 8.3 %broadcast_divide_fusion = f32[8,2,128,256]{3,2,1,0:T(8,128)S(1)} fusion(f32[8,2,128]{2,1,0:T(2,128)S(1)} %fusion.8, bf16[1152,8,256,1]{0,2,3,1:T(8,128)(2,1)} %bitcast.67, f32[8,2,1152,128]{3,2,1,0:T(8,128)} %copy-done.2, f32[8,2,128]{2,1,0:T(2,128)S(1)} %broadcast_maximum_fusion, pred[128,1152]{0,1:T(8,128)(4,1)S(1)} %compare_and_fusion), kind=kOutput, calls=%fused_computation.45 | convolution fusion | flops 1220280320 | bytes 16416768 | tf_op jit(solution)/shard_map/hmqk,khe->hmqe/dot_general | solution.py:85
  157.2 1.1 fusion.34
  158.3 2.0 copy.44
  160.3 5.7 %fusion.21 = bf16[128,2048]{1,0:T(8,128)(2,1)} fusion(bf16[128,2048]{0,1:T(8,128)(2,1)} %bitcast.69, bf16[2048,2048]{1,0:T(8,128)(2,1)} %param.21, bf16[128,2048]{1,0:T(8,128)(2,1)} %param.15), kind=kOutput, calls=%fused_computation.35 | convolution fusion | flops 1074528256 | bytes 9961472 | tf_op jit(solution)/shard_map/dot_general | solution.py:100
  166.3 33.9 %all-gather.5.cloned.1.call-done = bf16[1024,2048]{1,0:T(8,128)(2,1)} async-done(((bf16[128,2048]{1,0:T(8,128)(2,1)}), bf16[1024,2048]{1,0:T(8,128)(2,1)}) %all-gather.5.cloned.1.call-update) | async-done | bytes 4194320 | tf_op jit(solution)/shard_map/all_gather | solution.py:102
  200.1 3.2 fusion.3
  203.6 6.7 %fusion.26 = f32[1024,704]{0,1:T(8,128)} fusion(bf16[2048,704]{0,1:T(8,128)(2,1)} %param.23, bf16[1024,2048]{1,0:T(8,128)(2,1)S(1)} %copy-done.3, f32[2048]{0:T(1024)S(1)} %copy-done.10, f32[1024]{0:T(1024)S(1)} %add_rsqrt_fusion.1), kind=kOutput, calls=%fused_computation.37 | convolution fusion | flops 2961178624 | bytes 9973760 | tf_op jit(solution)/shard_map/dot_general | solution.py:104
  210.2 12.4 %convolution_convert_fusion = bf16[1024,2048]{1,0:T(8,128)(2,1)} fusion(bf16[704,2048]{1,0:T(8,128)(2,1)} %param.25, f32[1024,704]{0,1:T(8,128)} %fusion.26, bf16[2048,704]{0,1:T(8,128)(2,1)} %param.24, bf16[1024,2048]{1,0:T(8,128)(2,1)} %all-gather.5.cloned.1.call-done, f32[2048]{0:T(1024)S(1)} %copy-done.10, f32[1024]{0:T(1024)S(1)} %add_rsqrt_fusion.1), kind=kOutput, calls=%fused_computation.32 | convolution fusion | flops 5920391168 | bytes 17051648 | tf_op jit(solution)/shard_map/dot_general | solution.py:108
  222.7 72.6 %all-reduce.3.cloned.1.call-done = bf16[1024,2048]{1,0:T(8,128)(2,1)} async-done(((bf16[1024,2048]{1,0:T(8,128)(2,1)}), bf16[1024,2048]{1,0:T(8,128)(2,1)}) %all-reduce.3.cloned.1.call-update) | async-done | bytes 4194320 | tf_op jit(solution)/shard_map/psum | solution.py:107
  295.2 5.5 %fusion = (f32[1024]{0:T(1024)S(1)}, bf16[1024,2048]{1,0:T(8,128)(2,1)S(1)}) fusion(bf16[1024,2048]{1,0:T(8,128)(2,1)} %all-reduce.3.cloned.1.call-done, bf16[1024,2048]{1,0:T(8,128)(2,1)} %all-gather.5.cloned.1.call-done), kind=kLoop, calls=%fused_computation.13 | loop fusion | flops 14679040 | bytes 12587008 | tf_op jit(solution)/shard_map/reduce_sum | solution.py:19
  300.8 4.8 %fusion.22 = bf16[1024,768]{1,0:T(8,128)(2,1)} fusion(bf16[2048,768]{1,0:T(8,128)(2,1)S(1)} %copy-done, bf16[1024,2048]{1,0:T(8,128)(2,1)S(1)} %get-tuple-element.10, f32[2048]{0:T(1024)S(1)} %copy-done.11, f32[1024]{0:T(1024)S(1)} %add_rsqrt_fusion), kind=kOutput, calls=%fused_computation.36 | convolution fusion | flops 3230400512 | bytes 8925184 | tf_op jit(solution)/shard_map/dot_general | solution.py:114
  305.6 4.3 %all-to-all-start = ((bf16[8,128,768]{2,1,0:T(8,128)(2,1)}), bf16[8,128,768]{2,1,0:T(8,128)(2,1)}, u32[]{:S(2)}, u32[]{:S(2)}) async-start(bf16[8,128,768]{2,1,0:T(8,128)(2,1)} %bitcast.70), calls=%async_computation | async-start | bytes 3145728 | tf_op jit(solution)/shard_map/all_to_all | solution.py:119
  312.0 1.2 sort.35
  314.1 17.4 %all-to-all-done = bf16[8,128,768]{2,1,0:T(8,128)(2,1)} async-done(((bf16[8,128,768]{2,1,0:T(8,128)(2,1)}), bf16[8,128,768]{2,1,0:T(8,128)(2,1)}, u32[]{:S(2)}, u32[]{:S(2)}) %all-to-all-start) | async-done | bytes 1572896 | tf_op jit(solution)/shard_map/all_to_all | solution.py:119
  331.5 1.6 copy.52
  333.1 1.2 copy-done.4
  335.3 2.8 gather_fusion.1
  338.1 7.0 %all-to-all-start.1 = ((bf16[16,1,8,4096]{3,2,1,0:T(8,128)(2,1)}), bf16[16,1,8,4096]{3,2,1,0:T(8,128)(2,1)}, u32[]{:S(2)}, u32[]{:S(2)}) async-start(bf16[16,1,8,4096]{3,2,1,0:T(8,128)(2,1)} %bitcast.68), calls=%async_computation.1 | async-start | bytes 2097152 | tf_op jit(solution)/shard_map/all_to_all | solution.py:130
  345.8 1.9 constant_dynamic-slice_fusion.1
  347.7 1.9 slice.52
  349.6 13.0 %all-to-all-done.1 = bf16[16,1,8,4096]{3,2,1,0:T(8,128)(2,1)} async-done(((bf16[16,1,8,4096]{3,2,1,0:T(8,128)(2,1)}), bf16[16,1,8,4096]{3,2,1,0:T(8,128)(2,1)}, u32[]{:S(2)}, u32[]{:S(2)}) %all-to-all-start.1) | async-done | bytes 1048608 | tf_op jit(solution)/shard_map/all_to_all | solution.py:130
  363.6 3.4 scatter_fusion
  (63 shorter events, 8.3 us)
Async XLA Ops:
  7.2 293.6 %copy-start = (bf16[2048,768]{1,0:T(8,128)(2,1)S(1)}, bf16[2048,768]{1,0:T(8,128)(2,1)}, u32[]{:S(2)}) copy-start(bf16[2048,768]{1,0:T(8,128)(2,1)} %param.27) | copy-start | bytes 9437188
  7.2 8.8 %copy-start.7 = (f32[4,128]{1,0:T(4,128)S(1)}, f32[4,128]{1,0:T(4,128)}, u32[]{:S(2)}) copy-start(f32[4,128]{1,0:T(4,128)} %param.20) | copy-start | bytes 6148
  7.2 10.8 %copy-start.1 = (s32[1,2048]{1,0:T(1,128)S(1)}, s32[1,2048]{1,0:T(1,128)}, u32[]{:S(2)}) copy-start(s32[1,2048]{1,0:T(1,128)} %param.19) | copy-start | bytes 24580
  7.2 130.3 %all-gather.3.cloned.1.call-start = ((), (), s32[]{:S(2)}) async-start(), calls=%async_computation.2 | async-start | bytes 17825792 | tf_op jit(solution)/shard_map/all_gather | solution.py:60
  13.7 186.4 %all-gather.5.cloned.1.call-start = ((), (), s32[]{:S(2)}) async-start(), calls=%async_computation.3 | async-start | bytes 4718592 | tf_op jit(solution)/shard_map/all_gather | solution.py:102
  137.5 5.1 %copy-start.6 = (bf16[128,8,2,128]{3,2,1,0:T(2,128)(2,1)S(1)}, bf16[128,8,2,128]{3,2,1,0:T(2,128)(2,1)}, u32[]{:S(2)}) copy-start(bf16[128,8,2,128]{3,2,1,0:T(2,128)(2,1)} %reshape.141) | copy-start | bytes 1572868
  145.1 3.6 copy-start.2
  166.0 37.4 %copy-start.10 = (f32[2048]{0:T(1024)S(1)}, f32[2048]{0:T(1024)}, u32[]{:S(2)}) copy-start(f32[2048]{0:T(1024)} %param.22) | copy-start | bytes 24580
  166.0 129.2 %all-reduce.3.cloned.1.call-start = ((), (), s32[]{:S(2)}) async-start(), calls=%async_computation.4 | async-start | bytes 8388608 | tf_op jit(solution)/shard_map/psum | solution.py:107
  200.1 3.4 copy-start.3
  222.7 78.1 %copy-start.11 = (f32[2048]{0:T(1024)S(1)}, f32[2048]{0:T(1024)}, u32[]{:S(2)}) copy-start(f32[2048]{0:T(1024)} %param.26) | copy-start | bytes 24580
  300.7 4.9 %copy-start.5 = (bf16[1024,2048]{1,0:T(8,128)(2,1)}, bf16[1024,2048]{1,0:T(8,128)(2,1)S(1)}, u32[]{:S(2)}) copy-start(bf16[1024,2048]{1,0:T(8,128)(2,1)S(1)} %get-tuple-element.10) | copy-start | bytes 12582916
  300.8 9.7 %copy-start.8 = (s32[1,256]{1,0:T(1,128)S(1)}, s32[1,256]{1,0:T(1,128)}, u32[]{:S(2)}) copy-start(s32[1,256]{1,0:T(1,128)} %param.28) | copy-start | bytes 3076
  300.8 10.5 %copy-start.9 = (s32[1,256]{1,0:T(1,128)S(1)}, s32[1,256]{1,0:T(1,128)}, u32[]{:S(2)}) copy-start(s32[1,256]{1,0:T(1,128)} %param.29) | copy-start | bytes 3076
  305.6 25.9 %all-to-all-start = ((bf16[8,128,768]{2,1,0:T(8,128)(2,1)}), bf16[8,128,768]{2,1,0:T(8,128)(2,1)}, u32[]{:S(2)}, u32[]{:S(2)}) async-start(bf16[8,128,768]{2,1,0:T(8,128)(2,1)} %bitcast.70), calls=%async_computation | async-start | bytes 3145728 | tf_op jit(solution)/shard_map/all_to_all | solution.py:119
  333.1 1.2 copy-start.4
  338.1 24.5 %all-to-all-start.1 = ((bf16[16,1,8,4096]{3,2,1,0:T(8,128)(2,1)}), bf16[16,1,8,4096]{3,2,1,0:T(8,128)(2,1)}, u32[]{:S(2)}, u32[]{:S(2)}) async-start(bf16[16,1,8,4096]{3,2,1,0:T(8,128)(2,1)} %bitcast.68), calls=%async_computation.1 | async-start | bytes 2097152 | tf_op jit(solution)/shard_map/all_to_all | solution.py:130
Sparse Core Ops, SparseCore 0:
  13.9 123.6 all-gather.2
  166.1 33.9 all-gather.4
  222.8 72.4 all-reduce.2

commit v5 on v0

--- a/solution.py
+++ b/solution.py
@@ -1,8 +1,11 @@
+import functools
 import math
 
 import jax
 import jax.numpy as jnp
 from jax import lax
+from jax.experimental import pallas as pl
+from jax.experimental.pallas import tpu as pltpu
 from jax.sharding import PartitionSpec as P
 
 HEADS = 8
@@ -12,6 +15,7 @@
 NEG_FILL = -1e30
 LAMBDA_INIT = 0.2
 EPSILON = 1e-05
+MAX_SEG = 1024
 
 
 def rms_rows(values):
@@ -22,6 +26,71 @@
     first_term = jnp.exp(jnp.sum(lambda_parts[0] * lambda_parts[1]))
     second_term = jnp.exp(jnp.sum(lambda_parts[2] * lambda_parts[3]))
     return first_term - second_term + LAMBDA_INIT
+
+
+def attention_kernel(back, head_dim, scalars_ref, lam_ref, q_ref, k_ref, v_ref, qseg_ref, kseg_ref, out_ref):
+    rows = q_ref.shape[0]
+    span = (back + 1) * rows
+    start = pl.multiple_of(scalars_ref[0], rows)
+    query_places = scalars_ref[1] + lax.broadcasted_iota(jnp.int32, (rows, span), 0)
+    key_places = start + lax.broadcasted_iota(jnp.int32, (rows, span), 1)
+    key_segs = kseg_ref[:, pl.ds(start, span)]
+    visible = (key_segs == qseg_ref[...]) & (key_places <= query_places)
+    values = v_ref[pl.ds(start, span), :]
+    score_scale = 1.0 / math.sqrt(head_dim)
+    map_outputs = []
+    for map_index in range(2):
+        query_map = q_ref[:, map_index * head_dim:(map_index + 1) * head_dim]
+        key_map = k_ref[pl.ds(start, span), map_index * head_dim:(map_index + 1) * head_dim]
+        scores = (
+            lax.dot_general(
+                query_map, key_map, (((1,), (1,)), ((), ())), preferred_element_type=jnp.float32
+            )
+            * score_scale
+        )
+        scores = jnp.where(visible, scores, NEG_FILL)
+        row_max = jnp.max(scores, axis=1, keepdims=True)
+        weights = jnp.where(visible, jnp.exp(scores - row_max), 0.0)
+        totals = jnp.sum(weights, axis=1, keepdims=True)
+        map_out = (
+            jnp.dot(weights.astype(jnp.bfloat16), values, preferred_element_type=jnp.float32) / totals
+        )
+        map_outputs.append(map_out)
+    difference = map_outputs[0] - lam_ref[0] * map_outputs[1]
+    out_ref[...] = (rms_rows(difference) * (1.0 - LAMBDA_INIT)).astype(out_ref.dtype)
+
+
+def window_attention(q_in, all_kv, query_segs, seg_row, first_row, lambda_mix, back):
+    rows, width = q_in.shape
+    keys = all_kv.shape[0]
+    head_w = width // HEADS
+    start = jnp.maximum(first_row - back * rows, 0)
+    scalars = jnp.stack([start, first_row]).astype(jnp.int32)
+    lam = jnp.reshape(lambda_mix, (1,)).astype(jnp.float32)
+    span = (back + 1) * rows
+    flops = HEADS * 2 * (2 * rows * span * (head_w // 2) + 2 * rows * span * head_w)
+    smem = pl.BlockSpec(memory_space=pltpu.SMEM)
+    return pl.pallas_call(
+        functools.partial(attention_kernel, back, head_w // 2),
+        out_shape=jax.ShapeDtypeStruct((rows, width), jnp.bfloat16),
+        grid=(HEADS,),
+        in_specs=[
+            smem,
+            smem,
+            pl.BlockSpec((rows, head_w), lambda h: (0, h)),
+            pl.BlockSpec((keys, head_w), lambda h: (0, h)),
+            pl.BlockSpec((keys, head_w), lambda h: (0, HEADS + h)),
+            pl.BlockSpec((rows, 1), lambda h: (0, 0)),
+            pl.BlockSpec((1, keys), lambda h: (0, 0)),
+        ],
+        out_specs=pl.BlockSpec((rows, head_w), lambda h: (0, h)),
+        compiler_params=pltpu.CompilerParams(dimension_semantics=("arbitrary",)),
+        cost_estimate=pl.CostEstimate(
+            flops=flops,
+            bytes_accessed=2 * keys * width * 2 + 2 * rows * width * 2,
+            transcendentals=HEADS * 2 * rows * span,
+        ),
+    )(scalars, lam, q_in, all_kv, all_kv, query_segs.reshape(rows, 1), seg_row.reshape(1, keys))
 
 
 def body(
@@ -54,36 +123,10 @@
     score_scale = 1.0 / math.sqrt(head_dim)
     query_split = q_in.reshape(row_count, HEADS, 2, head_dim)
     run_max = jnp.full((HEADS, 2, row_count), NEG_FILL, jnp.float32)
-    key_rows = lax.all_gather(k_in, "tok", axis=0, tiled=True)
-    value_rows = lax.all_gather(v_in, "tok", axis=0, tiled=True)
-    piece_len = key_rows.shape[0]
-    key_split = key_rows.reshape(piece_len, HEADS, 2, head_dim)
-    value_split = value_rows.reshape(piece_len, HEADS, 2 * head_dim)
-    key_places = jnp.arange(piece_len)
-    visible = (seg_row[None, :] == query_segs[:, None]) & (
-        key_places[None, :] <= query_places[:, None]
-    )
-    scores = (
-        jnp.einsum("qhmd,khmd->hmqk", query_split, key_split, preferred_element_type=jnp.float32)
-        * score_scale
-    )
-    scores = jnp.where(visible, scores, NEG_FILL)
-    new_max = jnp.maximum(run_max, jnp.max(scores, axis=-1))
-    weights = jnp.where(visible, jnp.exp(scores - new_max[..., None]), 0.0)
-    totals = jnp.sum(weights, axis=-1)
-    weighted = jnp.einsum(
-        "hmqk,khe->hmqe",
-        weights.astype(jnp.bfloat16),
-        value_split,
-        preferred_element_type=jnp.float32,
-    )
-    run_max, totals, weighted = (new_max, totals, weighted)
-    map_outputs = weighted / totals[..., None]
-    difference = map_outputs[:, 0] - lambda_mix * map_outputs[:, 1]
-    head_outputs = rms_rows(difference) * (1.0 - LAMBDA_INIT)
-    attention = (
-        jnp.transpose(head_outputs, (1, 0, 2)).reshape(row_count, feat_width).astype(jnp.bfloat16)
-    )
+    back = -(-(MAX_SEG - 1) // row_count)
+    own_kv = jnp.concatenate([k_in, v_in], axis=1)
+    all_kv = lax.all_gather(own_kv, "tok", axis=0, tiled=True)
+    attention = window_attention(q_in, all_kv, query_segs, seg_row, first_row, lambda_mix, back)
     residual_mid = (
         layer_input.astype(jnp.float32)
         + jnp.dot(attention, out_weight, preferred_element_type=jnp.float32)

time: 396 us -> 346 us (0.87)
  waiting for transfers between devices: 271 us -> 244 us
  matrix products: 50.8 us -> 31.5 us
  Pallas kernels: 0 us -> 13.3 us
  local copies, waits for them, and re-layouts: 29.8 us -> 16.7 us
    all_gather x2 -> x1, waiting for transfers between devices: 138 us -> 111 us  [body(): all_kv = lax.all_gather(own_kv, 'tok', axis=0, tiled=True)]
    dot_general x2 -> x0, matrix products: 19.3 us -> none  [the longest x1 12.6 us: body(): jnp.einsum('hmqk,khe->hmqe', weights.astype(jnp.bfloat16), value_split, p...]
    pallas_call x0 -> x1, Pallas kernels: none -> 13.3 us  [window_attention(): pl.pallas_call(functools.partial(attention_kernel, back, head_w // 2), ou...]
    unnamed x26 -> x20, local copies, waits for them, and re-layouts: 12.8 us -> 2.67 us
    reduce_sum x1 -> x0, other arithmetic: 4.96 us -> none  [body(): totals = jnp.sum(weights, axis=-1)]
  transfers between devices with their start and end apart: 7 -> 6, of which waited for: 7 -> 6; matrix products, arithmetic and copies ran while one was open for 6% -> 3% of each run, Pallas kernels for 0% -> 0%
where the time goes in v5:
time: 346 us; the launch traced here: 345 us
  waiting for transfers between devices  244 us (71%)
  matrix products  31.5 us (9%)
  local copies, waits for them, and re-layouts  16.7 us (5%)
  between operations  15.3 us (4%)
  Pallas kernels  13.3 us (4%)
  other arithmetic  12.9 us (4%)
  starting transfers between devices  11.8 us (3%)
    all_gather x1, waiting for transfers between devices, body(): all_kv = lax.all_gather(own_kv, 'tok', axis=0, tiled=True)  111 us
    reduce_scatter x1, waiting for transfers between devices, body(): lax.psum_scatter(jnp.dot(hidden, down_weight, preferred_element_type=jnp....  37.7 us
    all_gather x1, waiting for transfers between devices, body(): gathered = lax.all_gather(residual_mid, 'req', axis=0, tiled=True)  31.8 us
    all_gather x1, waiting for transfers between devices, body(): lax.all_gather(next_normed, 'req', axis=0, tiled=True)  31.2 us
    all_to_all x1, waiting for transfers between devices, body(): lax.all_to_all(projected_cols, 'req', split_axis=0, concat_axis=1, tiled=...  18.2 us
    all_to_all x1, waiting for transfers between devices, body(): lax.all_to_all(outgoing, 'tok', split_axis=0, concat_axis=0, tiled=True)  14.1 us
    pallas_call x1, Pallas kernels, window_attention(): pl.pallas_call(functools.partial(attention_kernel, back, head_w // 2), ou...  13.3 us
    dot_general x1, matrix products, body(): jnp.dot(hidden, down_weight, preferred_element_type=jnp.float32)  12.4 us
  transfers between devices with their start and end apart: 6, of which 6 were waited for; matrix products, arithmetic and copies ran while one was open for 3% of the time, Pallas kernels for 0%

profile of v5, /device:TPU:0, one launch (start us, length us, event | category | flops | bytes accessed | tf_op | source)
XLA Modules:
  0.0 345.3 jit_solution(1676912133981982085)
XLA Ops:
  7.2 2.4 pad_maximum_fusion
  9.7 0.7 multiply_reduce_fusion
  11.8 0.7 dynamic-slice_bitcast_fusion
  12.5 0.7 copy.25.qseg_ref
  13.9 110.8 %all-gather.4.cloned.1.call-done.k_ref.v_ref = bf16[2048,4096]{1,0:T(8,128)(2,1)} async-done(((bf16[128,4096]{1,0:T(8,128)(2,1)}), bf16[2048,4096]{1,0:T(8,128)(2,1)}) %all-gather.4.cloned.1.call-update) | async-done | bytes 16777232 | tf_op jit(solution)/shard_map/all_gather | solution.py:128
  124.7 13.3 %shard_map.166 = bf16[128,2048]{1,0:T(8,128)(2,1)} custom-call(s32[2]{0:T(128)} %pad_add_fusion.scalars_ref, f32[1]{0:T(128)} %bitcast.2.lam_ref, bf16[128,2048]{1,0:T(8,128)(2,1)} %q_ref.1, bf16[2048,4096]{1,0:T(8,128)(2,1)} %all-gather.4.cloned.1.call-done.k_ref.v_ref, bf16[2048,4096]{1,0:T(8,128)(2,1)} %all-gather.4.cloned.1.call-done.k_ref.v_ref, ...), custom_call_target="tpu_custom_call" | custom-call | flops 1811939328 | bytes 17825792 | tf_op jit(solution)/shard_map/pallas_call | solution.py:73
  138.0 5.6 %fusion.3 = bf16[128,2048]{1,0:T(8,128)(2,1)} fusion(bf16[128,2048]{1,0:T(8,128)(2,1)} %shard_map.166, bf16[2048,2048]{1,0:T(8,128)(2,1)} %param.21, bf16[128,2048]{1,0:T(8,128)(2,1)} %param.15), kind=kOutput, calls=%fused_computation.11 | convolution fusion | flops 1074528256 | bytes 9961472 | tf_op jit(solution)/shard_map/dot_general | solution.py:132
  143.7 31.8 %all-gather.6.cloned.1.call-done = bf16[1024,2048]{1,0:T(8,128)(2,1)} async-done(((bf16[128,2048]{1,0:T(8,128)(2,1)}), bf16[1024,2048]{1,0:T(8,128)(2,1)}) %all-gather.6.cloned.1.call-update) | async-done | bytes 4194320 | tf_op jit(solution)/shard_map/all_gather | solution.py:134
  175.6 3.2 fusion
  179.0 6.7 %fusion.5 = f32[1024,704]{0,1:T(8,128)} fusion(bf16[2048,704]{0,1:T(8,128)(2,1)} %param.23, bf16[1024,2048]{1,0:T(8,128)(2,1)S(1)} %copy-done.2, f32[2048]{0:T(1024)S(1)} %copy-done.8, f32[1024]{0:T(1024)S(1)} %add_rsqrt_fusion), kind=kOutput, calls=%fused_computation.15 | convolution fusion | flops 2961178624 | bytes 9973760 | tf_op jit(solution)/shard_map/dot_general | solution.py:136
  185.7 12.4 %convolution_convert_fusion = bf16[1024,2048]{1,0:T(8,128)(2,1)} fusion(bf16[704,2048]{1,0:T(8,128)(2,1)} %param.25, f32[1024,704]{0,1:T(8,128)} %fusion.5, bf16[2048,704]{0,1:T(8,128)(2,1)} %param.24, bf16[1024,2048]{1,0:T(8,128)(2,1)} %all-gather.6.cloned.1.call-done, f32[2048]{0:T(1024)S(1)} %copy-done.8, f32[1024]{0:T(1024)S(1)} %add_rsqrt_fusion), kind=kOutput, calls=%fused_computation.8 | convolution fusion | flops 5920391168 | bytes 17051648 | tf_op jit(solution)/shard_map/dot_general | solution.py:140
  198.4 37.7 %reduce-scatter.2.cloned.1.call-done = bf16[128,2048]{1,0:T(8,128)(2,1)} async-done(((bf16[1024,2048]{1,0:T(8,128)(2,1)}), bf16[128,2048]{1,0:T(8,128)(2,1)}) %reduce-scatter.2.cloned.1.call-update) | async-done | bytes 524304 | tf_op jit(solution)/shard_map/reduce_scatter | solution.py:139
  236.0 1.5 fusion.9
  237.5 0.8 copy-done.3
  238.3 1.0 fusion.11
  239.3 31.2 %all-gather.8.cloned.1.call-done = bf16[1024,2048]{1,0:T(8,128)(2,1)} async-done(((bf16[128,2048]{1,0:T(8,128)(2,1)}), bf16[1024,2048]{1,0:T(8,128)(2,1)}) %all-gather.8.cloned.1.call-update) | async-done | bytes 4194320 | tf_op jit(solution)/shard_map/all_gather | solution.py:148
  270.5 6.8 %convolution_convert_fusion.1 = bf16[1024,768]{1,0:T(8,128)(2,1)} fusion(bf16[1024,2048]{1,0:T(8,128)(2,1)} %all-gather.8.cloned.1.call-done, bf16[2048,768]{1,0:T(8,128)(2,1)S(1)} %copy-done), kind=kOutput, calls=%fused_computation.12 | convolution fusion | flops 3222011904 | bytes 8912896 | tf_op jit(solution)/shard_map/dot_general | solution.py:147
  277.3 4.4 %all-to-all-start = ((bf16[8,128,768]{2,1,0:T(8,128)(2,1)}), bf16[8,128,768]{2,1,0:T(8,128)(2,1)}, u32[]{:S(2)}, u32[]{:S(2)}) async-start(bf16[8,128,768]{2,1,0:T(8,128)(2,1)} %bitcast.37), calls=%async_computation.1 | async-start | bytes 3145728 | tf_op jit(solution)/shard_map/all_to_all | solution.py:152
  282.2 0.7 reduce.8
  283.0 0.7 reduce.9
  283.8 1.2 sort.35
  285.1 18.2 %all-to-all-done = bf16[8,128,768]{2,1,0:T(8,128)(2,1)} async-done(((bf16[8,128,768]{2,1,0:T(8,128)(2,1)}), bf16[8,128,768]{2,1,0:T(8,128)(2,1)}, u32[]{:S(2)}, u32[]{:S(2)}) %all-to-all-start) | async-done | bytes 1572896 | tf_op jit(solution)/shard_map/all_to_all | solution.py:152
  303.3 1.6 copy.28
  304.9 1.1 copy-done.1
  306.0 1.0 slice_bitcast_fusion
  307.1 2.8 gather_fusion
  309.9 7.0 %all-to-all-start.1 = ((bf16[16,1,8,4096]{3,2,1,0:T(8,128)(2,1)}), bf16[16,1,8,4096]{3,2,1,0:T(8,128)(2,1)}, u32[]{:S(2)}, u32[]{:S(2)}) async-start(bf16[16,1,8,4096]{3,2,1,0:T(8,128)(2,1)} %bitcast.36), calls=%async_computation.2 | async-start | bytes 2097152 | tf_op jit(solution)/shard_map/all_to_all | solution.py:163
  317.0 0.7 sort.34
  318.4 1.9 slice.32
  320.3 14.1 %all-to-all-done.1 = bf16[16,1,8,4096]{3,2,1,0:T(8,128)(2,1)} async-done(((bf16[16,1,8,4096]{3,2,1,0:T(8,128)(2,1)}), bf16[16,1,8,4096]{3,2,1,0:T(8,128)(2,1)}, u32[]{:S(2)}, u32[]{:S(2)}) %all-to-all-start.1) | async-done | bytes 1048608 | tf_op jit(solution)/shard_map/all_to_all | solution.py:163
  334.3 1.1 broadcast_in_dim.20
  335.4 3.4 scatter_fusion
  (44 shorter events, 2.9 us)
Async XLA Ops:
  7.2 263.3 %copy-start = (bf16[2048,768]{1,0:T(8,128)(2,1)S(1)}, bf16[2048,768]{1,0:T(8,128)(2,1)}, u32[]{:S(2)}) copy-start(bf16[2048,768]{1,0:T(8,128)(2,1)} %param.27) | copy-start | bytes 9437188
  7.2 2.6 copy-start.5
  7.2 117.5 %all-gather.4.cloned.1.call-start = ((), (), s32[]{:S(2)}) async-start(), calls=%async_computation.3 | async-start | bytes 17825792 | tf_op jit(solution)/shard_map/all_gather | solution.py:128
  9.7 165.9 %all-gather.6.cloned.1.call-start = ((), (), s32[]{:S(2)}) async-start(), calls=%async_computation.4 | async-start | bytes 4718592 | tf_op jit(solution)/shard_map/all_gather | solution.py:134
  143.7 35.1 %copy-start.8 = (f32[2048]{0:T(1024)S(1)}, f32[2048]{0:T(1024)}, u32[]{:S(2)}) copy-start(f32[2048]{0:T(1024)} %param.22) | copy-start | bytes 24580
  143.7 92.4 %reduce-scatter.2.cloned.1.call-start = ((), (), s32[]{:S(2)}) async-start(), calls=%async_computation.5 | async-start | bytes 4718592 | tf_op jit(solution)/shard_map/reduce_scatter | solution.py:139
  175.6 3.4 copy-start.2
  198.1 40.2 %copy-start.4 = (f32[2048]{0:T(1024)S(1)}, f32[2048]{0:T(1024)}, u32[]{:S(2)}) copy-start(f32[2048]{0:T(1024)} %param.26) | copy-start | bytes 24580
  198.1 72.4 %all-gather.8.cloned.1.call-start = ((), (), s32[]{:S(2)}) async-start(), calls=%async_computation.6 | async-start | bytes 4718592 | tf_op jit(solution)/shard_map/all_gather | solution.py:148
  237.5 0.8 copy-start.3
  277.3 4.9 %copy-start.6 = (s32[1,256]{1,0:T(1,128)S(1)}, s32[1,256]{1,0:T(1,128)}, u32[]{:S(2)}) copy-start(s32[1,256]{1,0:T(1,128)} %param.29) | copy-start | bytes 3076
  277.3 5.7 %copy-start.7 = (s32[1,256]{1,0:T(1,128)S(1)}, s32[1,256]{1,0:T(1,128)}, u32[]{:S(2)}) copy-start(s32[1,256]{1,0:T(1,128)} %param.28) | copy-start | bytes 3076
  277.3 26.0 %all-to-all-start = ((bf16[8,128,768]{2,1,0:T(8,128)(2,1)}), bf16[8,128,768]{2,1,0:T(8,128)(2,1)}, u32[]{:S(2)}, u32[]{:S(2)}) async-start(bf16[8,128,768]{2,1,0:T(8,128)(2,1)} %bitcast.37), calls=%async_computation.1 | async-start | bytes 3145728 | tf_op jit(solution)/shard_map/all_to_all | solution.py:152
  304.9 1.2 copy-start.1
  309.9 24.4 %all-to-all-start.1 = ((bf16[16,1,8,4096]{3,2,1,0:T(8,128)(2,1)}), bf16[16,1,8,4096]{3,2,1,0:T(8,128)(2,1)}, u32[]{:S(2)}, u32[]{:S(2)}) async-start(bf16[16,1,8,4096]{3,2,1,0:T(8,128)(2,1)} %bitcast.36), calls=%async_computation.2 | async-start | bytes 2097152 | tf_op jit(solution)/shard_map/all_to_all | solution.py:163
Sparse Core Ops, SparseCore 0:
  10.7 113.9 all-gather.3
  143.8 31.6 all-gather.5
  198.3 37.7 reduce-scatter.1
  239.4 31.0 all-gather.7

commit v6 on v5

--- a/solution.py
+++ b/solution.py
@@ -91,6 +91,43 @@
             transcendentals=HEADS * 2 * rows * span,
         ),
     )(scalars, lam, q_in, all_kv, all_kv, query_segs.reshape(rows, 1), seg_row.reshape(1, keys))
+
+
+def ffn_kernel(x_ref, gain_ref, gate_ref, up_ref, down_ref, out_ref):
+    normed = (rms_rows(x_ref[...].astype(jnp.float32)) * gain_ref[...]).astype(jnp.bfloat16)
+    gate_proj = jnp.dot(normed, gate_ref[...], preferred_element_type=jnp.float32)
+    up_proj = jnp.dot(normed, up_ref[...], preferred_element_type=jnp.float32)
+    hidden = (gate_proj / (1.0 + jnp.exp(-gate_proj)) * up_proj).astype(jnp.bfloat16)
+    out_ref[...] = jnp.dot(hidden, down_ref[...], preferred_element_type=jnp.float32).astype(
+        out_ref.dtype
+    )
+
+
+def ffn_partial(rows, gain, gate_weight, up_weight, down_weight, tile):
+    count, width = rows.shape
+    hidden_w = gate_weight.shape[1]
+    full = lambda i: (0, 0)
+    return pl.pallas_call(
+        ffn_kernel,
+        out_shape=jax.ShapeDtypeStruct((count, width), jnp.bfloat16),
+        grid=(count // tile,),
+        in_specs=[
+            pl.BlockSpec((tile, width), lambda i: (i, 0)),
+            pl.BlockSpec((1, width), full),
+            pl.BlockSpec((width, hidden_w), full),
+            pl.BlockSpec((width, hidden_w), full),
+            pl.BlockSpec((hidden_w, width), full),
+        ],
+        out_specs=pl.BlockSpec((tile, width), lambda i: (i, 0)),
+        compiler_params=pltpu.CompilerParams(
+            dimension_semantics=("arbitrary",), vmem_limit_bytes=48 * 1024 * 1024
+        ),
+        cost_estimate=pl.CostEstimate(
+            flops=6 * count * width * hidden_w,
+            bytes_accessed=3 * width * hidden_w * 2 + 2 * count * width * 2,
+            transcendentals=count * hidden_w,
+        ),
+    )(rows, gain.reshape(1, width), gate_weight, up_weight, down_weight)
 
 
 def body(
@@ -132,16 +169,8 @@
         + jnp.dot(attention, out_weight, preferred_element_type=jnp.float32)
     ).astype(jnp.bfloat16)
     gathered = lax.all_gather(residual_mid, "req", axis=0, tiled=True)
-    normed = (rms_rows(gathered.astype(jnp.float32)) * ffn_gain).astype(jnp.bfloat16)
-    gate_proj = jnp.dot(normed, gate_weight, preferred_element_type=jnp.float32)
-    up_proj = jnp.dot(normed, up_weight, preferred_element_type=jnp.float32)
-    hidden = (jax.nn.silu(gate_proj) * up_proj).astype(jnp.bfloat16)
-    ffn_own = lax.psum_scatter(
-        jnp.dot(hidden, down_weight, preferred_element_type=jnp.float32).astype(jnp.bfloat16),
-        "req",
-        scatter_dimension=0,
-        tiled=True,
-    ).astype(jnp.float32)
+    partial = ffn_partial(gathered, ffn_gain, gate_weight, up_weight, down_weight, 256)
+    ffn_own = lax.psum_scatter(partial, "req", scatter_dimension=0, tiled=True).astype(jnp.float32)
     layer_output = (residual_mid.astype(jnp.float32) + ffn_own).astype(jnp.bfloat16)
     next_normed = (rms_rows(layer_output.astype(jnp.float32)) * next_gain).astype(jnp.bfloat16)
     projected_cols = jnp.dot(

time: 346 us -> 342 us (0.988)
  matrix products: 31.5 us -> 12.4 us
  Pallas kernels: 13.3 us -> 27.9 us
  local copies, waits for them, and re-layouts: 16.7 us -> 29.5 us
  waiting for transfers between devices: 244 us -> 235 us
    dot_general x2 -> x0, matrix products: 19.1 us -> none  [the longest x1 12.4 us: body(): jnp.dot(hidden, down_weight, preferred_element_type=jnp.float32)]
    pallas_call x0 -> x1, Pallas kernels: none -> 14.6 us  [ffn_partial(): pl.pallas_call(ffn_kernel, out_shape=jax.ShapeDtypeStruct((count, width),...]
    unnamed x20 -> x24, local copies, waits for them, and re-layouts: 2.67 us -> 15.4 us
    all_gather x1, waiting for transfers between devices: 31.8 us -> 22.5 us  [body(): gathered = lax.all_gather(residual_mid, 'req', axis=0, tiled=True)]
  transfers between devices with their start and end apart: 6 -> 6, of which waited for: 6 -> 6; matrix products, arithmetic and copies ran while one was open for 3% -> 5% of each run, Pallas kernels for 0% -> 0%
where the time goes in v6:
time: 342 us; the launch traced here: 341 us
  waiting for transfers between devices  235 us (69%)
  local copies, waits for them, and re-layouts  29.5 us (9%)
  Pallas kernels  27.9 us (8%)
  between operations  15.3 us (4%)
  matrix products  12.4 us (4%)
  starting transfers between devices  11.6 us (3%)
  other arithmetic  9.63 us (3%)
    all_gather x1, waiting for transfers between devices, body(): all_kv = lax.all_gather(own_kv, 'tok', axis=0, tiled=True)  111 us
    reduce_scatter x1, waiting for transfers between devices, body(): lax.psum_scatter(partial, 'req', scatter_dimension=0, tiled=True)  37.8 us
    all_gather x1, waiting for transfers between devices, body(): lax.all_gather(next_normed, 'req', axis=0, tiled=True)  31.2 us
    all_gather x1, waiting for transfers between devices, body(): gathered = lax.all_gather(residual_mid, 'req', axis=0, tiled=True)  22.5 us
    all_to_all x1, waiting for transfers between devices, body(): lax.all_to_all(projected_cols, 'req', split_axis=0, concat_axis=1, tiled=...  18.2 us
    unnamed x24, local copies, waits for them, and re-layouts  15.4 us
    pallas_call x1, Pallas kernels, ffn_partial(): pl.pallas_call(ffn_kernel, out_shape=jax.ShapeDtypeStruct((count, width),...  14.6 us
    all_to_all x1, waiting for transfers between devices, body(): lax.all_to_all(outgoing, 'tok', split_axis=0, concat_axis=0, tiled=True)  14.1 us
  transfers between devices with their start and end apart: 6, of which 6 were waited for; matrix products, arithmetic and copies ran while one was open for 5% of the time, Pallas kernels for 0%

profile of v6, /device:TPU:0, one launch (start us, length us, event | category | flops | bytes accessed | tf_op | source)
XLA Modules:
  0.0 341.0 jit_solution(4717435382813882056)
XLA Ops:
  7.2 2.4 pad_maximum_fusion
  9.7 0.7 multiply_reduce_fusion
  12.5 0.7 copy.31.qseg_ref
  13.9 110.8 %all-gather.4.cloned.1.call-done.k_ref.v_ref = bf16[2048,4096]{1,0:T(8,128)(2,1)} async-done(((bf16[128,4096]{1,0:T(8,128)(2,1)}), bf16[2048,4096]{1,0:T(8,128)(2,1)}) %all-gather.4.cloned.1.call-update) | async-done | bytes 16777232 | tf_op jit(solution)/shard_map/all_gather | solution.py:165
  124.7 13.3 %shard_map.166 = bf16[128,2048]{1,0:T(8,128)(2,1)} custom-call(s32[2]{0:T(128)} %pad_add_fusion.scalars_ref, f32[1]{0:T(128)} %bitcast.2.lam_ref, bf16[128,2048]{1,0:T(8,128)(2,1)} %q_ref.1, bf16[2048,4096]{1,0:T(8,128)(2,1)} %all-gather.4.cloned.1.call-done.k_ref.v_ref, bf16[2048,4096]{1,0:T(8,128)(2,1)} %all-gather.4.cloned.1.call-done.k_ref.v_ref, ...), custom_call_target="tpu_custom_call" | custom-call | flops 1811939328 | bytes 17825792 | tf_op jit(solution)/shard_map/pallas_call | solution.py:73
  138.0 5.6 %fusion = bf16[128,2048]{1,0:T(8,128)(2,1)} fusion(bf16[128,2048]{1,0:T(8,128)(2,1)} %shard_map.166, bf16[2048,2048]{1,0:T(8,128)(2,1)} %param.21, bf16[128,2048]{1,0:T(8,128)(2,1)} %param.15), kind=kOutput, calls=%fused_computation.4 | convolution fusion | flops 1074528256 | bytes 9961472 | tf_op jit(solution)/shard_map/dot_general | solution.py:169
  143.7 4.6 %copy.32.gate_ref = bf16[2048,704]{1,0:T(8,128)(2,1)} copy(bf16[2048,704]{0,1:T(8,128)(2,1)} %param.23) | data formatting | bytes 5767168 | tf_op args[8]
  148.4 4.7 %copy.33.up_ref = bf16[2048,704]{1,0:T(8,128)(2,1)} copy(bf16[2048,704]{0,1:T(8,128)(2,1)} %param.24) | data formatting | bytes 5767168 | tf_op args[9]
  153.0 22.5 %all-gather.6.cloned.1.call-done.x_ref = bf16[1024,2048]{1,0:T(8,128)(2,1)} async-done(((bf16[128,2048]{1,0:T(8,128)(2,1)}), bf16[1024,2048]{1,0:T(8,128)(2,1)}) %all-gather.6.cloned.1.call-update) | async-done | bytes 4194320 | tf_op jit(solution)/shard_map/all_gather | solution.py:171
  175.6 1.9 copy-done.1
  177.5 1.8 copy-done.2
  179.3 14.6 %shard_map.167 = bf16[1024,2048]{1,0:T(8,128)(2,1)} custom-call(bf16[1024,2048]{1,0:T(8,128)(2,1)} %all-gather.6.cloned.1.call-done.x_ref, f32[1,2048]{1,0:T(1,128)S(1)} %bitcast.32, bf16[2048,704]{1,0:T(8,128)(2,1)S(1)} %copy-done.1, bf16[2048,704]{1,0:T(8,128)(2,1)} %copy.33.up_ref, bf16[704,2048]{1,0:T(8,128)(2,1)S(1)} %copy-done.2), custom_call_target="tpu_custom_call" | custom-call | flops 8858370048 | bytes 17039360 | tf_op jit(solution)/shard_map/pallas_call | solution.py:110
  194.0 37.8 %reduce-scatter.2.cloned.1.call-done = bf16[128,2048]{1,0:T(8,128)(2,1)} async-done(((bf16[1024,2048]{1,0:T(8,128)(2,1)}), bf16[128,2048]{1,0:T(8,128)(2,1)}) %reduce-scatter.2.cloned.1.call-update) | async-done | bytes 524304 | tf_op jit(solution)/shard_map/reduce_scatter | solution.py:173
  231.8 1.5 fusion.1
  233.3 0.8 copy-done.5
  234.1 1.0 fusion.3
  235.1 31.2 %all-gather.8.cloned.1.call-done = bf16[1024,2048]{1,0:T(8,128)(2,1)} async-done(((bf16[128,2048]{1,0:T(8,128)(2,1)}), bf16[1024,2048]{1,0:T(8,128)(2,1)}) %all-gather.8.cloned.1.call-update) | async-done | bytes 4194320 | tf_op jit(solution)/shard_map/all_gather | solution.py:177
  266.2 6.8 %convolution_convert_fusion = bf16[1024,768]{1,0:T(8,128)(2,1)} fusion(bf16[1024,2048]{1,0:T(8,128)(2,1)} %all-gather.8.cloned.1.call-done, bf16[2048,768]{1,0:T(8,128)(2,1)S(1)} %copy-done), kind=kOutput, calls=%fused_computation.5 | convolution fusion | flops 3222011904 | bytes 8912896 | tf_op jit(solution)/shard_map/dot_general | solution.py:176
  273.0 4.4 %all-to-all-start = ((bf16[8,128,768]{2,1,0:T(8,128)(2,1)}), bf16[8,128,768]{2,1,0:T(8,128)(2,1)}, u32[]{:S(2)}, u32[]{:S(2)}) async-start(bf16[8,128,768]{2,1,0:T(8,128)(2,1)} %bitcast.36), calls=%async_computation.1 | async-start | bytes 3145728 | tf_op jit(solution)/shard_map/all_to_all | solution.py:181
  278.7 0.7 reduce.9
  279.6 1.2 sort.35
  280.8 18.2 %all-to-all-done = bf16[8,128,768]{2,1,0:T(8,128)(2,1)} async-done(((bf16[8,128,768]{2,1,0:T(8,128)(2,1)}), bf16[8,128,768]{2,1,0:T(8,128)(2,1)}, u32[]{:S(2)}, u32[]{:S(2)}) %all-to-all-start) | async-done | bytes 1572896 | tf_op jit(solution)/shard_map/all_to_all | solution.py:181
  299.0 1.6 copy.36
  300.6 1.1 copy-done.4
  301.8 1.0 slice_bitcast_fusion
  302.8 2.8 gather_fusion
  305.6 7.0 %all-to-all-start.1 = ((bf16[16,1,8,4096]{3,2,1,0:T(8,128)(2,1)}), bf16[16,1,8,4096]{3,2,1,0:T(8,128)(2,1)}, u32[]{:S(2)}, u32[]{:S(2)}) async-start(bf16[16,1,8,4096]{3,2,1,0:T(8,128)(2,1)} %bitcast.35), calls=%async_computation.2 | async-start | bytes 2097152 | tf_op jit(solution)/shard_map/all_to_all | solution.py:192
  312.7 0.7 sort.34
  314.1 1.9 slice.32
  316.0 14.1 %all-to-all-done.1 = bf16[16,1,8,4096]{3,2,1,0:T(8,128)(2,1)} async-done(((bf16[16,1,8,4096]{3,2,1,0:T(8,128)(2,1)}), bf16[16,1,8,4096]{3,2,1,0:T(8,128)(2,1)}, u32[]{:S(2)}, u32[]{:S(2)}) %all-to-all-start.1) | async-done | bytes 1048608 | tf_op jit(solution)/shard_map/all_to_all | solution.py:192
  330.1 1.1 broadcast_in_dim.27
  331.1 3.4 scatter_fusion
  (45 shorter events, 3.8 us)
Async XLA Ops:
  7.2 259.1 %copy-start = (bf16[2048,768]{1,0:T(8,128)(2,1)S(1)}, bf16[2048,768]{1,0:T(8,128)(2,1)}, u32[]{:S(2)}) copy-start(bf16[2048,768]{1,0:T(8,128)(2,1)} %param.27) | copy-start | bytes 9437188
  7.2 2.6 copy-start.7
  7.2 117.5 %all-gather.4.cloned.1.call-start = ((), (), s32[]{:S(2)}) async-start(), calls=%async_computation.3 | async-start | bytes 17825792 | tf_op jit(solution)/shard_map/all_gather | solution.py:165
  9.7 165.9 %all-gather.6.cloned.1.call-start = ((), (), s32[]{:S(2)}) async-start(), calls=%async_computation.4 | async-start | bytes 4718592 | tf_op jit(solution)/shard_map/all_gather | solution.py:171
  143.7 88.1 %reduce-scatter.2.cloned.1.call-start = ((), (), s32[]{:S(2)}) async-start(), calls=%async_computation.5 | async-start | bytes 4718592 | tf_op jit(solution)/shard_map/reduce_scatter | solution.py:173
  148.4 27.2 %copy-start.3 = (f32[2048]{0:T(1024)S(1)}, f32[2048]{0:T(1024)}, u32[]{:S(2)}) copy-start(f32[2048]{0:T(1024)} %param.22) | copy-start | bytes 24580
  175.6 1.9 copy-start.1
  177.4 1.8 copy-start.2
  193.9 40.2 %copy-start.6 = (f32[2048]{0:T(1024)S(1)}, f32[2048]{0:T(1024)}, u32[]{:S(2)}) copy-start(f32[2048]{0:T(1024)} %param.26) | copy-start | bytes 24580
  193.9 72.3 %all-gather.8.cloned.1.call-start = ((), (), s32[]{:S(2)}) async-start(), calls=%async_computation.6 | async-start | bytes 4718592 | tf_op jit(solution)/shard_map/all_gather | solution.py:177
  233.3 0.8 copy-start.5
  273.0 4.9 %copy-start.8 = (s32[1,256]{1,0:T(1,128)S(1)}, s32[1,256]{1,0:T(1,128)}, u32[]{:S(2)}) copy-start(s32[1,256]{1,0:T(1,128)} %param.29) | copy-start | bytes 3076
  273.0 5.7 %copy-start.9 = (s32[1,256]{1,0:T(1,128)S(1)}, s32[1,256]{1,0:T(1,128)}, u32[]{:S(2)}) copy-start(s32[1,256]{1,0:T(1,128)} %param.28) | copy-start | bytes 3076
  273.0 26.0 %all-to-all-start = ((bf16[8,128,768]{2,1,0:T(8,128)(2,1)}), bf16[8,128,768]{2,1,0:T(8,128)(2,1)}, u32[]{:S(2)}, u32[]{:S(2)}) async-start(bf16[8,128,768]{2,1,0:T(8,128)(2,1)} %bitcast.36), calls=%async_computation.1 | async-start | bytes 3145728 | tf_op jit(solution)/shard_map/all_to_all | solution.py:181
  300.6 1.2 copy-start.4
  305.6 24.4 %all-to-all-start.1 = ((bf16[16,1,8,4096]{3,2,1,0:T(8,128)(2,1)}), bf16[16,1,8,4096]{3,2,1,0:T(8,128)(2,1)}, u32[]{:S(2)}, u32[]{:S(2)}) async-start(bf16[16,1,8,4096]{3,2,1,0:T(8,128)(2,1)} %bitcast.35), calls=%async_computation.2 | async-start | bytes 2097152 | tf_op jit(solution)/shard_map/all_to_all | solution.py:192
Sparse Core Ops, SparseCore 0:
  10.7 113.9 all-gather.3
  143.8 31.6 all-gather.5
  194.0 37.7 reduce-scatter.1
  235.2 31.0 all-gather.7

commit v7 on v6

--- a/solution.py
+++ b/solution.py
@@ -95,8 +95,9 @@
 
 def ffn_kernel(x_ref, gain_ref, gate_ref, up_ref, down_ref, out_ref):
     normed = (rms_rows(x_ref[...].astype(jnp.float32)) * gain_ref[...]).astype(jnp.bfloat16)
-    gate_proj = jnp.dot(normed, gate_ref[...], preferred_element_type=jnp.float32)
-    up_proj = jnp.dot(normed, up_ref[...], preferred_element_type=jnp.float32)
+    contract = (((1,), (1,)), ((), ()))
+    gate_proj = lax.dot_general(normed, gate_ref[...], contract, preferred_element_type=jnp.float32)
+    up_proj = lax.dot_general(normed, up_ref[...], contract, preferred_element_type=jnp.float32)
     hidden = (gate_proj / (1.0 + jnp.exp(-gate_proj)) * up_proj).astype(jnp.bfloat16)
     out_ref[...] = jnp.dot(hidden, down_ref[...], preferred_element_type=jnp.float32).astype(
         out_ref.dtype
@@ -107,6 +108,8 @@
     count, width = rows.shape
     hidden_w = gate_weight.shape[1]
     full = lambda i: (0, 0)
+    gate_t = gate_weight.T
+    up_t = up_weight.T
     return pl.pallas_call(
         ffn_kernel,
         out_shape=jax.ShapeDtypeStruct((count, width), jnp.bfloat16),
@@ -114,8 +117,8 @@
         in_specs=[
             pl.BlockSpec((tile, width), lambda i: (i, 0)),
             pl.BlockSpec((1, width), full),
-            pl.BlockSpec((width, hidden_w), full),
-            pl.BlockSpec((width, hidden_w), full),
+            pl.BlockSpec((hidden_w, width), full),
+            pl.BlockSpec((hidden_w, width), full),
             pl.BlockSpec((hidden_w, width), full),
         ],
         out_specs=pl.BlockSpec((tile, width), lambda i: (i, 0)),
@@ -127,7 +130,7 @@
             bytes_accessed=3 * width * hidden_w * 2 + 2 * count * width * 2,
             transcendentals=count * hidden_w,
         ),
-    )(rows, gain.reshape(1, width), gate_weight, up_weight, down_weight)
+    )(rows, gain.reshape(1, width), gate_t, up_t, down_weight)
 
 
 def body(

time: 342 us -> 342 us (level)
  local copies, waits for them, and re-layouts: 29.5 us -> 20.2 us
  waiting for transfers between devices: 235 us -> 244 us
    unnamed x24 -> x22, local copies, waits for them, and re-layouts: 15.4 us -> 6.1 us
    all_gather x1, waiting for transfers between devices: 22.5 us -> 31.8 us  [body(): gathered = lax.all_gather(residual_mid, 'req', axis=0, tiled=True)]
  transfers between devices with their start and end apart: 6 -> 6, of which waited for: 6 -> 6; matrix products, arithmetic and copies ran while one was open for 5% -> 3% of each run, Pallas kernels for 0% -> 0%
where the time goes in v7:
time: 342 us; the launch traced here: 341 us
  waiting for transfers between devices  244 us (71%)
  Pallas kernels  27.9 us (8%)
  local copies, waits for them, and re-layouts  20.2 us (6%)
  between operations  15.3 us (4%)
  matrix products  12.4 us (4%)
  starting transfers between devices  11.6 us (3%)
  other arithmetic  9.63 us (3%)
    all_gather x1, waiting for transfers between devices, body(): all_kv = lax.all_gather(own_kv, 'tok', axis=0, tiled=True)  111 us
    reduce_scatter x1, waiting for transfers between devices, body(): lax.psum_scatter(partial, 'req', scatter_dimension=0, tiled=True)  37.9 us
    all_gather x1, waiting for transfers between devices, body(): gathered = lax.all_gather(residual_mid, 'req', axis=0, tiled=True)  31.8 us
    all_gather x1, waiting for transfers between devices, body(): lax.all_gather(next_normed, 'req', axis=0, tiled=True)  31.2 us
    all_to_all x1, waiting for transfers between devices, body(): lax.all_to_all(projected_cols, 'req', split_axis=0, concat_axis=1, tiled=...  18.2 us
    pallas_call x1, Pallas kernels, ffn_partial(): pl.pallas_call(ffn_kernel, out_shape=jax.ShapeDtypeStruct((count, width),...  14.5 us
    all_to_all x1, waiting for transfers between devices, body(): lax.all_to_all(outgoing, 'tok', split_axis=0, concat_axis=0, tiled=True)  14.1 us
    pallas_call x1, Pallas kernels, window_attention(): pl.pallas_call(functools.partial(attention_kernel, back, head_w // 2), ou...  13.3 us
  transfers between devices with their start and end apart: 6, of which 6 were waited for; matrix products, arithmetic and copies ran while one was open for 3% of the time, Pallas kernels for 0%

profile of v7, /device:TPU:0, one launch (start us, length us, event | category | flops | bytes accessed | tf_op | source)
XLA Modules:
  0.0 341.0 jit_solution(4074868297376361825)
XLA Ops:
  7.2 2.4 pad_maximum_fusion
  9.7 0.7 multiply_reduce_fusion
  11.8 0.7 dynamic-slice_bitcast_fusion
  12.5 0.7 copy.25.qseg_ref
  13.9 110.8 %all-gather.4.cloned.1.call-done.k_ref.v_ref = bf16[2048,4096]{1,0:T(8,128)(2,1)} async-done(((bf16[128,4096]{1,0:T(8,128)(2,1)}), bf16[2048,4096]{1,0:T(8,128)(2,1)}) %all-gather.4.cloned.1.call-update) | async-done | bytes 16777232 | tf_op jit(solution)/shard_map/all_gather | solution.py:168
  124.7 13.3 %shard_map.166 = bf16[128,2048]{1,0:T(8,128)(2,1)} custom-call(s32[2]{0:T(128)} %pad_add_fusion.scalars_ref, f32[1]{0:T(128)} %bitcast.2.lam_ref, bf16[128,2048]{1,0:T(8,128)(2,1)} %q_ref.1, bf16[2048,4096]{1,0:T(8,128)(2,1)} %all-gather.4.cloned.1.call-done.k_ref.v_ref, bf16[2048,4096]{1,0:T(8,128)(2,1)} %all-gather.4.cloned.1.call-done.k_ref.v_ref, ...), custom_call_target="tpu_custom_call" | custom-call | flops 1811939328 | bytes 17825792 | tf_op jit(solution)/shard_map/pallas_call | solution.py:73
  138.0 5.6 %fusion = bf16[128,2048]{1,0:T(8,128)(2,1)} fusion(bf16[128,2048]{1,0:T(8,128)(2,1)} %shard_map.166, bf16[2048,2048]{1,0:T(8,128)(2,1)} %param.21, bf16[128,2048]{1,0:T(8,128)(2,1)} %param.15), kind=kOutput, calls=%fused_computation.4 | convolution fusion | flops 1074528256 | bytes 9961472 | tf_op jit(solution)/shard_map/dot_general | solution.py:172
  143.8 31.8 %all-gather.6.cloned.1.call-done.x_ref = bf16[1024,2048]{1,0:T(8,128)(2,1)} async-done(((bf16[128,2048]{1,0:T(8,128)(2,1)}), bf16[1024,2048]{1,0:T(8,128)(2,1)}) %all-gather.6.cloned.1.call-update) | async-done | bytes 4194320 | tf_op jit(solution)/shard_map/all_gather | solution.py:174
  175.6 1.8 copy-done.1
  177.4 1.8 copy-done.2
  179.2 14.5 %shard_map.167 = bf16[1024,2048]{1,0:T(8,128)(2,1)} custom-call(bf16[1024,2048]{1,0:T(8,128)(2,1)} %all-gather.6.cloned.1.call-done.x_ref, f32[1,2048]{1,0:T(1,128)S(1)} %bitcast.36, bf16[704,2048]{1,0:T(8,128)(2,1)S(1)} %bitcast.34, bf16[704,2048]{1,0:T(8,128)(2,1)S(1)} %bitcast.35, bf16[704,2048]{1,0:T(8,128)(2,1)} %down_ref.1), custom_call_target="tpu_custom_call" | custom-call | flops 8858370048 | bytes 17039360 | tf_op jit(solution)/shard_map/pallas_call | solution.py:113
  193.8 37.9 %reduce-scatter.2.cloned.1.call-done = bf16[128,2048]{1,0:T(8,128)(2,1)} async-done(((bf16[1024,2048]{1,0:T(8,128)(2,1)}), bf16[128,2048]{1,0:T(8,128)(2,1)}) %reduce-scatter.2.cloned.1.call-update) | async-done | bytes 524304 | tf_op jit(solution)/shard_map/reduce_scatter | solution.py:176
  231.7 1.5 fusion.1
  233.2 0.8 copy-done.5
  234.0 1.0 fusion.3
  235.0 31.2 %all-gather.8.cloned.1.call-done = bf16[1024,2048]{1,0:T(8,128)(2,1)} async-done(((bf16[128,2048]{1,0:T(8,128)(2,1)}), bf16[1024,2048]{1,0:T(8,128)(2,1)}) %all-gather.8.cloned.1.call-update) | async-done | bytes 4194320 | tf_op jit(solution)/shard_map/all_gather | solution.py:180
  266.2 6.8 %convolution_convert_fusion = bf16[1024,768]{1,0:T(8,128)(2,1)} fusion(bf16[1024,2048]{1,0:T(8,128)(2,1)} %all-gather.8.cloned.1.call-done, bf16[2048,768]{1,0:T(8,128)(2,1)S(1)} %copy-done), kind=kOutput, calls=%fused_computation.5 | convolution fusion | flops 3222011904 | bytes 8912896 | tf_op jit(solution)/shard_map/dot_general | solution.py:179
  272.9 4.4 %all-to-all-start = ((bf16[8,128,768]{2,1,0:T(8,128)(2,1)}), bf16[8,128,768]{2,1,0:T(8,128)(2,1)}, u32[]{:S(2)}, u32[]{:S(2)}) async-start(bf16[8,128,768]{2,1,0:T(8,128)(2,1)} %bitcast.40), calls=%async_computation.1 | async-start | bytes 3145728 | tf_op jit(solution)/shard_map/all_to_all | solution.py:184
  277.9 0.7 reduce.8
  278.6 0.7 reduce.9
  279.5 1.2 sort.35
  280.7 18.2 %all-to-all-done = bf16[8,128,768]{2,1,0:T(8,128)(2,1)} async-done(((bf16[8,128,768]{2,1,0:T(8,128)(2,1)}), bf16[8,128,768]{2,1,0:T(8,128)(2,1)}, u32[]{:S(2)}, u32[]{:S(2)}) %all-to-all-start) | async-done | bytes 1572896 | tf_op jit(solution)/shard_map/all_to_all | solution.py:184
  298.9 1.6 copy.28
  300.5 1.1 copy-done.4
  301.7 1.0 slice_bitcast_fusion
  302.7 2.8 gather_fusion
  305.5 7.0 %all-to-all-start.1 = ((bf16[16,1,8,4096]{3,2,1,0:T(8,128)(2,1)}), bf16[16,1,8,4096]{3,2,1,0:T(8,128)(2,1)}, u32[]{:S(2)}, u32[]{:S(2)}) async-start(bf16[16,1,8,4096]{3,2,1,0:T(8,128)(2,1)} %bitcast.39), calls=%async_computation.2 | async-start | bytes 2097152 | tf_op jit(solution)/shard_map/all_to_all | solution.py:195
  312.6 0.7 sort.34
  314.0 1.9 slice.32
  315.9 14.1 %all-to-all-done.1 = bf16[16,1,8,4096]{3,2,1,0:T(8,128)(2,1)} async-done(((bf16[16,1,8,4096]{3,2,1,0:T(8,128)(2,1)}), bf16[16,1,8,4096]{3,2,1,0:T(8,128)(2,1)}, u32[]{:S(2)}, u32[]{:S(2)}) %all-to-all-start.1) | async-done | bytes 1048608 | tf_op jit(solution)/shard_map/all_to_all | solution.py:195
  330.0 1.1 broadcast_in_dim.27
  331.1 3.4 scatter_fusion
  (43 shorter events, 2.5 us)
Async XLA Ops:
  7.2 259.0 %copy-start = (bf16[2048,768]{1,0:T(8,128)(2,1)S(1)}, bf16[2048,768]{1,0:T(8,128)(2,1)}, u32[]{:S(2)}) copy-start(bf16[2048,768]{1,0:T(8,128)(2,1)} %param.27) | copy-start | bytes 9437188
  7.2 2.6 copy-start.7
  7.2 117.5 %all-gather.4.cloned.1.call-start = ((), (), s32[]{:S(2)}) async-start(), calls=%async_computation.3 | async-start | bytes 17825792 | tf_op jit(solution)/shard_map/all_gather | solution.py:168
  9.7 165.9 %all-gather.6.cloned.1.call-start = ((), (), s32[]{:S(2)}) async-start(), calls=%async_computation.4 | async-start | bytes 4718592 | tf_op jit(solution)/shard_map/all_gather | solution.py:174
  138.0 37.5 %copy-start.3 = (f32[2048]{0:T(1024)S(1)}, f32[2048]{0:T(1024)}, u32[]{:S(2)}) copy-start(f32[2048]{0:T(1024)} %param.22) | copy-start | bytes 24580
  143.7 88.0 %reduce-scatter.2.cloned.1.call-start = ((), (), s32[]{:S(2)}) async-start(), calls=%async_computation.5 | async-start | bytes 4718592 | tf_op jit(solution)/shard_map/reduce_scatter | solution.py:176
  175.6 1.8 copy-start.1
  177.4 1.8 copy-start.2
  193.7 40.2 %copy-start.6 = (f32[2048]{0:T(1024)S(1)}, f32[2048]{0:T(1024)}, u32[]{:S(2)}) copy-start(f32[2048]{0:T(1024)} %param.26) | copy-start | bytes 24580
  193.8 72.4 %all-gather.8.cloned.1.call-start = ((), (), s32[]{:S(2)}) async-start(), calls=%async_computation.6 | async-start | bytes 4718592 | tf_op jit(solution)/shard_map/all_gather | solution.py:180
  233.2 0.8 copy-start.5
  272.9 4.9 %copy-start.8 = (s32[1,256]{1,0:T(1,128)S(1)}, s32[1,256]{1,0:T(1,128)}, u32[]{:S(2)}) copy-start(s32[1,256]{1,0:T(1,128)} %param.29) | copy-start | bytes 3076
  272.9 5.7 %copy-start.9 = (s32[1,256]{1,0:T(1,128)S(1)}, s32[1,256]{1,0:T(1,128)}, u32[]{:S(2)}) copy-start(s32[1,256]{1,0:T(1,128)} %param.28) | copy-start | bytes 3076
  272.9 26.0 %all-to-all-start = ((bf16[8,128,768]{2,1,0:T(8,128)(2,1)}), bf16[8,128,768]{2,1,0:T(8,128)(2,1)}, u32[]{:S(2)}, u32[]{:S(2)}) async-start(bf16[8,128,768]{2,1,0:T(8,128)(2,1)} %bitcast.40), calls=%async_computation.1 | async-start | bytes 3145728 | tf_op jit(solution)/shard_map/all_to_all | solution.py:184
  300.5 1.2 copy-start.4
  305.5 24.5 %all-to-all-start.1 = ((bf16[16,1,8,4096]{3,2,1,0:T(8,128)(2,1)}), bf16[16,1,8,4096]{3,2,1,0:T(8,128)(2,1)}, u32[]{:S(2)}, u32[]{:S(2)}) async-start(bf16[16,1,8,4096]{3,2,1,0:T(8,128)(2,1)} %bitcast.39), calls=%async_computation.2 | async-start | bytes 2097152 | tf_op jit(solution)/shard_map/all_to_all | solution.py:195
Sparse Core Ops, SparseCore 0:
  10.7 113.9 all-gather.3
  143.8 31.6 all-gather.5
  193.9 37.7 reduce-scatter.1
  235.1 31.0 all-gather.7

commit v8 on v7

--- a/solution.py
+++ b/solution.py
@@ -181,28 +181,31 @@
         qkv_weight,
         preferred_element_type=jnp.float32,
     ).astype(jnp.bfloat16)
-    projected = lax.all_to_all(projected_cols, "req", split_axis=0, concat_axis=1, tiled=True)
+    n_req = lax.axis_size("req")
+    col_w = projected_cols.shape[1]
+    arrived = lax.all_to_all(
+        projected_cols.reshape(n_req, row_count, col_w), "req", 0, 0, tiled=True
+    )
+    projected = jnp.transpose(arrived, (1, 0, 2)).reshape(row_count, n_req * col_w)
     q_next = projected[:, :feat_width]
     pages_dev = row_count // PAGE
-    per_owner = pages_dev // peer_count
+    assert pages_dev == peer_count
     key_values = projected[:, feat_width:].reshape(pages_dev, PAGE, 2 * feat_width)
     owner_all = page_owner[0].reshape(peer_count, pages_dev)
     slot_all = page_slot[0].reshape(peer_count, pages_dev)
-    page_numbers = jnp.arange(pages_dev, dtype=jnp.int32)
+    numbers = jnp.arange(pages_dev, dtype=jnp.int32)
     my_owners = lax.dynamic_index_in_dim(owner_all, tok_place, 0, keepdims=False)
-    send_order = jnp.argsort(my_owners * pages_dev + page_numbers)
-    outgoing = key_values[send_order].reshape(peer_count, per_owner, PAGE, 2 * feat_width)
+    send_order = jnp.sum(
+        jnp.where(my_owners[None, :] == numbers[:, None], numbers[None, :], 0), axis=1
+    )
+    outgoing = key_values[send_order].reshape(peer_count, 1, PAGE, 2 * feat_width)
     incoming = lax.all_to_all(outgoing, "tok", split_axis=0, concat_axis=0, tiled=True)
-    rank_keys = jnp.where(
-        owner_all == tok_place, page_numbers[None, :], pages_dev + page_numbers[None, :]
-    )
-    chosen_pages = jnp.argsort(rank_keys, axis=1)[:, :per_owner]
-    slot_list = jnp.take_along_axis(slot_all, chosen_pages, axis=1).reshape(pages_dev)
-    page_cache = (
-        jnp.zeros((pages_dev, PAGE, 2 * feat_width), jnp.bfloat16)
-        .at[slot_list]
-        .set(incoming.reshape(pages_dev, PAGE, 2 * feat_width))
-    )
+    incoming = incoming.reshape(pages_dev, PAGE, 2 * feat_width)
+    slot_list = jnp.sum(jnp.where(owner_all == tok_place, slot_all, 0), axis=1)
+    source_of_slot = jnp.sum(
+        jnp.where(slot_list[None, :] == numbers[:, None], numbers[None, :], 0), axis=1
+    )
+    page_cache = incoming[source_of_slot]
     return (layer_output, q_next, page_cache)
 
 

time: 342 us -> 340 us (level)
  transfers between devices with their start and end apart: 6 -> 6, of which waited for: 6 -> 6; matrix products, arithmetic and copies ran while one was open for 3% -> 2% of each run, Pallas kernels for 0% -> 0%
where the time goes in v8:
time: 340 us; the launch traced here: 339 us
  waiting for transfers between devices  247 us (73%)
  Pallas kernels  27.9 us (8%)
  local copies, waits for them, and re-layouts  17.8 us (5%)
  between operations  15.3 us (4%)
  matrix products  12.4 us (4%)
  starting transfers between devices  11.6 us (3%)
  other arithmetic  7.81 us (2%)
    all_gather x1, waiting for transfers between devices, body(): all_kv = lax.all_gather(own_kv, 'tok', axis=0, tiled=True)  111 us
    reduce_scatter x1, waiting for transfers between devices, body(): lax.psum_scatter(partial, 'req', scatter_dimension=0, tiled=True)  37.9 us
    all_gather x1, waiting for transfers between devices, body(): gathered = lax.all_gather(residual_mid, 'req', axis=0, tiled=True)  31.8 us
    all_gather x1, waiting for transfers between devices, body(): lax.all_gather(next_normed, 'req', axis=0, tiled=True)  31.2 us
    all_to_all x1, waiting for transfers between devices, body(): lax.all_to_all(projected_cols.reshape(n_req, row_count, col_w), 'req', 0,...  20.2 us
    all_to_all x1, waiting for transfers between devices, body(): lax.all_to_all(outgoing, 'tok', split_axis=0, concat_axis=0, tiled=True)  14.5 us
    pallas_call x1, Pallas kernels, ffn_partial(): pl.pallas_call(ffn_kernel, out_shape=jax.ShapeDtypeStruct((count, width),...  14.5 us
    pallas_call x1, Pallas kernels, window_attention(): pl.pallas_call(functools.partial(attention_kernel, back, head_w // 2), ou...  13.3 us
  transfers between devices with their start and end apart: 6, of which 6 were waited for; matrix products, arithmetic and copies ran while one was open for 2% of the time, Pallas kernels for 0%

profile of v8, /device:TPU:0, one launch (start us, length us, event | category | flops | bytes accessed | tf_op | source)
XLA Modules:
  0.0 339.3 jit_solution(4217412698618177053)
XLA Ops:
  7.2 2.4 pad_maximum_fusion
  9.7 0.6 multiply_reduce_fusion
  11.7 0.7 dynamic-slice_bitcast_fusion.1
  12.4 0.7 copy.22.qseg_ref
  13.2 0.6 pad_add_fusion.scalars_ref
  13.8 110.9 %all-gather.4.cloned.1.call-done.k_ref.v_ref = bf16[2048,4096]{1,0:T(8,128)(2,1)} async-done(((bf16[128,4096]{1,0:T(8,128)(2,1)}), bf16[2048,4096]{1,0:T(8,128)(2,1)}) %all-gather.4.cloned.1.call-update) | async-done | bytes 16777232 | tf_op jit(solution)/shard_map/all_gather | solution.py:168
  124.7 13.3 %shard_map.166 = bf16[128,2048]{1,0:T(8,128)(2,1)} custom-call(s32[2]{0:T(128)} %pad_add_fusion.scalars_ref, f32[1]{0:T(128)} %bitcast.2.lam_ref, bf16[128,2048]{1,0:T(8,128)(2,1)} %q_ref.1, bf16[2048,4096]{1,0:T(8,128)(2,1)} %all-gather.4.cloned.1.call-done.k_ref.v_ref, bf16[2048,4096]{1,0:T(8,128)(2,1)} %all-gather.4.cloned.1.call-done.k_ref.v_ref, ...), custom_call_target="tpu_custom_call" | custom-call | flops 1811939328 | bytes 17825792 | tf_op jit(solution)/shard_map/pallas_call | solution.py:73
  138.0 5.6 %fusion = bf16[128,2048]{1,0:T(8,128)(2,1)} fusion(bf16[128,2048]{1,0:T(8,128)(2,1)} %shard_map.166, bf16[2048,2048]{1,0:T(8,128)(2,1)} %param.21, bf16[128,2048]{1,0:T(8,128)(2,1)} %param.15), kind=kOutput, calls=%fused_computation.3 | convolution fusion | flops 1074528256 | bytes 9961472 | tf_op jit(solution)/shard_map/dot_general | solution.py:172
  143.8 31.8 %all-gather.6.cloned.1.call-done.x_ref = bf16[1024,2048]{1,0:T(8,128)(2,1)} async-done(((bf16[128,2048]{1,0:T(8,128)(2,1)}), bf16[1024,2048]{1,0:T(8,128)(2,1)}) %all-gather.6.cloned.1.call-update) | async-done | bytes 4194320 | tf_op jit(solution)/shard_map/all_gather | solution.py:174
  175.6 1.8 copy-done.1
  177.4 1.8 copy-done.2
  179.2 14.5 %shard_map.167 = bf16[1024,2048]{1,0:T(8,128)(2,1)} custom-call(bf16[1024,2048]{1,0:T(8,128)(2,1)} %all-gather.6.cloned.1.call-done.x_ref, f32[1,2048]{1,0:T(1,128)S(1)} %bitcast.32, bf16[704,2048]{1,0:T(8,128)(2,1)S(1)} %bitcast.30, bf16[704,2048]{1,0:T(8,128)(2,1)S(1)} %bitcast.31, bf16[704,2048]{1,0:T(8,128)(2,1)} %down_ref.1), custom_call_target="tpu_custom_call" | custom-call | flops 8858370048 | bytes 17039360 | tf_op jit(solution)/shard_map/pallas_call | solution.py:113
  193.8 37.9 %reduce-scatter.2.cloned.1.call-done = bf16[128,2048]{1,0:T(8,128)(2,1)} async-done(((bf16[1024,2048]{1,0:T(8,128)(2,1)}), bf16[128,2048]{1,0:T(8,128)(2,1)}) %reduce-scatter.2.cloned.1.call-update) | async-done | bytes 524304 | tf_op jit(solution)/shard_map/reduce_scatter | solution.py:176
  231.7 1.5 fusion.1
  233.2 0.8 copy-done.5
  234.0 1.0 fusion.3
  235.0 31.2 %all-gather.8.cloned.1.call-done = bf16[1024,2048]{1,0:T(8,128)(2,1)} async-done(((bf16[128,2048]{1,0:T(8,128)(2,1)}), bf16[1024,2048]{1,0:T(8,128)(2,1)}) %all-gather.8.cloned.1.call-update) | async-done | bytes 4194320 | tf_op jit(solution)/shard_map/all_gather | solution.py:180
  266.2 6.8 %convolution_convert_fusion = bf16[1024,768]{1,0:T(8,128)(2,1)} fusion(bf16[1024,2048]{1,0:T(8,128)(2,1)} %all-gather.8.cloned.1.call-done, bf16[2048,768]{1,0:T(8,128)(2,1)S(1)} %copy-done), kind=kOutput, calls=%fused_computation.4 | convolution fusion | flops 3222011904 | bytes 8912896 | tf_op jit(solution)/shard_map/dot_general | solution.py:179
  272.9 4.4 %all-to-all-start = ((bf16[8,128,768]{2,1,0:T(8,128)(2,1)}), bf16[8,128,768]{2,1,0:T(8,128)(2,1)}, u32[]{:S(2)}, u32[]{:S(2)}) async-start(bf16[8,128,768]{2,1,0:T(8,128)(2,1)} %bitcast.36), calls=%async_computation.1 | async-start | bytes 3145728 | tf_op jit(solution)/shard_map/all_to_all | solution.py:186
  277.4 0.5 broadcast.75
  277.9 0.7 reduce.8
  278.6 0.1 select_reduce_fusion.2
  278.8 20.2 %all-to-all-done = bf16[8,128,768]{2,1,0:T(8,128)(2,1)} async-done(((bf16[8,128,768]{2,1,0:T(8,128)(2,1)}), bf16[8,128,768]{2,1,0:T(8,128)(2,1)}, u32[]{:S(2)}, u32[]{:S(2)}) %all-to-all-start) | async-done | bytes 1572896 | tf_op jit(solution)/shard_map/all_to_all | solution.py:186
  298.9 1.6 copy.24
  300.5 1.2 copy-done.4
  301.7 1.0 slice_bitcast_fusion
  302.7 2.8 gather_fusion
  305.5 7.0 %all-to-all-start.1 = ((bf16[16,1,8,4096]{3,2,1,0:T(8,128)(2,1)}), bf16[16,1,8,4096]{3,2,1,0:T(8,128)(2,1)}, u32[]{:S(2)}, u32[]{:S(2)}) async-start(bf16[16,1,8,4096]{3,2,1,0:T(8,128)(2,1)} %bitcast.35), calls=%async_computation.2 | async-start | bytes 2097152 | tf_op jit(solution)/shard_map/all_to_all | solution.py:202
  312.5 0.7 reduce.9
  313.5 1.9 slice.28
  315.4 14.5 %all-to-all-done.1 = bf16[16,1,8,4096]{3,2,1,0:T(8,128)(2,1)} async-done(((bf16[16,1,8,4096]{3,2,1,0:T(8,128)(2,1)}), bf16[16,1,8,4096]{3,2,1,0:T(8,128)(2,1)}, u32[]{:S(2)}, u32[]{:S(2)}) %all-to-all-start.1) | async-done | bytes 1048608 | tf_op jit(solution)/shard_map/all_to_all | solution.py:202
  330.0 2.8 gather_fusion.1
  (34 shorter events, 0.7 us)
Async XLA Ops:
  7.2 259.0 %copy-start = (bf16[2048,768]{1,0:T(8,128)(2,1)S(1)}, bf16[2048,768]{1,0:T(8,128)(2,1)}, u32[]{:S(2)}) copy-start(bf16[2048,768]{1,0:T(8,128)(2,1)} %param.27) | copy-start | bytes 9437188
  7.2 2.6 copy-start.7
  7.2 117.5 %all-gather.4.cloned.1.call-start = ((), (), s32[]{:S(2)}) async-start(), calls=%async_computation.3 | async-start | bytes 17825792 | tf_op jit(solution)/shard_map/all_gather | solution.py:168
  9.7 165.9 %all-gather.6.cloned.1.call-start = ((), (), s32[]{:S(2)}) async-start(), calls=%async_computation.4 | async-start | bytes 4718592 | tf_op jit(solution)/shard_map/all_gather | solution.py:174
  138.0 37.5 %copy-start.3 = (f32[2048]{0:T(1024)S(1)}, f32[2048]{0:T(1024)}, u32[]{:S(2)}) copy-start(f32[2048]{0:T(1024)} %param.22) | copy-start | bytes 24580
  143.7 88.0 %reduce-scatter.2.cloned.1.call-start = ((), (), s32[]{:S(2)}) async-start(), calls=%async_computation.5 | async-start | bytes 4718592 | tf_op jit(solution)/shard_map/reduce_scatter | solution.py:176
  175.6 1.8 copy-start.1
  177.4 1.8 copy-start.2
  193.7 40.2 %copy-start.6 = (f32[2048]{0:T(1024)S(1)}, f32[2048]{0:T(1024)}, u32[]{:S(2)}) copy-start(f32[2048]{0:T(1024)} %param.26) | copy-start | bytes 24580
  193.8 72.4 %all-gather.8.cloned.1.call-start = ((), (), s32[]{:S(2)}) async-start(), calls=%async_computation.6 | async-start | bytes 4718592 | tf_op jit(solution)/shard_map/all_gather | solution.py:180
  233.2 0.8 copy-start.5
  272.9 4.9 %copy-start.8 = (s32[1,256]{1,0:T(1,128)S(1)}, s32[1,256]{1,0:T(1,128)}, u32[]{:S(2)}) copy-start(s32[1,256]{1,0:T(1,128)} %param.28) | copy-start | bytes 3076
  272.9 26.0 %all-to-all-start = ((bf16[8,128,768]{2,1,0:T(8,128)(2,1)}), bf16[8,128,768]{2,1,0:T(8,128)(2,1)}, u32[]{:S(2)}, u32[]{:S(2)}) async-start(bf16[8,128,768]{2,1,0:T(8,128)(2,1)} %bitcast.36), calls=%async_computation.1 | async-start | bytes 3145728 | tf_op jit(solution)/shard_map/all_to_all | solution.py:186
  300.5 1.2 copy-start.4
  301.7 10.9 %copy-start.9 = (s32[1,256]{1,0:T(1,128)S(1)}, s32[1,256]{1,0:T(1,128)}, u32[]{:S(2)}) copy-start(s32[1,256]{1,0:T(1,128)} %param.29) | copy-start | bytes 3076
  305.5 24.4 %all-to-all-start.1 = ((bf16[16,1,8,4096]{3,2,1,0:T(8,128)(2,1)}), bf16[16,1,8,4096]{3,2,1,0:T(8,128)(2,1)}, u32[]{:S(2)}, u32[]{:S(2)}) async-start(bf16[16,1,8,4096]{3,2,1,0:T(8,128)(2,1)} %bitcast.35), calls=%async_computation.2 | async-start | bytes 2097152 | tf_op jit(solution)/shard_map/all_to_all | solution.py:202
Sparse Core Ops, SparseCore 0:
  10.7 113.9 all-gather.3
  143.8 31.6 all-gather.5
  193.9 37.7 reduce-scatter.1
  235.1 31.0 all-gather.7

commit v9 on v8

--- a/solution.py
+++ b/solution.py
@@ -93,44 +93,58 @@
     )(scalars, lam, q_in, all_kv, all_kv, query_segs.reshape(rows, 1), seg_row.reshape(1, keys))
 
 
-def ffn_kernel(x_ref, gain_ref, gate_ref, up_ref, down_ref, out_ref):
-    normed = (rms_rows(x_ref[...].astype(jnp.float32)) * gain_ref[...]).astype(jnp.bfloat16)
+def ffn_kernel(x_ref, gain_ref, gate_ref, up_ref, down_ref, out_ref, normed_ref, total_ref):
+    step = pl.program_id(0)
+
+    @pl.when(step == 0)
+    def _():
+        normed_ref[...] = (rms_rows(x_ref[...].astype(jnp.float32)) * gain_ref[...]).astype(
+            jnp.bfloat16
+        )
+        total_ref[...] = jnp.zeros_like(total_ref)
+
+    normed = normed_ref[...]
     contract = (((1,), (1,)), ((), ()))
     gate_proj = lax.dot_general(normed, gate_ref[...], contract, preferred_element_type=jnp.float32)
     up_proj = lax.dot_general(normed, up_ref[...], contract, preferred_element_type=jnp.float32)
     hidden = (gate_proj / (1.0 + jnp.exp(-gate_proj)) * up_proj).astype(jnp.bfloat16)
-    out_ref[...] = jnp.dot(hidden, down_ref[...], preferred_element_type=jnp.float32).astype(
-        out_ref.dtype
-    )
-
-
-def ffn_partial(rows, gain, gate_weight, up_weight, down_weight, tile):
+    total_ref[...] += jnp.dot(hidden, down_ref[...], preferred_element_type=jnp.float32)
+
+    @pl.when(step == pl.num_programs(0) - 1)
+    def _():
+        out_ref[...] = total_ref[...].astype(out_ref.dtype)
+
+
+def ffn_partial(rows, gain, gate_weight, up_weight, down_weight, chunk):
     count, width = rows.shape
     hidden_w = gate_weight.shape[1]
     full = lambda i: (0, 0)
-    gate_t = gate_weight.T
-    up_t = up_weight.T
+    part = lambda i: (i, 0)
     return pl.pallas_call(
         ffn_kernel,
         out_shape=jax.ShapeDtypeStruct((count, width), jnp.bfloat16),
-        grid=(count // tile,),
+        grid=(hidden_w // chunk,),
         in_specs=[
-            pl.BlockSpec((tile, width), lambda i: (i, 0)),
+            pl.BlockSpec((count, width), full),
             pl.BlockSpec((1, width), full),
-            pl.BlockSpec((hidden_w, width), full),
-            pl.BlockSpec((hidden_w, width), full),
-            pl.BlockSpec((hidden_w, width), full),
+            pl.BlockSpec((chunk, width), part),
+            pl.BlockSpec((chunk, width), part),
+            pl.BlockSpec((chunk, width), part),
         ],
-        out_specs=pl.BlockSpec((tile, width), lambda i: (i, 0)),
+        out_specs=pl.BlockSpec((count, width), full),
+        scratch_shapes=[
+            pltpu.VMEM((count, width), jnp.bfloat16),
+            pltpu.VMEM((count, width), jnp.float32),
+        ],
         compiler_params=pltpu.CompilerParams(
-            dimension_semantics=("arbitrary",), vmem_limit_bytes=48 * 1024 * 1024
+            dimension_semantics=("arbitrary",), vmem_limit_bytes=56 * 1024 * 1024
         ),
         cost_estimate=pl.CostEstimate(
             flops=6 * count * width * hidden_w,
             bytes_accessed=3 * width * hidden_w * 2 + 2 * count * width * 2,
             transcendentals=count * hidden_w,
         ),
-    )(rows, gain.reshape(1, width), gate_t, up_t, down_weight)
+    )(rows, gain.reshape(1, width), gate_weight.T, up_weight.T, down_weight)
 
 
 def body(
@@ -172,7 +186,7 @@
         + jnp.dot(attention, out_weight, preferred_element_type=jnp.float32)
     ).astype(jnp.bfloat16)
     gathered = lax.all_gather(residual_mid, "req", axis=0, tiled=True)
-    partial = ffn_partial(gathered, ffn_gain, gate_weight, up_weight, down_weight, 256)
+    partial = ffn_partial(gathered, ffn_gain, gate_weight, up_weight, down_weight, 176)
     ffn_own = lax.psum_scatter(partial, "req", scatter_dimension=0, tiled=True).astype(jnp.float32)
     layer_output = (residual_mid.astype(jnp.float32) + ffn_own).astype(jnp.bfloat16)
     next_normed = (rms_rows(layer_output.astype(jnp.float32)) * next_gain).astype(jnp.bfloat16)

time: 340 us -> 343 us (level)
  Pallas kernels: 27.9 us -> 34.7 us
  local copies, waits for them, and re-layouts: 17.8 us -> 14.2 us
    pallas_call x1, Pallas kernels: 14.5 us -> 21.3 us  [ffn_partial(): pl.pallas_call(ffn_kernel, out_shape=jax.ShapeDtypeStruct((count, width),...]
    unnamed x21 -> x15, local copies, waits for them, and re-layouts: 6.1 us -> 2.46 us
where the time goes in v9:
time: 343 us; the launch traced here: 342 us
  waiting for transfers between devices  246 us (72%)
  Pallas kernels  34.7 us (10%)
  between operations  15.3 us (4%)
  local copies, waits for them, and re-layouts  14.2 us (4%)
  matrix products  12.4 us (4%)
  starting transfers between devices  11.6 us (3%)
  other arithmetic  7.91 us (2%)
    all_gather x1, waiting for transfers between devices, body(): all_kv = lax.all_gather(own_kv, 'tok', axis=0, tiled=True)  111 us
    reduce_scatter x1, waiting for transfers between devices, body(): lax.psum_scatter(partial, 'req', scatter_dimension=0, tiled=True)  37.9 us
    all_gather x1, waiting for transfers between devices, body(): gathered = lax.all_gather(residual_mid, 'req', axis=0, tiled=True)  31.8 us
    all_gather x1, waiting for transfers between devices, body(): lax.all_gather(next_normed, 'req', axis=0, tiled=True)  31.2 us
    pallas_call x1, Pallas kernels, ffn_partial(): pl.pallas_call(ffn_kernel, out_shape=jax.ShapeDtypeStruct((count, width),...  21.3 us
    all_to_all x1, waiting for transfers between devices, body(): lax.all_to_all(projected_cols.reshape(n_req, row_count, col_w), 'req', 0,...  20.2 us
    all_to_all x1, waiting for transfers between devices, body(): lax.all_to_all(outgoing, 'tok', split_axis=0, concat_axis=0, tiled=True)  14.5 us
    pallas_call x1, Pallas kernels, window_attention(): pl.pallas_call(functools.partial(attention_kernel, back, head_w // 2), ou...  13.3 us
  transfers between devices with their start and end apart: 6, of which 6 were waited for; matrix products, arithmetic and copies ran while one was open for 2% of the time, Pallas kernels for 0%

profile of v9, /device:TPU:0, one launch (start us, length us, event | category | flops | bytes accessed | tf_op | source)
XLA Modules:
  0.0 342.5 jit_solution(14670785614184048249)
XLA Ops:
  7.2 2.4 pad_maximum_fusion
  9.7 0.7 multiply_reduce_fusion
  11.8 0.7 dynamic-slice_bitcast_fusion.1
  12.5 0.7 copy.22.qseg_ref
  13.3 0.7 pad_add_fusion.scalars_ref
  13.9 110.8 %all-gather.4.cloned.1.call-done.k_ref.v_ref = bf16[2048,4096]{1,0:T(8,128)(2,1)} async-done(((bf16[128,4096]{1,0:T(8,128)(2,1)}), bf16[2048,4096]{1,0:T(8,128)(2,1)}) %all-gather.4.cloned.1.call-update) | async-done | bytes 16777232 | tf_op jit(solution)/shard_map/all_gather | solution.py:182
  124.7 13.3 %shard_map.166 = bf16[128,2048]{1,0:T(8,128)(2,1)} custom-call(s32[2]{0:T(128)} %pad_add_fusion.scalars_ref, f32[1]{0:T(128)} %bitcast.2.lam_ref, bf16[128,2048]{1,0:T(8,128)(2,1)} %q_ref.1, bf16[2048,4096]{1,0:T(8,128)(2,1)} %all-gather.4.cloned.1.call-done.k_ref.v_ref, bf16[2048,4096]{1,0:T(8,128)(2,1)} %all-gather.4.cloned.1.call-done.k_ref.v_ref, ...), custom_call_target="tpu_custom_call" | custom-call | flops 1811939328 | bytes 17825792 | tf_op jit(solution)/shard_map/pallas_call | solution.py:73
  138.0 5.6 %fusion = bf16[128,2048]{1,0:T(8,128)(2,1)} fusion(bf16[128,2048]{1,0:T(8,128)(2,1)} %shard_map.166, bf16[2048,2048]{1,0:T(8,128)(2,1)} %param.21, bf16[128,2048]{1,0:T(8,128)(2,1)} %param.15), kind=kOutput, calls=%fused_computation.3 | convolution fusion | flops 1074528256 | bytes 9961472 | tf_op jit(solution)/shard_map/dot_general | solution.py:186
  143.7 31.8 %all-gather.6.cloned.1.call-done.x_ref = bf16[1024,2048]{1,0:T(8,128)(2,1)} async-done(((bf16[128,2048]{1,0:T(8,128)(2,1)}), bf16[1024,2048]{1,0:T(8,128)(2,1)}) %all-gather.6.cloned.1.call-update) | async-done | bytes 4194320 | tf_op jit(solution)/shard_map/all_gather | solution.py:188
  175.6 21.3 %shard_map.167 = bf16[1024,2048]{1,0:T(8,128)(2,1)} custom-call(bf16[1024,2048]{1,0:T(8,128)(2,1)} %all-gather.6.cloned.1.call-done.x_ref, f32[1,2048]{1,0:T(1,128)} %bitcast.36, bf16[704,2048]{1,0:T(8,128)(2,1)} %bitcast.34, bf16[704,2048]{1,0:T(8,128)(2,1)} %bitcast.35, bf16[704,2048]{1,0:T(8,128)(2,1)} %down_ref.1), custom_call_target="tpu_custom_call" | custom-call | flops 8858370048 | bytes 17039360 | tf_op jit(solution)/shard_map/pallas_call | solution.py:123
  197.0 37.9 %reduce-scatter.2.cloned.1.call-done = bf16[128,2048]{1,0:T(8,128)(2,1)} async-done(((bf16[1024,2048]{1,0:T(8,128)(2,1)}), bf16[128,2048]{1,0:T(8,128)(2,1)}) %reduce-scatter.2.cloned.1.call-update) | async-done | bytes 524304 | tf_op jit(solution)/shard_map/reduce_scatter | solution.py:190
  234.9 1.5 fusion.1
  236.3 0.8 copy-done.2
  237.1 1.0 fusion.3
  238.1 31.2 %all-gather.8.cloned.1.call-done = bf16[1024,2048]{1,0:T(8,128)(2,1)} async-done(((bf16[128,2048]{1,0:T(8,128)(2,1)}), bf16[1024,2048]{1,0:T(8,128)(2,1)}) %all-gather.8.cloned.1.call-update) | async-done | bytes 4194320 | tf_op jit(solution)/shard_map/all_gather | solution.py:194
  269.3 6.8 %convolution_convert_fusion = bf16[1024,768]{1,0:T(8,128)(2,1)} fusion(bf16[1024,2048]{1,0:T(8,128)(2,1)} %all-gather.8.cloned.1.call-done, bf16[2048,768]{1,0:T(8,128)(2,1)S(1)} %copy-done), kind=kOutput, calls=%fused_computation.4 | convolution fusion | flops 3222011904 | bytes 8912896 | tf_op jit(solution)/shard_map/dot_general | solution.py:193
  276.1 4.4 %all-to-all-start = ((bf16[8,128,768]{2,1,0:T(8,128)(2,1)}), bf16[8,128,768]{2,1,0:T(8,128)(2,1)}, u32[]{:S(2)}, u32[]{:S(2)}) async-start(bf16[8,128,768]{2,1,0:T(8,128)(2,1)} %bitcast.33), calls=%async_computation.1 | async-start | bytes 3145728 | tf_op jit(solution)/shard_map/all_to_all | solution.py:200
  280.5 0.5 broadcast.75
  281.0 0.7 reduce.8
  281.8 0.1 select_reduce_fusion.2
  281.9 20.2 %all-to-all-done = bf16[8,128,768]{2,1,0:T(8,128)(2,1)} async-done(((bf16[8,128,768]{2,1,0:T(8,128)(2,1)}), bf16[8,128,768]{2,1,0:T(8,128)(2,1)}, u32[]{:S(2)}, u32[]{:S(2)}) %all-to-all-start) | async-done | bytes 1572896 | tf_op jit(solution)/shard_map/all_to_all | solution.py:200
  302.1 1.6 copy.24
  303.7 1.1 copy-done.1
  304.8 1.0 slice_bitcast_fusion
  305.8 2.8 gather_fusion
  308.7 7.0 %all-to-all-start.1 = ((bf16[16,1,8,4096]{3,2,1,0:T(8,128)(2,1)}), bf16[16,1,8,4096]{3,2,1,0:T(8,128)(2,1)}, u32[]{:S(2)}, u32[]{:S(2)}) async-start(bf16[16,1,8,4096]{3,2,1,0:T(8,128)(2,1)} %bitcast.32), calls=%async_computation.2 | async-start | bytes 2097152 | tf_op jit(solution)/shard_map/all_to_all | solution.py:216
  315.7 0.7 reduce.9
  316.4 0.1 select_reduce_fusion.1
  316.6 0.1 select_reduce_fusion
  316.7 1.9 slice.28
  318.6 14.5 %all-to-all-done.1 = bf16[16,1,8,4096]{3,2,1,0:T(8,128)(2,1)} async-done(((bf16[16,1,8,4096]{3,2,1,0:T(8,128)(2,1)}), bf16[16,1,8,4096]{3,2,1,0:T(8,128)(2,1)}, u32[]{:S(2)}, u32[]{:S(2)}) %all-to-all-start.1) | async-done | bytes 1048608 | tf_op jit(solution)/shard_map/all_to_all | solution.py:216
  333.1 2.8 gather_fusion.1
  (28 shorter events, 0.5 us)
Async XLA Ops:
  7.2 262.1 %copy-start = (bf16[2048,768]{1,0:T(8,128)(2,1)S(1)}, bf16[2048,768]{1,0:T(8,128)(2,1)}, u32[]{:S(2)}) copy-start(bf16[2048,768]{1,0:T(8,128)(2,1)} %param.27) | copy-start | bytes 9437188
  7.2 2.6 copy-start.4
  7.2 117.5 %all-gather.4.cloned.1.call-start = ((), (), s32[]{:S(2)}) async-start(), calls=%async_computation.3 | async-start | bytes 17825792 | tf_op jit(solution)/shard_map/all_gather | solution.py:182
  9.7 165.9 %all-gather.6.cloned.1.call-start = ((), (), s32[]{:S(2)}) async-start(), calls=%async_computation.4 | async-start | bytes 4718592 | tf_op jit(solution)/shard_map/all_gather | solution.py:188
  143.7 91.2 %reduce-scatter.2.cloned.1.call-start = ((), (), s32[]{:S(2)}) async-start(), calls=%async_computation.5 | async-start | bytes 4718592 | tf_op jit(solution)/shard_map/reduce_scatter | solution.py:190
  196.9 40.2 %copy-start.3 = (f32[2048]{0:T(1024)S(1)}, f32[2048]{0:T(1024)}, u32[]{:S(2)}) copy-start(f32[2048]{0:T(1024)} %param.26) | copy-start | bytes 24580
  196.9 72.4 %all-gather.8.cloned.1.call-start = ((), (), s32[]{:S(2)}) async-start(), calls=%async_computation.6 | async-start | bytes 4718592 | tf_op jit(solution)/shard_map/all_gather | solution.py:194
  236.3 0.8 copy-start.2
  276.1 4.9 %copy-start.5 = (s32[1,256]{1,0:T(1,128)S(1)}, s32[1,256]{1,0:T(1,128)}, u32[]{:S(2)}) copy-start(s32[1,256]{1,0:T(1,128)} %param.28) | copy-start | bytes 3076
  276.1 26.0 %all-to-all-start = ((bf16[8,128,768]{2,1,0:T(8,128)(2,1)}), bf16[8,128,768]{2,1,0:T(8,128)(2,1)}, u32[]{:S(2)}, u32[]{:S(2)}) async-start(bf16[8,128,768]{2,1,0:T(8,128)(2,1)} %bitcast.33), calls=%async_computation.1 | async-start | bytes 3145728 | tf_op jit(solution)/shard_map/all_to_all | solution.py:200
  303.6 1.2 copy-start.1
  304.8 10.9 %copy-start.6 = (s32[1,256]{1,0:T(1,128)S(1)}, s32[1,256]{1,0:T(1,128)}, u32[]{:S(2)}) copy-start(s32[1,256]{1,0:T(1,128)} %param.29) | copy-start | bytes 3076
  308.7 24.5 %all-to-all-start.1 = ((bf16[16,1,8,4096]{3,2,1,0:T(8,128)(2,1)}), bf16[16,1,8,4096]{3,2,1,0:T(8,128)(2,1)}, u32[]{:S(2)}, u32[]{:S(2)}) async-start(bf16[16,1,8,4096]{3,2,1,0:T(8,128)(2,1)} %bitcast.32), calls=%async_computation.2 | async-start | bytes 2097152 | tf_op jit(solution)/shard_map/all_to_all | solution.py:216
Sparse Core Ops, SparseCore 0:
  10.7 113.9 all-gather.3
  143.8 31.6 all-gather.5
  197.0 37.7 reduce-scatter.1
  238.3 30.9 all-gather.7

commit v10 on v8

--- a/solution.py
+++ b/solution.py
@@ -28,7 +28,9 @@
     return first_term - second_term + LAMBDA_INIT
 
 
-def attention_kernel(back, head_dim, scalars_ref, lam_ref, q_ref, k_ref, v_ref, qseg_ref, kseg_ref, out_ref):
+def attention_kernel(
+    back, head_dim, scalars_ref, lam_ref, q_ref, k_ref, v_ref, qseg_ref, kseg_ref, w_ref, base_ref, out_ref, total_ref
+):
     rows = q_ref.shape[0]
     span = (back + 1) * rows
     start = pl.multiple_of(scalars_ref[0], rows)
@@ -57,10 +59,21 @@
         )
         map_outputs.append(map_out)
     difference = map_outputs[0] - lam_ref[0] * map_outputs[1]
-    out_ref[...] = (rms_rows(difference) * (1.0 - LAMBDA_INIT)).astype(out_ref.dtype)
-
-
-def window_attention(q_in, all_kv, query_segs, seg_row, first_row, lambda_mix, back):
+    head_out = (rms_rows(difference) * (1.0 - LAMBDA_INIT)).astype(jnp.bfloat16)
+    step = pl.program_id(0)
+
+    @pl.when(step == 0)
+    def _():
+        total_ref[...] = jnp.zeros_like(total_ref)
+
+    total_ref[...] += jnp.dot(head_out, w_ref[...], preferred_element_type=jnp.float32)
+
+    @pl.when(step == pl.num_programs(0) - 1)
+    def _():
+        out_ref[...] = (base_ref[...].astype(jnp.float32) + total_ref[...]).astype(out_ref.dtype)
+
+
+def window_attention(q_in, all_kv, query_segs, seg_row, first_row, lambda_mix, back, out_weight, base):
     rows, width = q_in.shape
     keys = all_kv.shape[0]
     head_w = width // HEADS
@@ -68,7 +81,7 @@
     scalars = jnp.stack([start, first_row]).astype(jnp.int32)
     lam = jnp.reshape(lambda_mix, (1,)).astype(jnp.float32)
     span = (back + 1) * rows
-    flops = HEADS * 2 * (2 * rows * span * (head_w // 2) + 2 * rows * span * head_w)
+    flops = HEADS * 2 * (2 * rows * span * (head_w // 2) + 2 * rows * span * head_w) + 2 * rows * width * width
     smem = pl.BlockSpec(memory_space=pltpu.SMEM)
     return pl.pallas_call(
         functools.partial(attention_kernel, back, head_w // 2),
@@ -82,15 +95,28 @@
             pl.BlockSpec((keys, head_w), lambda h: (0, HEADS + h)),
             pl.BlockSpec((rows, 1), lambda h: (0, 0)),
             pl.BlockSpec((1, keys), lambda h: (0, 0)),
+            pl.BlockSpec((head_w, width), lambda h: (h, 0)),
+            pl.BlockSpec((rows, width), lambda h: (0, 0)),
         ],
-        out_specs=pl.BlockSpec((rows, head_w), lambda h: (0, h)),
+        out_specs=pl.BlockSpec((rows, width), lambda h: (0, 0)),
+        scratch_shapes=[pltpu.VMEM((rows, width), jnp.float32)],
         compiler_params=pltpu.CompilerParams(dimension_semantics=("arbitrary",)),
         cost_estimate=pl.CostEstimate(
             flops=flops,
-            bytes_accessed=2 * keys * width * 2 + 2 * rows * width * 2,
+            bytes_accessed=2 * keys * width * 2 + 3 * rows * width * 2 + width * width * 2,
             transcendentals=HEADS * 2 * rows * span,
         ),
-    )(scalars, lam, q_in, all_kv, all_kv, query_segs.reshape(rows, 1), seg_row.reshape(1, keys))
+    )(
+        scalars,
+        lam,
+        q_in,
+        all_kv,
+        all_kv,
+        query_segs.reshape(rows, 1),
+        seg_row.reshape(1, keys),
+        out_weight,
+        base,
+    )
 
 
 def ffn_kernel(x_ref, gain_ref, gate_ref, up_ref, down_ref, out_ref):
@@ -166,11 +192,9 @@
     back = -(-(MAX_SEG - 1) // row_count)
     own_kv = jnp.concatenate([k_in, v_in], axis=1)
     all_kv = lax.all_gather(own_kv, "tok", axis=0, tiled=True)
-    attention = window_attention(q_in, all_kv, query_segs, seg_row, first_row, lambda_mix, back)
-    residual_mid = (
-        layer_input.astype(jnp.float32)
-        + jnp.dot(attention, out_weight, preferred_element_type=jnp.float32)
-    ).astype(jnp.bfloat16)
+    residual_mid = window_attention(
+        q_in, all_kv, query_segs, seg_row, first_row, lambda_mix, back, out_weight, layer_input
+    )
     gathered = lax.all_gather(residual_mid, "req", axis=0, tiled=True)
     partial = ffn_partial(gathered, ffn_gain, gate_weight, up_weight, down_weight, 256)
     ffn_own = lax.psum_scatter(partial, "req", scatter_dimension=0, tiled=True).astype(jnp.float32)

time: 340 us -> 338 us (level)
  matrix products: 12.4 us -> 6.78 us
    dot_general x1 -> x0, matrix products: 5.65 us -> none  [body(): jnp.dot(attention, out_weight, preferred_element_type=jnp.float32)]
where the time goes in v10:
time: 338 us; the launch traced here: 337 us
  waiting for transfers between devices  247 us (73%)
  Pallas kernels  31.2 us (9%)
  local copies, waits for them, and re-layouts  17.8 us (5%)
  between operations  15.3 us (5%)
  starting transfers between devices  11.6 us (3%)
  other arithmetic  7.81 us (2%)
  matrix products  6.78 us (2%)
    all_gather x1, waiting for transfers between devices, body(): all_kv = lax.all_gather(own_kv, 'tok', axis=0, tiled=True)  111 us
    reduce_scatter x1, waiting for transfers between devices, body(): lax.psum_scatter(partial, 'req', scatter_dimension=0, tiled=True)  37.9 us
    all_gather x1, waiting for transfers between devices, body(): gathered = lax.all_gather(residual_mid, 'req', axis=0, tiled=True)  31.8 us
    all_gather x1, waiting for transfers between devices, body(): lax.all_gather(next_normed, 'req', axis=0, tiled=True)  31.2 us
    all_to_all x1, waiting for transfers between devices, body(): lax.all_to_all(projected_cols.reshape(n_req, row_count, col_w), 'req', 0,...  20.2 us
    pallas_call x1, Pallas kernels, window_attention(): pl.pallas_call(functools.partial(attention_kernel, back, head_w // 2), ou...  16.6 us
    pallas_call x1, Pallas kernels, ffn_partial(): pl.pallas_call(ffn_kernel, out_shape=jax.ShapeDtypeStruct((count, width),...  14.6 us
    all_to_all x1, waiting for transfers between devices, body(): lax.all_to_all(outgoing, 'tok', split_axis=0, concat_axis=0, tiled=True)  14.5 us
  transfers between devices with their start and end apart: 6, of which 6 were waited for; matrix products, arithmetic and copies ran while one was open for 2% of the time, Pallas kernels for 0%

profile of v10, /device:TPU:0, one launch (start us, length us, event | category | flops | bytes accessed | tf_op | source)
XLA Modules:
  0.0 337.0 jit_solution(5100782503680402163)
XLA Ops:
  7.2 2.4 pad_maximum_fusion
  9.7 0.6 multiply_reduce_fusion
  11.7 0.7 dynamic-slice_bitcast_fusion.1
  12.4 0.7 copy.22.qseg_ref
  13.2 0.6 pad_add_fusion.scalars_ref
  13.8 110.9 %all-gather.4.cloned.1.call-done.k_ref.v_ref = bf16[2048,4096]{1,0:T(8,128)(2,1)} async-done(((bf16[128,4096]{1,0:T(8,128)(2,1)}), bf16[2048,4096]{1,0:T(8,128)(2,1)}) %all-gather.4.cloned.1.call-update) | async-done | bytes 16777232 | tf_op jit(solution)/shard_map/all_gather | solution.py:194
  124.7 16.6 %shard_map.166 = bf16[128,2048]{1,0:T(8,128)(2,1)} custom-call(s32[2]{0:T(128)} %pad_add_fusion.scalars_ref, f32[1]{0:T(128)} %bitcast.2.lam_ref, bf16[128,2048]{1,0:T(8,128)(2,1)} %q_ref.1, bf16[2048,4096]{1,0:T(8,128)(2,1)} %all-gather.4.cloned.1.call-done.k_ref.v_ref, bf16[2048,4096]{1,0:T(8,128)(2,1)} %all-gather.4.cloned.1.call-done.k_ref.v_ref, ...), custom_call_target="tpu_custom_call" | custom-call | flops 2885681152 | bytes 26738688 | tf_op jit(solution)/shard_map/pallas_call | solution.py:86
  141.4 31.8 %all-gather.6.cloned.1.call-done.x_ref = bf16[1024,2048]{1,0:T(8,128)(2,1)} async-done(((bf16[128,2048]{1,0:T(8,128)(2,1)}), bf16[1024,2048]{1,0:T(8,128)(2,1)}) %all-gather.6.cloned.1.call-update) | async-done | bytes 4194320 | tf_op jit(solution)/shard_map/all_gather | solution.py:198
  173.2 1.8 copy-done.1
  175.1 1.8 copy-done.2
  176.9 14.6 %shard_map.167 = bf16[1024,2048]{1,0:T(8,128)(2,1)} custom-call(bf16[1024,2048]{1,0:T(8,128)(2,1)} %all-gather.6.cloned.1.call-done.x_ref, f32[1,2048]{1,0:T(1,128)S(1)} %bitcast.30, bf16[704,2048]{1,0:T(8,128)(2,1)S(1)} %bitcast.28, bf16[704,2048]{1,0:T(8,128)(2,1)S(1)} %bitcast.29, bf16[704,2048]{1,0:T(8,128)(2,1)} %down_ref.1), custom_call_target="tpu_custom_call" | custom-call | flops 8858370048 | bytes 17039360 | tf_op jit(solution)/shard_map/pallas_call | solution.py:139
  191.5 37.9 %reduce-scatter.2.cloned.1.call-done = bf16[128,2048]{1,0:T(8,128)(2,1)} async-done(((bf16[1024,2048]{1,0:T(8,128)(2,1)}), bf16[128,2048]{1,0:T(8,128)(2,1)}) %reduce-scatter.2.cloned.1.call-update) | async-done | bytes 524304 | tf_op jit(solution)/shard_map/reduce_scatter | solution.py:200
  229.4 1.5 fusion
  230.9 0.8 copy-done.5
  231.7 1.0 fusion.2
  232.7 31.2 %all-gather.8.cloned.1.call-done = bf16[1024,2048]{1,0:T(8,128)(2,1)} async-done(((bf16[128,2048]{1,0:T(8,128)(2,1)}), bf16[1024,2048]{1,0:T(8,128)(2,1)}) %all-gather.8.cloned.1.call-update) | async-done | bytes 4194320 | tf_op jit(solution)/shard_map/all_gather | solution.py:204
  263.8 6.8 %convolution_convert_fusion = bf16[1024,768]{1,0:T(8,128)(2,1)} fusion(bf16[1024,2048]{1,0:T(8,128)(2,1)} %all-gather.8.cloned.1.call-done, bf16[2048,768]{1,0:T(8,128)(2,1)S(1)} %copy-done), kind=kOutput, calls=%fused_computation.2 | convolution fusion | flops 3222011904 | bytes 8912896 | tf_op jit(solution)/shard_map/dot_general | solution.py:203
  270.6 4.4 %all-to-all-start = ((bf16[8,128,768]{2,1,0:T(8,128)(2,1)}), bf16[8,128,768]{2,1,0:T(8,128)(2,1)}, u32[]{:S(2)}, u32[]{:S(2)}) async-start(bf16[8,128,768]{2,1,0:T(8,128)(2,1)} %bitcast.34), calls=%async_computation.1 | async-start | bytes 3145728 | tf_op jit(solution)/shard_map/all_to_all | solution.py:210
  275.0 0.5 broadcast.75
  275.6 0.7 reduce.8
  276.3 0.1 select_reduce_fusion.2
  276.4 20.2 %all-to-all-done = bf16[8,128,768]{2,1,0:T(8,128)(2,1)} async-done(((bf16[8,128,768]{2,1,0:T(8,128)(2,1)}), bf16[8,128,768]{2,1,0:T(8,128)(2,1)}, u32[]{:S(2)}, u32[]{:S(2)}) %all-to-all-start) | async-done | bytes 1572896 | tf_op jit(solution)/shard_map/all_to_all | solution.py:210
  296.6 1.6 copy.24
  298.2 1.2 copy-done.4
  299.4 1.0 slice_bitcast_fusion
  300.4 2.8 gather_fusion
  303.2 7.0 %all-to-all-start.1 = ((bf16[16,1,8,4096]{3,2,1,0:T(8,128)(2,1)}), bf16[16,1,8,4096]{3,2,1,0:T(8,128)(2,1)}, u32[]{:S(2)}, u32[]{:S(2)}) async-start(bf16[16,1,8,4096]{3,2,1,0:T(8,128)(2,1)} %bitcast.33), calls=%async_computation.2 | async-start | bytes 2097152 | tf_op jit(solution)/shard_map/all_to_all | solution.py:226
  310.2 0.7 reduce.9
  311.1 0.1 select_reduce_fusion
  311.2 1.9 slice.28
  313.1 14.5 %all-to-all-done.1 = bf16[16,1,8,4096]{3,2,1,0:T(8,128)(2,1)} async-done(((bf16[16,1,8,4096]{3,2,1,0:T(8,128)(2,1)}), bf16[16,1,8,4096]{3,2,1,0:T(8,128)(2,1)}, u32[]{:S(2)}, u32[]{:S(2)}) %all-to-all-start.1) | async-done | bytes 1048608 | tf_op jit(solution)/shard_map/all_to_all | solution.py:226
  327.7 2.8 gather_fusion.1
  (33 shorter events, 0.6 us)
Async XLA Ops:
  7.2 256.7 %copy-start = (bf16[2048,768]{1,0:T(8,128)(2,1)S(1)}, bf16[2048,768]{1,0:T(8,128)(2,1)}, u32[]{:S(2)}) copy-start(bf16[2048,768]{1,0:T(8,128)(2,1)} %param.27) | copy-start | bytes 9437188
  7.2 2.6 copy-start.7
  7.2 117.5 %all-gather.4.cloned.1.call-start = ((), (), s32[]{:S(2)}) async-start(), calls=%async_computation.3 | async-start | bytes 17825792 | tf_op jit(solution)/shard_map/all_gather | solution.py:194
  9.7 163.6 %all-gather.6.cloned.1.call-start = ((), (), s32[]{:S(2)}) async-start(), calls=%async_computation.4 | async-start | bytes 4718592 | tf_op jit(solution)/shard_map/all_gather | solution.py:198
  124.7 48.5 %copy-start.3 = (f32[2048]{0:T(1024)S(1)}, f32[2048]{0:T(1024)}, u32[]{:S(2)}) copy-start(f32[2048]{0:T(1024)} %param.22) | copy-start | bytes 24580
  141.4 88.0 %reduce-scatter.2.cloned.1.call-start = ((), (), s32[]{:S(2)}) async-start(), calls=%async_computation.5 | async-start | bytes 4718592 | tf_op jit(solution)/shard_map/reduce_scatter | solution.py:200
  173.2 1.8 copy-start.1
  175.1 1.8 copy-start.2
  191.4 40.2 %copy-start.6 = (f32[2048]{0:T(1024)S(1)}, f32[2048]{0:T(1024)}, u32[]{:S(2)}) copy-start(f32[2048]{0:T(1024)} %param.26) | copy-start | bytes 24580
  191.5 72.4 %all-gather.8.cloned.1.call-start = ((), (), s32[]{:S(2)}) async-start(), calls=%async_computation.6 | async-start | bytes 4718592 | tf_op jit(solution)/shard_map/all_gather | solution.py:204
  230.9 0.8 copy-start.5
  270.6 4.9 %copy-start.8 = (s32[1,256]{1,0:T(1,128)S(1)}, s32[1,256]{1,0:T(1,128)}, u32[]{:S(2)}) copy-start(s32[1,256]{1,0:T(1,128)} %param.28) | copy-start | bytes 3076
  270.6 26.0 %all-to-all-start = ((bf16[8,128,768]{2,1,0:T(8,128)(2,1)}), bf16[8,128,768]{2,1,0:T(8,128)(2,1)}, u32[]{:S(2)}, u32[]{:S(2)}) async-start(bf16[8,128,768]{2,1,0:T(8,128)(2,1)} %bitcast.34), calls=%async_computation.1 | async-start | bytes 3145728 | tf_op jit(solution)/shard_map/all_to_all | solution.py:210
  298.2 1.2 copy-start.4
  299.4 10.9 %copy-start.9 = (s32[1,256]{1,0:T(1,128)S(1)}, s32[1,256]{1,0:T(1,128)}, u32[]{:S(2)}) copy-start(s32[1,256]{1,0:T(1,128)} %param.29) | copy-start | bytes 3076
  303.2 24.4 %all-to-all-start.1 = ((bf16[16,1,8,4096]{3,2,1,0:T(8,128)(2,1)}), bf16[16,1,8,4096]{3,2,1,0:T(8,128)(2,1)}, u32[]{:S(2)}, u32[]{:S(2)}) async-start(bf16[16,1,8,4096]{3,2,1,0:T(8,128)(2,1)} %bitcast.33), calls=%async_computation.2 | async-start | bytes 2097152 | tf_op jit(solution)/shard_map/all_to_all | solution.py:226
Sparse Core Ops, SparseCore 0:
  10.7 113.9 all-gather.3
  141.5 31.6 all-gather.5
  191.6 37.7 reduce-scatter.1
  232.8 31.0 all-gather.7

commit v11 on v10

--- a/solution.py
+++ b/solution.py
@@ -157,6 +157,35 @@
             transcendentals=count * hidden_w,
         ),
     )(rows, gain.reshape(1, width), gate_t, up_t, down_weight)
+
+
+def project_kernel(x_ref, w_ref, out_ref):
+    out_ref[...] = jnp.dot(x_ref[...], w_ref[...], preferred_element_type=jnp.float32).astype(
+        out_ref.dtype
+    )
+
+
+def project_rows(rows, weight, tile):
+    count, width = rows.shape
+    cols = weight.shape[1]
+    return pl.pallas_call(
+        project_kernel,
+        out_shape=jax.ShapeDtypeStruct((count, cols), jnp.bfloat16),
+        grid=(count // tile,),
+        in_specs=[
+            pl.BlockSpec((tile, width), lambda i: (i, 0)),
+            pl.BlockSpec((width, cols), lambda i: (0, 0)),
+        ],
+        out_specs=pl.BlockSpec((tile, cols), lambda i: (i, 0)),
+        compiler_params=pltpu.CompilerParams(
+            dimension_semantics=("arbitrary",), vmem_limit_bytes=48 * 1024 * 1024
+        ),
+        cost_estimate=pl.CostEstimate(
+            flops=2 * count * width * cols,
+            bytes_accessed=2 * (count * width + width * cols + count * cols),
+            transcendentals=0,
+        ),
+    )(rows, weight)
 
 
 def body(
@@ -200,11 +229,9 @@
     ffn_own = lax.psum_scatter(partial, "req", scatter_dimension=0, tiled=True).astype(jnp.float32)
     layer_output = (residual_mid.astype(jnp.float32) + ffn_own).astype(jnp.bfloat16)
     next_normed = (rms_rows(layer_output.astype(jnp.float32)) * next_gain).astype(jnp.bfloat16)
-    projected_cols = jnp.dot(
-        lax.all_gather(next_normed, "req", axis=0, tiled=True),
-        qkv_weight,
-        preferred_element_type=jnp.float32,
-    ).astype(jnp.bfloat16)
+    projected_cols = project_rows(
+        lax.all_gather(next_normed, "req", axis=0, tiled=True), qkv_weight, 256
+    )
     n_req = lax.axis_size("req")
     col_w = projected_cols.shape[1]
     arrived = lax.all_to_all(

time: 338 us -> 329 us (0.973)
  local copies, waits for them, and re-layouts: 17.8 us -> 8.95 us
  matrix products: 6.78 us -> 0 us
  Pallas kernels: 31.2 us -> 37.7 us
    dot_general x1 -> x0, matrix products: 6.78 us -> none  [body(): jnp.dot(lax.all_gather(next_normed, 'req', axis=0, tiled=True), qkv_weigh...]
    pallas_call x0 -> x1, Pallas kernels: none -> 6.4 us  [project_rows(): pl.pallas_call(project_kernel, out_shape=jax.ShapeDtypeStruct((count, col...]
where the time goes in v11:
time: 329 us; the launch traced here: 328 us
  waiting for transfers between devices  248 us (75%)
  Pallas kernels  37.7 us (11%)
  between operations  15.2 us (5%)
  starting transfers between devices  10.8 us (3%)
  local copies, waits for them, and re-layouts  8.95 us (3%)
  other arithmetic  7.68 us (2%)
    all_gather x1, waiting for transfers between devices, body(): all_kv = lax.all_gather(own_kv, 'tok', axis=0, tiled=True)  111 us
    reduce_scatter x1, waiting for transfers between devices, body(): lax.psum_scatter(partial, 'req', scatter_dimension=0, tiled=True)  37.9 us
    all_gather x1, waiting for transfers between devices, body(): gathered = lax.all_gather(residual_mid, 'req', axis=0, tiled=True)  31.8 us
    all_gather x1, waiting for transfers between devices, body(): lax.all_gather(next_normed, 'req', axis=0, tiled=True)  31.2 us
    all_to_all x1, waiting for transfers between devices, body(): lax.all_to_all(projected_cols.reshape(n_req, row_count, col_w), 'req', 0,...  20.1 us
    pallas_call x1, Pallas kernels, window_attention(): pl.pallas_call(functools.partial(attention_kernel, back, head_w // 2), ou...  16.8 us
    all_to_all x1, waiting for transfers between devices, body(): lax.all_to_all(outgoing, 'tok', split_axis=0, concat_axis=0, tiled=True)  15.5 us
    pallas_call x1, Pallas kernels, ffn_partial(): pl.pallas_call(ffn_kernel, out_shape=jax.ShapeDtypeStruct((count, width),...  14.5 us
  transfers between devices with their start and end apart: 6, of which 6 were waited for; matrix products, arithmetic and copies ran while one was open for 2% of the time, Pallas kernels for 0%

profile of v11, /device:TPU:0, one launch (start us, length us, event | category | flops | bytes accessed | tf_op | source)
XLA Modules:
  0.0 328.1 jit_solution(10938434784330982706)
XLA Ops:
  7.2 2.3 pad_maximum_fusion
  9.6 0.6 multiply_reduce_fusion
  11.6 0.7 dynamic-slice_bitcast_fusion.1
  12.2 0.7 copy.22.qseg_ref
  13.0 0.6 pad_add_fusion.scalars_ref
  13.6 111.1 %all-gather.4.cloned.1.call-done.k_ref.v_ref = bf16[2048,4096]{1,0:T(8,128)(2,1)} async-done(((bf16[128,4096]{1,0:T(8,128)(2,1)}), bf16[2048,4096]{1,0:T(8,128)(2,1)}) %all-gather.4.cloned.1.call-update) | async-done | bytes 16777232 | tf_op jit(solution)/shard_map/all_gather | solution.py:223
  124.7 16.8 %shard_map.166 = bf16[128,2048]{1,0:T(8,128)(2,1)} custom-call(s32[2]{0:T(128)} %pad_add_fusion.scalars_ref, f32[1]{0:T(128)} %bitcast.2.lam_ref, bf16[128,2048]{1,0:T(8,128)(2,1)} %q_ref.1, bf16[2048,4096]{1,0:T(8,128)(2,1)} %all-gather.4.cloned.1.call-done.k_ref.v_ref, bf16[2048,4096]{1,0:T(8,128)(2,1)} %all-gather.4.cloned.1.call-done.k_ref.v_ref, ...), custom_call_target="tpu_custom_call" | custom-call | flops 2885681152 | bytes 26738688 | tf_op jit(solution)/shard_map/pallas_call | solution.py:86
  141.6 31.8 %all-gather.6.cloned.1.call-done.x_ref = bf16[1024,2048]{1,0:T(8,128)(2,1)} async-done(((bf16[128,2048]{1,0:T(8,128)(2,1)}), bf16[1024,2048]{1,0:T(8,128)(2,1)}) %all-gather.6.cloned.1.call-update) | async-done | bytes 4194320 | tf_op jit(solution)/shard_map/all_gather | solution.py:227
  173.4 1.8 copy-done.2
  175.2 14.5 %shard_map.167 = bf16[1024,2048]{1,0:T(8,128)(2,1)} custom-call(bf16[1024,2048]{1,0:T(8,128)(2,1)} %all-gather.6.cloned.1.call-done.x_ref, f32[1,2048]{1,0:T(1,128)S(1)} %bitcast.28, bf16[704,2048]{1,0:T(8,128)(2,1)S(1)} %bitcast.26, bf16[704,2048]{1,0:T(8,128)(2,1)S(1)} %bitcast.27, bf16[704,2048]{1,0:T(8,128)(2,1)} %down_ref.1), custom_call_target="tpu_custom_call" | custom-call | flops 8858370048 | bytes 17039360 | tf_op jit(solution)/shard_map/pallas_call | solution.py:139
  189.8 37.9 %reduce-scatter.2.cloned.1.call-done = bf16[128,2048]{1,0:T(8,128)(2,1)} async-done(((bf16[1024,2048]{1,0:T(8,128)(2,1)}), bf16[128,2048]{1,0:T(8,128)(2,1)}) %reduce-scatter.2.cloned.1.call-update) | async-done | bytes 524304 | tf_op jit(solution)/shard_map/reduce_scatter | solution.py:229
  227.7 1.5 fusion
  229.2 0.8 copy-done.4
  230.0 1.0 fusion.2
  231.0 31.2 %all-gather.8.cloned.1.call-done.x_ref = bf16[1024,2048]{1,0:T(8,128)(2,1)} async-done(((bf16[128,2048]{1,0:T(8,128)(2,1)}), bf16[1024,2048]{1,0:T(8,128)(2,1)}) %all-gather.8.cloned.1.call-update) | async-done | bytes 4194320 | tf_op jit(solution)/shard_map/all_gather | solution.py:233
  262.2 6.4 %shard_map.168 = bf16[1024,768]{1,0:T(8,128)(2,1)} custom-call(bf16[1024,2048]{1,0:T(8,128)(2,1)} %all-gather.8.cloned.1.call-done.x_ref, bf16[2048,768]{1,0:T(8,128)(2,1)S(1)} %copy-done), custom_call_target="tpu_custom_call" | custom-call | flops 3221225472 | bytes 8912896 | tf_op jit(solution)/shard_map/pallas_call | solution.py:171
  268.6 3.7 %all-to-all-start = ((bf16[8,128,768]{2,1,0:T(8,128)(2,1)}), bf16[8,128,768]{2,1,0:T(8,128)(2,1)S(1)}, u32[]{:S(2)}, u32[]{:S(2)}) async-start(bf16[8,128,768]{2,1,0:T(8,128)(2,1)} %bitcast.7), calls=%async_computation.1 | async-start | bytes 3145728 | tf_op jit(solution)/shard_map/all_to_all | solution.py:237
  272.3 0.5 broadcast.75
  272.8 0.7 reduce.8
  273.5 0.1 reshape_squeeze.6
  273.6 0.1 select_reduce_fusion.2
  273.7 20.1 %all-to-all-done = bf16[8,128,768]{2,1,0:T(8,128)(2,1)S(1)} async-done(((bf16[8,128,768]{2,1,0:T(8,128)(2,1)}), bf16[8,128,768]{2,1,0:T(8,128)(2,1)S(1)}, u32[]{:S(2)}, u32[]{:S(2)}) %all-to-all-start) | async-done | bytes 1572896 | tf_op jit(solution)/shard_map/all_to_all | solution.py:237
  293.8 0.2 copy.24
  294.0 0.1 slice_bitcast_fusion
  294.1 1.6 gather_fusion
  295.6 6.9 %all-to-all-start.1 = ((bf16[16,1,8,4096]{3,2,1,0:T(8,128)(2,1)}), bf16[16,1,8,4096]{3,2,1,0:T(8,128)(2,1)S(1)}, u32[]{:S(2)}, u32[]{:S(2)}) async-start(bf16[16,1,8,4096]{3,2,1,0:T(8,128)(2,1)} %bitcast.33), calls=%async_computation.2 | async-start | bytes 2097152 | tf_op jit(solution)/shard_map/all_to_all | solution.py:253
  302.6 0.7 reduce.9
  303.4 0.1 select_reduce_fusion.1
  303.5 0.1 select_reduce_fusion
  303.6 0.8 slice.28
  304.4 15.5 %all-to-all-done.1 = bf16[16,1,8,4096]{3,2,1,0:T(8,128)(2,1)S(1)} async-done(((bf16[16,1,8,4096]{3,2,1,0:T(8,128)(2,1)}), bf16[16,1,8,4096]{3,2,1,0:T(8,128)(2,1)S(1)}, u32[]{:S(2)}, u32[]{:S(2)}) %all-to-all-start.1) | async-done | bytes 1048608 | tf_op jit(solution)/shard_map/all_to_all | solution.py:253
  320.0 1.6 gather_fusion.1
  (31 shorter events, 0.4 us)
Async XLA Ops:
  7.2 2.4 copy-start.6
  7.2 117.5 %all-gather.4.cloned.1.call-start = ((), (), s32[]{:S(2)}) async-start(), calls=%async_computation.3 | async-start | bytes 17825792 | tf_op jit(solution)/shard_map/all_gather | solution.py:223
  9.5 163.9 %all-gather.6.cloned.1.call-start = ((), (), s32[]{:S(2)}) async-start(), calls=%async_computation.4 | async-start | bytes 4718592 | tf_op jit(solution)/shard_map/all_gather | solution.py:227
  124.7 48.7 %copy-start.1 = (bf16[2048,704]{0,1:T(8,128)(2,1)S(1)}, bf16[2048,704]{0,1:T(8,128)(2,1)}, u32[]{:S(2)}) copy-start(bf16[2048,704]{0,1:T(8,128)(2,1)} %param.23) | copy-start | bytes 8650756
  124.7 48.7 %copy-start.3 = (f32[2048]{0:T(1024)S(1)}, f32[2048]{0:T(1024)}, u32[]{:S(2)}) copy-start(f32[2048]{0:T(1024)} %param.22) | copy-start | bytes 24580
  141.5 86.2 %reduce-scatter.2.cloned.1.call-start = ((), (), s32[]{:S(2)}) async-start(), calls=%async_computation.5 | async-start | bytes 4718592 | tf_op jit(solution)/shard_map/reduce_scatter | solution.py:229
  173.4 1.8 copy-start.2
  189.8 40.2 %copy-start.5 = (f32[2048]{0:T(1024)S(1)}, f32[2048]{0:T(1024)}, u32[]{:S(2)}) copy-start(f32[2048]{0:T(1024)} %param.26) | copy-start | bytes 24580
  189.8 72.4 %copy-start = (bf16[2048,768]{1,0:T(8,128)(2,1)S(1)}, bf16[2048,768]{1,0:T(8,128)(2,1)}, u32[]{:S(2)}) copy-start(bf16[2048,768]{1,0:T(8,128)(2,1)} %w_ref.3) | copy-start | bytes 9437188
  189.8 72.4 %all-gather.8.cloned.1.call-start = ((), (), s32[]{:S(2)}) async-start(), calls=%async_computation.6 | async-start | bytes 4718592 | tf_op jit(solution)/shard_map/all_gather | solution.py:233
  229.2 0.8 copy-start.4
  268.6 4.2 %copy-start.7 = (s32[1,256]{1,0:T(1,128)S(1)}, s32[1,256]{1,0:T(1,128)}, u32[]{:S(2)}) copy-start(s32[1,256]{1,0:T(1,128)} %param.28) | copy-start | bytes 3076
  268.6 25.2 %all-to-all-start = ((bf16[8,128,768]{2,1,0:T(8,128)(2,1)}), bf16[8,128,768]{2,1,0:T(8,128)(2,1)S(1)}, u32[]{:S(2)}, u32[]{:S(2)}) async-start(bf16[8,128,768]{2,1,0:T(8,128)(2,1)} %bitcast.7), calls=%async_computation.1 | async-start | bytes 3145728 | tf_op jit(solution)/shard_map/all_to_all | solution.py:237
  293.9 8.6 %copy-start.8 = (s32[1,256]{1,0:T(1,128)S(1)}, s32[1,256]{1,0:T(1,128)}, u32[]{:S(2)}) copy-start(s32[1,256]{1,0:T(1,128)} %param.29) | copy-start | bytes 3076
  295.6 24.3 %all-to-all-start.1 = ((bf16[16,1,8,4096]{3,2,1,0:T(8,128)(2,1)}), bf16[16,1,8,4096]{3,2,1,0:T(8,128)(2,1)S(1)}, u32[]{:S(2)}, u32[]{:S(2)}) async-start(bf16[16,1,8,4096]{3,2,1,0:T(8,128)(2,1)} %bitcast.33), calls=%async_computation.2 | async-start | bytes 2097152 | tf_op jit(solution)/shard_map/all_to_all | solution.py:253
Sparse Core Ops, SparseCore 0:
  10.7 113.9 all-gather.3
  141.6 31.6 all-gather.5
  189.9 37.7 reduce-scatter.1
  231.1 31.0 all-gather.7

commit v12 on v11

--- a/solution.py
+++ b/solution.py
@@ -186,6 +186,31 @@
             transcendentals=0,
         ),
     )(rows, weight)
+
+
+def output_kernel(mid_ref, ffn_ref, gain_ref, out_ref, normed_ref):
+    layer_output = (mid_ref[...].astype(jnp.float32) + ffn_ref[...].astype(jnp.float32)).astype(
+        out_ref.dtype
+    )
+    out_ref[...] = layer_output
+    normed_ref[...] = (rms_rows(layer_output.astype(jnp.float32)) * gain_ref[...]).astype(
+        normed_ref.dtype
+    )
+
+
+def finish_rows(residual_mid, ffn_own, gain):
+    rows, width = residual_mid.shape
+    vmem = pl.BlockSpec(memory_space=pltpu.VMEM)
+    shape = jax.ShapeDtypeStruct((rows, width), jnp.bfloat16)
+    return pl.pallas_call(
+        output_kernel,
+        out_shape=(shape, shape),
+        in_specs=[vmem, vmem, vmem],
+        out_specs=(vmem, vmem),
+        cost_estimate=pl.CostEstimate(
+            flops=6 * rows * width, bytes_accessed=8 * rows * width, transcendentals=rows
+        ),
+    )(residual_mid, ffn_own, gain.reshape(1, width))
 
 
 def body(
@@ -226,9 +251,8 @@
     )
     gathered = lax.all_gather(residual_mid, "req", axis=0, tiled=True)
     partial = ffn_partial(gathered, ffn_gain, gate_weight, up_weight, down_weight, 256)
-    ffn_own = lax.psum_scatter(partial, "req", scatter_dimension=0, tiled=True).astype(jnp.float32)
-    layer_output = (residual_mid.astype(jnp.float32) + ffn_own).astype(jnp.bfloat16)
-    next_normed = (rms_rows(layer_output.astype(jnp.float32)) * next_gain).astype(jnp.bfloat16)
+    ffn_own = lax.psum_scatter(partial, "req", scatter_dimension=0, tiled=True)
+    layer_output, next_normed = finish_rows(residual_mid, ffn_own, next_gain)
     projected_cols = project_rows(
         lax.all_gather(next_normed, "req", axis=0, tiled=True), qkv_weight, 256
     )

time: 329 us -> 328 us (level)
  no operation moved by 1% of the time
where the time goes in v12:
time: 328 us; the launch traced here: 327 us
  waiting for transfers between devices  248 us (76%)
  Pallas kernels  40.1 us (12%)
  between operations  15.2 us (5%)
  starting transfers between devices  10.8 us (3%)
  local copies, waits for them, and re-layouts  8.17 us (2%)
  other arithmetic  5.21 us (2%)
    all_gather x1, waiting for transfers between devices, body(): all_kv = lax.all_gather(own_kv, 'tok', axis=0, tiled=True)  111 us
    reduce_scatter x1, waiting for transfers between devices, body(): ffn_own = lax.psum_scatter(partial, 'req', scatter_dimension=0, tiled=True)  37.9 us
    all_gather x1, waiting for transfers between devices, body(): gathered = lax.all_gather(residual_mid, 'req', axis=0, tiled=True)  31.8 us
    all_gather x1, waiting for transfers between devices, body(): lax.all_gather(next_normed, 'req', axis=0, tiled=True)  31.2 us
    all_to_all x1, waiting for transfers between devices, body(): lax.all_to_all(projected_cols.reshape(n_req, row_count, col_w), 'req', 0,...  20.1 us
    pallas_call x1, Pallas kernels, window_attention(): pl.pallas_call(functools.partial(attention_kernel, back, head_w // 2), ou...  16.8 us
    all_to_all x1, waiting for transfers between devices, body(): lax.all_to_all(outgoing, 'tok', split_axis=0, concat_axis=0, tiled=True)  15.5 us
    pallas_call x1, Pallas kernels, ffn_partial(): pl.pallas_call(ffn_kernel, out_shape=jax.ShapeDtypeStruct((count, width),...  14.5 us
  transfers between devices with their start and end apart: 6, of which 6 were waited for; matrix products, arithmetic and copies ran while one was open for 2% of the time, Pallas kernels for 0%

profile of v12, /device:TPU:0, one launch (start us, length us, event | category | flops | bytes accessed | tf_op | source)
XLA Modules:
  0.0 327.2 jit_solution(11620960808034668306)
XLA Ops:
  7.2 2.3 pad_maximum_fusion
  9.5 0.0 all-gather.6.cloned.1.call-start
  9.6 0.6 multiply_reduce_fusion
  11.6 0.7 dynamic-slice_bitcast_fusion.1
  12.2 0.7 copy.22.qseg_ref
  13.0 0.6 pad_add_fusion.scalars_ref
  13.6 111.1 %all-gather.4.cloned.1.call-done.k_ref.v_ref = bf16[2048,4096]{1,0:T(8,128)(2,1)} async-done(((bf16[128,4096]{1,0:T(8,128)(2,1)}), bf16[2048,4096]{1,0:T(8,128)(2,1)}) %all-gather.4.cloned.1.call-update) | async-done | bytes 16777232 | tf_op jit(solution)/shard_map/all_gather | solution.py:248
  124.7 16.8 %shard_map.166.mid_ref = bf16[128,2048]{1,0:T(8,128)(2,1)} custom-call(s32[2]{0:T(128)} %pad_add_fusion.scalars_ref, f32[1]{0:T(128)} %bitcast.2.lam_ref, bf16[128,2048]{1,0:T(8,128)(2,1)} %q_ref.1, bf16[2048,4096]{1,0:T(8,128)(2,1)} %all-gather.4.cloned.1.call-done.k_ref.v_ref, bf16[2048,4096]{1,0:T(8,128)(2,1)} %all-gather.4.cloned.1.call-done.k_ref.v_ref, ...), custom_call_target="tpu_custom_call" | custom-call | flops 2885681152 | bytes 26738688 | tf_op jit(solution)/shard_map/pallas_call | solution.py:86
  141.6 31.8 %all-gather.6.cloned.1.call-done.x_ref = bf16[1024,2048]{1,0:T(8,128)(2,1)} async-done(((bf16[128,2048]{1,0:T(8,128)(2,1)}), bf16[1024,2048]{1,0:T(8,128)(2,1)}) %all-gather.6.cloned.1.call-update) | async-done | bytes 4194320 | tf_op jit(solution)/shard_map/all_gather | solution.py:252
  173.4 1.8 copy-done.2
  175.2 14.5 %shard_map.167 = bf16[1024,2048]{1,0:T(8,128)(2,1)} custom-call(bf16[1024,2048]{1,0:T(8,128)(2,1)} %all-gather.6.cloned.1.call-done.x_ref, f32[1,2048]{1,0:T(1,128)S(1)} %bitcast.29, bf16[704,2048]{1,0:T(8,128)(2,1)S(1)} %bitcast.27, bf16[704,2048]{1,0:T(8,128)(2,1)S(1)} %bitcast.28, bf16[704,2048]{1,0:T(8,128)(2,1)} %down_ref.1), custom_call_target="tpu_custom_call" | custom-call | flops 8858370048 | bytes 17039360 | tf_op jit(solution)/shard_map/pallas_call | solution.py:139
  189.8 37.9 %reduce-scatter.2.cloned.1.call-done.ffn_ref = bf16[128,2048]{1,0:T(8,128)(2,1)} async-done(((bf16[1024,2048]{1,0:T(8,128)(2,1)}), bf16[128,2048]{1,0:T(8,128)(2,1)}) %reduce-scatter.2.cloned.1.call-update) | async-done | bytes 524304 | tf_op jit(solution)/shard_map/reduce_scatter | solution.py:254
  227.7 2.3 shard_map.168
  230.1 31.2 %all-gather.8.cloned.1.call-done.x_ref = bf16[1024,2048]{1,0:T(8,128)(2,1)} async-done(((bf16[128,2048]{1,0:T(8,128)(2,1)}), bf16[1024,2048]{1,0:T(8,128)(2,1)}) %all-gather.8.cloned.1.call-update) | async-done | bytes 4194320 | tf_op jit(solution)/shard_map/all_gather | solution.py:257
  261.2 6.4 %shard_map.169 = bf16[1024,768]{1,0:T(8,128)(2,1)} custom-call(bf16[1024,2048]{1,0:T(8,128)(2,1)} %all-gather.8.cloned.1.call-done.x_ref, bf16[2048,768]{1,0:T(8,128)(2,1)S(1)} %copy-done), custom_call_target="tpu_custom_call" | custom-call | flops 3221225472 | bytes 8912896 | tf_op jit(solution)/shard_map/pallas_call | solution.py:171
  267.7 3.7 %all-to-all-start = ((bf16[8,128,768]{2,1,0:T(8,128)(2,1)}), bf16[8,128,768]{2,1,0:T(8,128)(2,1)S(1)}, u32[]{:S(2)}, u32[]{:S(2)}) async-start(bf16[8,128,768]{2,1,0:T(8,128)(2,1)} %bitcast.8), calls=%async_computation.1 | async-start | bytes 3145728 | tf_op jit(solution)/shard_map/all_to_all | solution.py:261
  271.4 0.5 broadcast.63
  271.9 0.7 reduce.8
  272.6 0.1 reshape_squeeze.6
  272.6 0.1 select_reduce_fusion.2
  272.8 20.1 %all-to-all-done = bf16[8,128,768]{2,1,0:T(8,128)(2,1)S(1)} async-done(((bf16[8,128,768]{2,1,0:T(8,128)(2,1)}), bf16[8,128,768]{2,1,0:T(8,128)(2,1)S(1)}, u32[]{:S(2)}, u32[]{:S(2)}) %all-to-all-start) | async-done | bytes 1572896 | tf_op jit(solution)/shard_map/all_to_all | solution.py:261
  292.9 0.2 copy.24
  293.0 0.1 slice_bitcast_fusion
  293.1 1.6 gather_fusion
  294.7 6.9 %all-to-all-start.1 = ((bf16[16,1,8,4096]{3,2,1,0:T(8,128)(2,1)}), bf16[16,1,8,4096]{3,2,1,0:T(8,128)(2,1)S(1)}, u32[]{:S(2)}, u32[]{:S(2)}) async-start(bf16[16,1,8,4096]{3,2,1,0:T(8,128)(2,1)} %bitcast.34), calls=%async_computation.2 | async-start | bytes 2097152 | tf_op jit(solution)/shard_map/all_to_all | solution.py:277
  301.7 0.7 reduce.9
  302.4 0.1 reshape_squeeze.7
  302.4 0.1 select_reduce_fusion.1
  302.6 0.1 select_reduce_fusion
  302.7 0.8 slice.28
  303.5 15.5 %all-to-all-done.1 = bf16[16,1,8,4096]{3,2,1,0:T(8,128)(2,1)S(1)} async-done(((bf16[16,1,8,4096]{3,2,1,0:T(8,128)(2,1)}), bf16[16,1,8,4096]{3,2,1,0:T(8,128)(2,1)S(1)}, u32[]{:S(2)}, u32[]{:S(2)}) %all-to-all-start.1) | async-done | bytes 1048608 | tf_op jit(solution)/shard_map/all_to_all | solution.py:277
  319.1 1.6 gather_fusion.1
  (25 shorter events, 0.2 us)
Async XLA Ops:
  7.2 2.4 copy-start.4
  7.2 117.5 %all-gather.4.cloned.1.call-start = ((), (), s32[]{:S(2)}) async-start(), calls=%async_computation.3 | async-start | bytes 17825792 | tf_op jit(solution)/shard_map/all_gather | solution.py:248
  9.5 163.9 %all-gather.6.cloned.1.call-start = ((), (), s32[]{:S(2)}) async-start(), calls=%async_computation.4 | async-start | bytes 4718592 | tf_op jit(solution)/shard_map/all_gather | solution.py:252
  124.7 48.7 %copy-start.1 = (bf16[2048,704]{0,1:T(8,128)(2,1)S(1)}, bf16[2048,704]{0,1:T(8,128)(2,1)}, u32[]{:S(2)}) copy-start(bf16[2048,704]{0,1:T(8,128)(2,1)} %param.23) | copy-start | bytes 8650756
  124.7 48.7 %copy-start.3 = (f32[2048]{0:T(1024)S(1)}, f32[2048]{0:T(1024)}, u32[]{:S(2)}) copy-start(f32[2048]{0:T(1024)} %param.22) | copy-start | bytes 24580
  141.5 86.2 %reduce-scatter.2.cloned.1.call-start = ((), (), s32[]{:S(2)}) async-start(), calls=%async_computation.5 | async-start | bytes 4718592 | tf_op jit(solution)/shard_map/reduce_scatter | solution.py:254
  173.4 1.8 copy-start.2
  189.7 71.5 %copy-start = (bf16[2048,768]{1,0:T(8,128)(2,1)S(1)}, bf16[2048,768]{1,0:T(8,128)(2,1)}, u32[]{:S(2)}) copy-start(bf16[2048,768]{1,0:T(8,128)(2,1)} %w_ref.3) | copy-start | bytes 9437188
  189.8 71.5 %all-gather.8.cloned.1.call-start = ((), (), s32[]{:S(2)}) async-start(), calls=%async_computation.6 | async-start | bytes 4718592 | tf_op jit(solution)/shard_map/all_gather | solution.py:257
  267.6 4.2 %copy-start.5 = (s32[1,256]{1,0:T(1,128)S(1)}, s32[1,256]{1,0:T(1,128)}, u32[]{:S(2)}) copy-start(s32[1,256]{1,0:T(1,128)} %param.28) | copy-start | bytes 3076
  267.7 25.2 %all-to-all-start = ((bf16[8,128,768]{2,1,0:T(8,128)(2,1)}), bf16[8,128,768]{2,1,0:T(8,128)(2,1)S(1)}, u32[]{:S(2)}, u32[]{:S(2)}) async-start(bf16[8,128,768]{2,1,0:T(8,128)(2,1)} %bitcast.8), calls=%async_computation.1 | async-start | bytes 3145728 | tf_op jit(solution)/shard_map/all_to_all | solution.py:261
  293.0 8.6 %copy-start.6 = (s32[1,256]{1,0:T(1,128)S(1)}, s32[1,256]{1,0:T(1,128)}, u32[]{:S(2)}) copy-start(s32[1,256]{1,0:T(1,128)} %param.29) | copy-start | bytes 3076
  294.7 24.3 %all-to-all-start.1 = ((bf16[16,1,8,4096]{3,2,1,0:T(8,128)(2,1)}), bf16[16,1,8,4096]{3,2,1,0:T(8,128)(2,1)S(1)}, u32[]{:S(2)}, u32[]{:S(2)}) async-start(bf16[16,1,8,4096]{3,2,1,0:T(8,128)(2,1)} %bitcast.34), calls=%async_computation.2 | async-start | bytes 2097152 | tf_op jit(solution)/shard_map/all_to_all | solution.py:277
Sparse Core Ops, SparseCore 0:
  10.7 113.9 all-gather.3
  141.6 31.6 all-gather.5
  189.9 37.7 reduce-scatter.1
  230.2 31.0 all-gather.7

commit v13 on v12

--- a/solution.py
+++ b/solution.py
@@ -213,6 +213,24 @@
     )(residual_mid, ffn_own, gain.reshape(1, width))
 
 
+def join_kernel(k_ref, v_ref, out_ref):
+    width = k_ref.shape[1]
+    out_ref[:, :width] = k_ref[...]
+    out_ref[:, width:] = v_ref[...]
+
+
+def join_columns(k_in, v_in):
+    rows, width = k_in.shape
+    vmem = pl.BlockSpec(memory_space=pltpu.VMEM)
+    return pl.pallas_call(
+        join_kernel,
+        out_shape=jax.ShapeDtypeStruct((rows, 2 * width), k_in.dtype),
+        in_specs=[vmem, vmem],
+        out_specs=vmem,
+        cost_estimate=pl.CostEstimate(flops=0, bytes_accessed=8 * rows * width, transcendentals=0),
+    )(k_in, v_in)
+
+
 def body(
     layer_input,
     q_in,
@@ -244,7 +262,7 @@
     query_split = q_in.reshape(row_count, HEADS, 2, head_dim)
     run_max = jnp.full((HEADS, 2, row_count), NEG_FILL, jnp.float32)
     back = -(-(MAX_SEG - 1) // row_count)
-    own_kv = jnp.concatenate([k_in, v_in], axis=1)
+    own_kv = join_columns(k_in, v_in)
     all_kv = lax.all_gather(own_kv, "tok", axis=0, tiled=True)
     residual_mid = window_attention(
         q_in, all_kv, query_segs, seg_row, first_row, lambda_mix, back, out_weight, layer_input

time: 328 us -> 328 us (level)
  no operation moved by 1% of the time
where the time goes in v13:
time: 328 us; the launch traced here: 327 us
  waiting for transfers between devices  248 us (76%)
  Pallas kernels  42.3 us (13%)
  between operations  15.2 us (5%)
  starting transfers between devices  10.8 us (3%)
  local copies, waits for them, and re-layouts  8.17 us (2%)
    all_gather x1, waiting for transfers between devices, body(): all_kv = lax.all_gather(own_kv, 'tok', axis=0, tiled=True)  111 us
    reduce_scatter x1, waiting for transfers between devices, body(): ffn_own = lax.psum_scatter(partial, 'req', scatter_dimension=0, tiled=True)  37.9 us
    all_gather x1, waiting for transfers between devices, body(): gathered = lax.all_gather(residual_mid, 'req', axis=0, tiled=True)  31.8 us
    all_gather x1, waiting for transfers between devices, body(): lax.all_gather(next_normed, 'req', axis=0, tiled=True)  31.2 us
    all_to_all x1, waiting for transfers between devices, body(): lax.all_to_all(projected_cols.reshape(n_req, row_count, col_w), 'req', 0,...  20.1 us
    pallas_call x1, Pallas kernels, window_attention(): pl.pallas_call(functools.partial(attention_kernel, back, head_w // 2), ou...  16.8 us
    all_to_all x1, waiting for transfers between devices, body(): lax.all_to_all(outgoing, 'tok', split_axis=0, concat_axis=0, tiled=True)  15.5 us
    pallas_call x1, Pallas kernels, ffn_partial(): pl.pallas_call(ffn_kernel, out_shape=jax.ShapeDtypeStruct((count, width),...  14.5 us
  transfers between devices with their start and end apart: 6, of which 6 were waited for; matrix products, arithmetic and copies ran while one was open for 2% of the time, Pallas kernels for 0%

profile of v13, /device:TPU:0, one launch (start us, length us, event | category | flops | bytes accessed | tf_op | source)
XLA Modules:
  0.0 327.2 jit_solution(11605700487932672531)
XLA Ops:
  7.2 2.2 shard_map.166
  9.5 0.0 all-gather.6.cloned.1.call-start
  9.6 0.6 multiply_reduce_fusion
  11.6 0.7 dynamic-slice_bitcast_fusion.1
  12.2 0.7 copy.22.qseg_ref
  13.0 0.6 pad_add_fusion.scalars_ref
  13.6 111.1 %all-gather.4.cloned.1.call-done.k_ref.v_ref = bf16[2048,4096]{1,0:T(8,128)(2,1)} async-done(((bf16[128,4096]{1,0:T(8,128)(2,1)}), bf16[2048,4096]{1,0:T(8,128)(2,1)}) %all-gather.4.cloned.1.call-update) | async-done | bytes 16777232 | tf_op jit(solution)/shard_map/all_gather | solution.py:266
  124.7 16.8 %shard_map.167.mid_ref = bf16[128,2048]{1,0:T(8,128)(2,1)} custom-call(s32[2]{0:T(128)} %pad_add_fusion.scalars_ref, f32[1]{0:T(128)} %bitcast.2.lam_ref, bf16[128,2048]{1,0:T(8,128)(2,1)} %q_ref.1, bf16[2048,4096]{1,0:T(8,128)(2,1)} %all-gather.4.cloned.1.call-done.k_ref.v_ref, bf16[2048,4096]{1,0:T(8,128)(2,1)} %all-gather.4.cloned.1.call-done.k_ref.v_ref, ...), custom_call_target="tpu_custom_call" | custom-call | flops 2885681152 | bytes 26738688 | tf_op jit(solution)/shard_map/pallas_call | solution.py:86
  141.6 31.8 %all-gather.6.cloned.1.call-done.x_ref = bf16[1024,2048]{1,0:T(8,128)(2,1)} async-done(((bf16[128,2048]{1,0:T(8,128)(2,1)}), bf16[1024,2048]{1,0:T(8,128)(2,1)}) %all-gather.6.cloned.1.call-update) | async-done | bytes 4194320 | tf_op jit(solution)/shard_map/all_gather | solution.py:270
  173.4 1.8 copy-done.2
  175.2 14.5 %shard_map.168 = bf16[1024,2048]{1,0:T(8,128)(2,1)} custom-call(bf16[1024,2048]{1,0:T(8,128)(2,1)} %all-gather.6.cloned.1.call-done.x_ref, f32[1,2048]{1,0:T(1,128)S(1)} %bitcast.29, bf16[704,2048]{1,0:T(8,128)(2,1)S(1)} %bitcast.27, bf16[704,2048]{1,0:T(8,128)(2,1)S(1)} %bitcast.28, bf16[704,2048]{1,0:T(8,128)(2,1)} %down_ref.1), custom_call_target="tpu_custom_call" | custom-call | flops 8858370048 | bytes 17039360 | tf_op jit(solution)/shard_map/pallas_call | solution.py:139
  189.8 37.9 %reduce-scatter.2.cloned.1.call-done.ffn_ref = bf16[128,2048]{1,0:T(8,128)(2,1)} async-done(((bf16[1024,2048]{1,0:T(8,128)(2,1)}), bf16[128,2048]{1,0:T(8,128)(2,1)}) %reduce-scatter.2.cloned.1.call-update) | async-done | bytes 524304 | tf_op jit(solution)/shard_map/reduce_scatter | solution.py:272
  227.7 2.3 shard_map.169
  230.1 31.2 %all-gather.8.cloned.1.call-done.x_ref = bf16[1024,2048]{1,0:T(8,128)(2,1)} async-done(((bf16[128,2048]{1,0:T(8,128)(2,1)}), bf16[1024,2048]{1,0:T(8,128)(2,1)}) %all-gather.8.cloned.1.call-update) | async-done | bytes 4194320 | tf_op jit(solution)/shard_map/all_gather | solution.py:275
  261.2 6.4 %shard_map.170 = bf16[1024,768]{1,0:T(8,128)(2,1)} custom-call(bf16[1024,2048]{1,0:T(8,128)(2,1)} %all-gather.8.cloned.1.call-done.x_ref, bf16[2048,768]{1,0:T(8,128)(2,1)S(1)} %copy-done), custom_call_target="tpu_custom_call" | custom-call | flops 3221225472 | bytes 8912896 | tf_op jit(solution)/shard_map/pallas_call | solution.py:171
  267.7 3.7 %all-to-all-start = ((bf16[8,128,768]{2,1,0:T(8,128)(2,1)}), bf16[8,128,768]{2,1,0:T(8,128)(2,1)S(1)}, u32[]{:S(2)}, u32[]{:S(2)}) async-start(bf16[8,128,768]{2,1,0:T(8,128)(2,1)} %bitcast.8), calls=%async_computation.1 | async-start | bytes 3145728 | tf_op jit(solution)/shard_map/all_to_all | solution.py:279
  271.4 0.5 broadcast.63
  271.9 0.7 reduce.8
  272.6 0.1 reshape_squeeze.6
  272.6 0.1 select_reduce_fusion.2
  272.8 20.1 %all-to-all-done = bf16[8,128,768]{2,1,0:T(8,128)(2,1)S(1)} async-done(((bf16[8,128,768]{2,1,0:T(8,128)(2,1)}), bf16[8,128,768]{2,1,0:T(8,128)(2,1)S(1)}, u32[]{:S(2)}, u32[]{:S(2)}) %all-to-all-start) | async-done | bytes 1572896 | tf_op jit(solution)/shard_map/all_to_all | solution.py:279
  292.9 0.2 copy.24
  293.0 0.1 slice_bitcast_fusion
  293.1 1.6 gather_fusion
  294.7 6.9 %all-to-all-start.1 = ((bf16[16,1,8,4096]{3,2,1,0:T(8,128)(2,1)}), bf16[16,1,8,4096]{3,2,1,0:T(8,128)(2,1)S(1)}, u32[]{:S(2)}, u32[]{:S(2)}) async-start(bf16[16,1,8,4096]{3,2,1,0:T(8,128)(2,1)} %bitcast.34), calls=%async_computation.2 | async-start | bytes 2097152 | tf_op jit(solution)/shard_map/all_to_all | solution.py:295
  301.7 0.7 reduce.9
  302.4 0.1 reshape_squeeze.7
  302.4 0.1 select_reduce_fusion.1
  302.6 0.1 select_reduce_fusion
  302.7 0.8 slice.28
  303.5 15.5 %all-to-all-done.1 = bf16[16,1,8,4096]{3,2,1,0:T(8,128)(2,1)S(1)} async-done(((bf16[16,1,8,4096]{3,2,1,0:T(8,128)(2,1)}), bf16[16,1,8,4096]{3,2,1,0:T(8,128)(2,1)S(1)}, u32[]{:S(2)}, u32[]{:S(2)}) %all-to-all-start.1) | async-done | bytes 1048608 | tf_op jit(solution)/shard_map/all_to_all | solution.py:295
  319.1 1.6 gather_fusion.1
  (25 shorter events, 0.2 us)
Async XLA Ops:
  7.2 2.4 copy-start.4
  7.2 117.5 %all-gather.4.cloned.1.call-start = ((), (), s32[]{:S(2)}) async-start(), calls=%async_computation.3 | async-start | bytes 17825792 | tf_op jit(solution)/shard_map/all_gather | solution.py:266
  9.5 163.9 %all-gather.6.cloned.1.call-start = ((), (), s32[]{:S(2)}) async-start(), calls=%async_computation.4 | async-start | bytes 4718592 | tf_op jit(solution)/shard_map/all_gather | solution.py:270
  124.7 48.7 %copy-start.1 = (bf16[2048,704]{0,1:T(8,128)(2,1)S(1)}, bf16[2048,704]{0,1:T(8,128)(2,1)}, u32[]{:S(2)}) copy-start(bf16[2048,704]{0,1:T(8,128)(2,1)} %param.23) | copy-start | bytes 8650756
  124.7 48.7 %copy-start.3 = (f32[2048]{0:T(1024)S(1)}, f32[2048]{0:T(1024)}, u32[]{:S(2)}) copy-start(f32[2048]{0:T(1024)} %param.22) | copy-start | bytes 24580
  141.5 86.2 %reduce-scatter.2.cloned.1.call-start = ((), (), s32[]{:S(2)}) async-start(), calls=%async_computation.5 | async-start | bytes 4718592 | tf_op jit(solution)/shard_map/reduce_scatter | solution.py:272
  173.4 1.8 copy-start.2
  189.7 71.5 %copy-start = (bf16[2048,768]{1,0:T(8,128)(2,1)S(1)}, bf16[2048,768]{1,0:T(8,128)(2,1)}, u32[]{:S(2)}) copy-start(bf16[2048,768]{1,0:T(8,128)(2,1)} %w_ref.3) | copy-start | bytes 9437188
  189.8 71.5 %all-gather.8.cloned.1.call-start = ((), (), s32[]{:S(2)}) async-start(), calls=%async_computation.6 | async-start | bytes 4718592 | tf_op jit(solution)/shard_map/all_gather | solution.py:275
  267.6 4.2 %copy-start.5 = (s32[1,256]{1,0:T(1,128)S(1)}, s32[1,256]{1,0:T(1,128)}, u32[]{:S(2)}) copy-start(s32[1,256]{1,0:T(1,128)} %param.28) | copy-start | bytes 3076
  267.7 25.2 %all-to-all-start = ((bf16[8,128,768]{2,1,0:T(8,128)(2,1)}), bf16[8,128,768]{2,1,0:T(8,128)(2,1)S(1)}, u32[]{:S(2)}, u32[]{:S(2)}) async-start(bf16[8,128,768]{2,1,0:T(8,128)(2,1)} %bitcast.8), calls=%async_computation.1 | async-start | bytes 3145728 | tf_op jit(solution)/shard_map/all_to_all | solution.py:279
  293.0 8.6 %copy-start.6 = (s32[1,256]{1,0:T(1,128)S(1)}, s32[1,256]{1,0:T(1,128)}, u32[]{:S(2)}) copy-start(s32[1,256]{1,0:T(1,128)} %param.29) | copy-start | bytes 3076
  294.7 24.3 %all-to-all-start.1 = ((bf16[16,1,8,4096]{3,2,1,0:T(8,128)(2,1)}), bf16[16,1,8,4096]{3,2,1,0:T(8,128)(2,1)S(1)}, u32[]{:S(2)}, u32[]{:S(2)}) async-start(bf16[16,1,8,4096]{3,2,1,0:T(8,128)(2,1)} %bitcast.34), calls=%async_computation.2 | async-start | bytes 2097152 | tf_op jit(solution)/shard_map/all_to_all | solution.py:295
Sparse Core Ops, SparseCore 0:
  10.7 113.9 all-gather.3
  141.6 31.6 all-gather.5
  189.9 37.7 reduce-scatter.1
  230.2 31.0 all-gather.7

commit v14 on v12

--- a/solution.py
+++ b/solution.py
@@ -38,28 +38,34 @@
     key_places = start + lax.broadcasted_iota(jnp.int32, (rows, span), 1)
     key_segs = kseg_ref[:, pl.ds(start, span)]
     visible = (key_segs == qseg_ref[...]) & (key_places <= query_places)
-    values = v_ref[pl.ds(start, span), :]
     score_scale = 1.0 / math.sqrt(head_dim)
-    map_outputs = []
-    for map_index in range(2):
-        query_map = q_ref[:, map_index * head_dim:(map_index + 1) * head_dim]
-        key_map = k_ref[pl.ds(start, span), map_index * head_dim:(map_index + 1) * head_dim]
-        scores = (
-            lax.dot_general(
-                query_map, key_map, (((1,), (1,)), ((), ())), preferred_element_type=jnp.float32
+    head_w = 2 * head_dim
+    head_outs = []
+    for head in range(q_ref.shape[1] // head_w):
+        values = v_ref[pl.ds(start, span), head * head_w:(head + 1) * head_w]
+        map_outputs = []
+        for map_index in range(2):
+            first = head * head_w + map_index * head_dim
+            query_map = q_ref[:, first:first + head_dim]
+            key_map = k_ref[pl.ds(start, span), first:first + head_dim]
+            scores = (
+                lax.dot_general(
+                    query_map, key_map, (((1,), (1,)), ((), ())), preferred_element_type=jnp.float32
+                )
+                * score_scale
             )
-            * score_scale
-        )
-        scores = jnp.where(visible, scores, NEG_FILL)
-        row_max = jnp.max(scores, axis=1, keepdims=True)
-        weights = jnp.where(visible, jnp.exp(scores - row_max), 0.0)
-        totals = jnp.sum(weights, axis=1, keepdims=True)
-        map_out = (
-            jnp.dot(weights.astype(jnp.bfloat16), values, preferred_element_type=jnp.float32) / totals
-        )
-        map_outputs.append(map_out)
-    difference = map_outputs[0] - lam_ref[0] * map_outputs[1]
-    head_out = (rms_rows(difference) * (1.0 - LAMBDA_INIT)).astype(jnp.bfloat16)
+            scores = jnp.where(visible, scores, NEG_FILL)
+            row_max = jnp.max(scores, axis=1, keepdims=True)
+            weights = jnp.exp(scores - row_max)
+            totals = jnp.sum(weights, axis=1, keepdims=True)
+            map_out = (
+                jnp.dot(weights.astype(jnp.bfloat16), values, preferred_element_type=jnp.float32)
+                / totals
+            )
+            map_outputs.append(map_out)
+        difference = map_outputs[0] - lam_ref[0] * map_outputs[1]
+        head_outs.append((rms_rows(difference) * (1.0 - LAMBDA_INIT)).astype(jnp.bfloat16))
+    head_out = jnp.concatenate(head_outs, axis=1)
     step = pl.program_id(0)
 
     @pl.when(step == 0)
@@ -83,19 +89,21 @@
     span = (back + 1) * rows
     flops = HEADS * 2 * (2 * rows * span * (head_w // 2) + 2 * rows * span * head_w) + 2 * rows * width * width
     smem = pl.BlockSpec(memory_space=pltpu.SMEM)
+    steps = HEADS // 2
+    step_w = width // steps
     return pl.pallas_call(
         functools.partial(attention_kernel, back, head_w // 2),
         out_shape=jax.ShapeDtypeStruct((rows, width), jnp.bfloat16),
-        grid=(HEADS,),
+        grid=(steps,),
         in_specs=[
             smem,
             smem,
-            pl.BlockSpec((rows, head_w), lambda h: (0, h)),
-            pl.BlockSpec((keys, head_w), lambda h: (0, h)),
-            pl.BlockSpec((keys, head_w), lambda h: (0, HEADS + h)),
+            pl.BlockSpec((rows, step_w), lambda h: (0, h)),
+            pl.BlockSpec((keys, step_w), lambda h: (0, h)),
+            pl.BlockSpec((keys, step_w), lambda h: (0, steps + h)),
             pl.BlockSpec((rows, 1), lambda h: (0, 0)),
             pl.BlockSpec((1, keys), lambda h: (0, 0)),
-            pl.BlockSpec((head_w, width), lambda h: (h, 0)),
+            pl.BlockSpec((step_w, width), lambda h: (h, 0)),
             pl.BlockSpec((rows, width), lambda h: (0, 0)),
         ],
         out_specs=pl.BlockSpec((rows, width), lambda h: (0, 0)),

time: 328 us -> 325 us (level)
  no operation moved by 1% of the time
where the time goes in v14:
time: 325 us; the launch traced here: 324 us
  waiting for transfers between devices  248 us (76%)
  Pallas kernels  37.3 us (11%)
  between operations  15.2 us (5%)
  starting transfers between devices  10.8 us (3%)
  local copies, waits for them, and re-layouts  8.17 us (3%)
  other arithmetic  5.21 us (2%)
    all_gather x1, waiting for transfers between devices, body(): all_kv = lax.all_gather(own_kv, 'tok', axis=0, tiled=True)  111 us
    reduce_scatter x1, waiting for transfers between devices, body(): ffn_own = lax.psum_scatter(partial, 'req', scatter_dimension=0, tiled=True)  37.9 us
    all_gather x1, waiting for transfers between devices, body(): gathered = lax.all_gather(residual_mid, 'req', axis=0, tiled=True)  31.8 us
    all_gather x1, waiting for transfers between devices, body(): lax.all_gather(next_normed, 'req', axis=0, tiled=True)  31.2 us
    all_to_all x1, waiting for transfers between devices, body(): lax.all_to_all(projected_cols.reshape(n_req, row_count, col_w), 'req', 0,...  20.1 us
    all_to_all x1, waiting for transfers between devices, body(): lax.all_to_all(outgoing, 'tok', split_axis=0, concat_axis=0, tiled=True)  15.5 us
    pallas_call x1, Pallas kernels, ffn_partial(): pl.pallas_call(ffn_kernel, out_shape=jax.ShapeDtypeStruct((count, width),...  14.6 us
    pallas_call x1, Pallas kernels, window_attention(): pl.pallas_call(functools.partial(attention_kernel, back, head_w // 2), ou...  14 us
  transfers between devices with their start and end apart: 6, of which 6 were waited for; matrix products, arithmetic and copies ran while one was open for 2% of the time, Pallas kernels for 0%

profile of v14, /device:TPU:0, one launch (start us, length us, event | category | flops | bytes accessed | tf_op | source)
XLA Modules:
  0.0 324.4 jit_solution(6318435527684632526)
XLA Ops:
  7.2 2.3 pad_maximum_fusion
  9.5 0.0 all-gather.6.cloned.1.call-start
  9.6 0.6 multiply_reduce_fusion
  11.6 0.7 dynamic-slice_bitcast_fusion.1
  12.2 0.7 copy.22.qseg_ref
  13.0 0.6 pad_add_fusion.scalars_ref
  13.6 111.1 %all-gather.4.cloned.1.call-done.k_ref.v_ref = bf16[2048,4096]{1,0:T(8,128)(2,1)} async-done(((bf16[128,4096]{1,0:T(8,128)(2,1)}), bf16[2048,4096]{1,0:T(8,128)(2,1)}) %all-gather.4.cloned.1.call-update) | async-done | bytes 16777232 | tf_op jit(solution)/shard_map/all_gather | solution.py:256
  124.7 14.0 %shard_map.166.mid_ref = bf16[128,2048]{1,0:T(8,128)(2,1)} custom-call(s32[2]{0:T(128)} %pad_add_fusion.scalars_ref, f32[1]{0:T(128)} %bitcast.2.lam_ref, bf16[128,2048]{1,0:T(8,128)(2,1)} %q_ref.1, bf16[2048,4096]{1,0:T(8,128)(2,1)} %all-gather.4.cloned.1.call-done.k_ref.v_ref, bf16[2048,4096]{1,0:T(8,128)(2,1)} %all-gather.4.cloned.1.call-done.k_ref.v_ref, ...), custom_call_target="tpu_custom_call" | custom-call | flops 2885681152 | bytes 26738688 | tf_op jit(solution)/shard_map/pallas_call | solution.py:94
  138.7 31.8 %all-gather.6.cloned.1.call-done.x_ref = bf16[1024,2048]{1,0:T(8,128)(2,1)} async-done(((bf16[128,2048]{1,0:T(8,128)(2,1)}), bf16[1024,2048]{1,0:T(8,128)(2,1)}) %all-gather.6.cloned.1.call-update) | async-done | bytes 4194320 | tf_op jit(solution)/shard_map/all_gather | solution.py:260
  170.6 1.8 copy-done.2
  172.4 14.6 %shard_map.167 = bf16[1024,2048]{1,0:T(8,128)(2,1)} custom-call(bf16[1024,2048]{1,0:T(8,128)(2,1)} %all-gather.6.cloned.1.call-done.x_ref, f32[1,2048]{1,0:T(1,128)S(1)} %bitcast.29, bf16[704,2048]{1,0:T(8,128)(2,1)S(1)} %bitcast.27, bf16[704,2048]{1,0:T(8,128)(2,1)S(1)} %bitcast.28, bf16[704,2048]{1,0:T(8,128)(2,1)} %down_ref.1), custom_call_target="tpu_custom_call" | custom-call | flops 8858370048 | bytes 17039360 | tf_op jit(solution)/shard_map/pallas_call | solution.py:147
  187.0 37.9 %reduce-scatter.2.cloned.1.call-done.ffn_ref = bf16[128,2048]{1,0:T(8,128)(2,1)} async-done(((bf16[1024,2048]{1,0:T(8,128)(2,1)}), bf16[128,2048]{1,0:T(8,128)(2,1)}) %reduce-scatter.2.cloned.1.call-update) | async-done | bytes 524304 | tf_op jit(solution)/shard_map/reduce_scatter | solution.py:262
  224.9 2.3 shard_map.168
  227.2 31.2 %all-gather.8.cloned.1.call-done.x_ref = bf16[1024,2048]{1,0:T(8,128)(2,1)} async-done(((bf16[128,2048]{1,0:T(8,128)(2,1)}), bf16[1024,2048]{1,0:T(8,128)(2,1)}) %all-gather.8.cloned.1.call-update) | async-done | bytes 4194320 | tf_op jit(solution)/shard_map/all_gather | solution.py:265
  258.4 6.4 %shard_map.169 = bf16[1024,768]{1,0:T(8,128)(2,1)} custom-call(bf16[1024,2048]{1,0:T(8,128)(2,1)} %all-gather.8.cloned.1.call-done.x_ref, bf16[2048,768]{1,0:T(8,128)(2,1)S(1)} %copy-done), custom_call_target="tpu_custom_call" | custom-call | flops 3221225472 | bytes 8912896 | tf_op jit(solution)/shard_map/pallas_call | solution.py:179
  264.8 3.7 %all-to-all-start = ((bf16[8,128,768]{2,1,0:T(8,128)(2,1)}), bf16[8,128,768]{2,1,0:T(8,128)(2,1)S(1)}, u32[]{:S(2)}, u32[]{:S(2)}) async-start(bf16[8,128,768]{2,1,0:T(8,128)(2,1)} %bitcast.8), calls=%async_computation.1 | async-start | bytes 3145728 | tf_op jit(solution)/shard_map/all_to_all | solution.py:269
  268.6 0.5 broadcast.63
  269.1 0.7 reduce.8
  269.7 0.1 reshape_squeeze.6
  269.8 0.1 select_reduce_fusion.2
  270.0 20.1 %all-to-all-done = bf16[8,128,768]{2,1,0:T(8,128)(2,1)S(1)} async-done(((bf16[8,128,768]{2,1,0:T(8,128)(2,1)}), bf16[8,128,768]{2,1,0:T(8,128)(2,1)S(1)}, u32[]{:S(2)}, u32[]{:S(2)}) %all-to-all-start) | async-done | bytes 1572896 | tf_op jit(solution)/shard_map/all_to_all | solution.py:269
  290.1 0.2 copy.24
  290.2 0.1 slice_bitcast_fusion
  290.3 1.6 gather_fusion
  291.9 6.9 %all-to-all-start.1 = ((bf16[16,1,8,4096]{3,2,1,0:T(8,128)(2,1)}), bf16[16,1,8,4096]{3,2,1,0:T(8,128)(2,1)S(1)}, u32[]{:S(2)}, u32[]{:S(2)}) async-start(bf16[16,1,8,4096]{3,2,1,0:T(8,128)(2,1)} %bitcast.34), calls=%async_computation.2 | async-start | bytes 2097152 | tf_op jit(solution)/shard_map/all_to_all | solution.py:285
  298.9 0.7 reduce.9
  299.5 0.1 reshape_squeeze.7
  299.6 0.1 select_reduce_fusion.1
  299.7 0.1 select_reduce_fusion
  299.9 0.8 slice.28
  300.7 15.5 %all-to-all-done.1 = bf16[16,1,8,4096]{3,2,1,0:T(8,128)(2,1)S(1)} async-done(((bf16[16,1,8,4096]{3,2,1,0:T(8,128)(2,1)}), bf16[16,1,8,4096]{3,2,1,0:T(8,128)(2,1)S(1)}, u32[]{:S(2)}, u32[]{:S(2)}) %all-to-all-start.1) | async-done | bytes 1048608 | tf_op jit(solution)/shard_map/all_to_all | solution.py:285
  316.3 1.6 gather_fusion.1
  (25 shorter events, 0.2 us)
Async XLA Ops:
  7.2 2.4 copy-start.4
  7.2 117.5 %all-gather.4.cloned.1.call-start = ((), (), s32[]{:S(2)}) async-start(), calls=%async_computation.3 | async-start | bytes 17825792 | tf_op jit(solution)/shard_map/all_gather | solution.py:256
  9.5 161.0 %all-gather.6.cloned.1.call-start = ((), (), s32[]{:S(2)}) async-start(), calls=%async_computation.4 | async-start | bytes 4718592 | tf_op jit(solution)/shard_map/all_gather | solution.py:260
  124.7 45.9 %copy-start.1 = (bf16[2048,704]{0,1:T(8,128)(2,1)S(1)}, bf16[2048,704]{0,1:T(8,128)(2,1)}, u32[]{:S(2)}) copy-start(bf16[2048,704]{0,1:T(8,128)(2,1)} %param.23) | copy-start | bytes 8650756
  124.7 45.9 %copy-start.3 = (f32[2048]{0:T(1024)S(1)}, f32[2048]{0:T(1024)}, u32[]{:S(2)}) copy-start(f32[2048]{0:T(1024)} %param.22) | copy-start | bytes 24580
  138.7 86.2 %reduce-scatter.2.cloned.1.call-start = ((), (), s32[]{:S(2)}) async-start(), calls=%async_computation.5 | async-start | bytes 4718592 | tf_op jit(solution)/shard_map/reduce_scatter | solution.py:262
  170.6 1.8 copy-start.2
  186.9 71.5 %copy-start = (bf16[2048,768]{1,0:T(8,128)(2,1)S(1)}, bf16[2048,768]{1,0:T(8,128)(2,1)}, u32[]{:S(2)}) copy-start(bf16[2048,768]{1,0:T(8,128)(2,1)} %w_ref.3) | copy-start | bytes 9437188
  187.0 71.5 %all-gather.8.cloned.1.call-start = ((), (), s32[]{:S(2)}) async-start(), calls=%async_computation.6 | async-start | bytes 4718592 | tf_op jit(solution)/shard_map/all_gather | solution.py:265
  264.8 4.2 %copy-start.5 = (s32[1,256]{1,0:T(1,128)S(1)}, s32[1,256]{1,0:T(1,128)}, u32[]{:S(2)}) copy-start(s32[1,256]{1,0:T(1,128)} %param.28) | copy-start | bytes 3076
  264.8 25.2 %all-to-all-start = ((bf16[8,128,768]{2,1,0:T(8,128)(2,1)}), bf16[8,128,768]{2,1,0:T(8,128)(2,1)S(1)}, u32[]{:S(2)}, u32[]{:S(2)}) async-start(bf16[8,128,768]{2,1,0:T(8,128)(2,1)} %bitcast.8), calls=%async_computation.1 | async-start | bytes 3145728 | tf_op jit(solution)/shard_map/all_to_all | solution.py:269
  290.2 8.6 %copy-start.6 = (s32[1,256]{1,0:T(1,128)S(1)}, s32[1,256]{1,0:T(1,128)}, u32[]{:S(2)}) copy-start(s32[1,256]{1,0:T(1,128)} %param.29) | copy-start | bytes 3076
  291.9 24.3 %all-to-all-start.1 = ((bf16[16,1,8,4096]{3,2,1,0:T(8,128)(2,1)}), bf16[16,1,8,4096]{3,2,1,0:T(8,128)(2,1)S(1)}, u32[]{:S(2)}, u32[]{:S(2)}) async-start(bf16[16,1,8,4096]{3,2,1,0:T(8,128)(2,1)} %bitcast.34), calls=%async_computation.2 | async-start | bytes 2097152 | tf_op jit(solution)/shard_map/all_to_all | solution.py:285
Sparse Core Ops, SparseCore 0:
  10.7 113.9 all-gather.3
  138.8 31.6 all-gather.5
  187.1 37.7 reduce-scatter.1
  227.4 31.0 all-gather.7

commit v15 on v14

--- a/solution.py
+++ b/solution.py
@@ -89,7 +89,7 @@
     span = (back + 1) * rows
     flops = HEADS * 2 * (2 * rows * span * (head_w // 2) + 2 * rows * span * head_w) + 2 * rows * width * width
     smem = pl.BlockSpec(memory_space=pltpu.SMEM)
-    steps = HEADS // 2
+    steps = HEADS // 4
     step_w = width // steps
     return pl.pallas_call(
         functools.partial(attention_kernel, back, head_w // 2),

time: 325 us -> 325 us (level)
  no operation moved by 1% of the time
where the time goes in v15:
time: 325 us
  waiting for transfers between devices  248 us (76%)
  Pallas kernels  37.6 us (12%)
  between operations  15.2 us (5%)
  starting transfers between devices  10.8 us (3%)
  local copies, waits for them, and re-layouts  8.17 us (3%)
  other arithmetic  5.21 us (2%)
    all_gather x1, waiting for transfers between devices, body(): all_kv = lax.all_gather(own_kv, 'tok', axis=0, tiled=True)  111 us
    reduce_scatter x1, waiting for transfers between devices, body(): ffn_own = lax.psum_scatter(partial, 'req', scatter_dimension=0, tiled=True)  38 us
    all_gather x1, waiting for transfers between devices, body(): gathered = lax.all_gather(residual_mid, 'req', axis=0, tiled=True)  31.8 us
    all_gather x1, waiting for transfers between devices, body(): lax.all_gather(next_normed, 'req', axis=0, tiled=True)  31.1 us
    all_to_all x1, waiting for transfers between devices, body(): lax.all_to_all(projected_cols.reshape(n_req, row_count, col_w), 'req', 0,...  20.1 us
    all_to_all x1, waiting for transfers between devices, body(): lax.all_to_all(outgoing, 'tok', split_axis=0, concat_axis=0, tiled=True)  15.5 us
    pallas_call x1, Pallas kernels, ffn_partial(): pl.pallas_call(ffn_kernel, out_shape=jax.ShapeDtypeStruct((count, width),...  14.5 us
    pallas_call x1, Pallas kernels, window_attention(): pl.pallas_call(functools.partial(attention_kernel, back, head_w // 2), ou...  14.3 us
  transfers between devices with their start and end apart: 6, of which 6 were waited for; matrix products, arithmetic and copies ran while one was open for 2% of the time, Pallas kernels for 0%

profile of v15, /device:TPU:0, one launch (start us, length us, event | category | flops | bytes accessed | tf_op | source)
XLA Modules:
  0.0 324.7 jit_solution(16221457150571650392)
XLA Ops:
  7.2 2.3 pad_maximum_fusion
  9.5 0.0 all-gather.6.cloned.1.call-start
  9.6 0.6 multiply_reduce_fusion
  11.6 0.7 dynamic-slice_bitcast_fusion.1
  12.2 0.7 copy.22.qseg_ref
  13.0 0.6 pad_add_fusion.scalars_ref
  13.6 111.1 %all-gather.4.cloned.1.call-done.k_ref.v_ref = bf16[2048,4096]{1,0:T(8,128)(2,1)} async-done(((bf16[128,4096]{1,0:T(8,128)(2,1)}), bf16[2048,4096]{1,0:T(8,128)(2,1)}) %all-gather.4.cloned.1.call-update) | async-done | bytes 16777232 | tf_op jit(solution)/shard_map/all_gather | solution.py:256
  124.7 14.3 %shard_map.166.mid_ref = bf16[128,2048]{1,0:T(8,128)(2,1)} custom-call(s32[2]{0:T(128)} %pad_add_fusion.scalars_ref, f32[1]{0:T(128)} %bitcast.2.lam_ref, bf16[128,2048]{1,0:T(8,128)(2,1)} %q_ref.1, bf16[2048,4096]{1,0:T(8,128)(2,1)} %all-gather.4.cloned.1.call-done.k_ref.v_ref, bf16[2048,4096]{1,0:T(8,128)(2,1)} %all-gather.4.cloned.1.call-done.k_ref.v_ref, ...), custom_call_target="tpu_custom_call" | custom-call | flops 2885681152 | bytes 26738688 | tf_op jit(solution)/shard_map/pallas_call | solution.py:94
  139.1 31.8 %all-gather.6.cloned.1.call-done.x_ref = bf16[1024,2048]{1,0:T(8,128)(2,1)} async-done(((bf16[128,2048]{1,0:T(8,128)(2,1)}), bf16[1024,2048]{1,0:T(8,128)(2,1)}) %all-gather.6.cloned.1.call-update) | async-done | bytes 4194320 | tf_op jit(solution)/shard_map/all_gather | solution.py:260
  170.9 1.8 copy-done.2
  172.7 14.5 %shard_map.167 = bf16[1024,2048]{1,0:T(8,128)(2,1)} custom-call(bf16[1024,2048]{1,0:T(8,128)(2,1)} %all-gather.6.cloned.1.call-done.x_ref, f32[1,2048]{1,0:T(1,128)S(1)} %bitcast.29, bf16[704,2048]{1,0:T(8,128)(2,1)S(1)} %bitcast.27, bf16[704,2048]{1,0:T(8,128)(2,1)S(1)} %bitcast.28, bf16[704,2048]{1,0:T(8,128)(2,1)} %down_ref.1), custom_call_target="tpu_custom_call" | custom-call | flops 8858370048 | bytes 17039360 | tf_op jit(solution)/shard_map/pallas_call | solution.py:147
  187.3 38.0 %reduce-scatter.2.cloned.1.call-done.ffn_ref = bf16[128,2048]{1,0:T(8,128)(2,1)} async-done(((bf16[1024,2048]{1,0:T(8,128)(2,1)}), bf16[128,2048]{1,0:T(8,128)(2,1)}) %reduce-scatter.2.cloned.1.call-update) | async-done | bytes 524304 | tf_op jit(solution)/shard_map/reduce_scatter | solution.py:262
  225.3 2.3 shard_map.168
  227.6 31.1 %all-gather.8.cloned.1.call-done.x_ref = bf16[1024,2048]{1,0:T(8,128)(2,1)} async-done(((bf16[128,2048]{1,0:T(8,128)(2,1)}), bf16[1024,2048]{1,0:T(8,128)(2,1)}) %all-gather.8.cloned.1.call-update) | async-done | bytes 4194320 | tf_op jit(solution)/shard_map/all_gather | solution.py:265
  258.7 6.4 %shard_map.169 = bf16[1024,768]{1,0:T(8,128)(2,1)} custom-call(bf16[1024,2048]{1,0:T(8,128)(2,1)} %all-gather.8.cloned.1.call-done.x_ref, bf16[2048,768]{1,0:T(8,128)(2,1)S(1)} %copy-done), custom_call_target="tpu_custom_call" | custom-call | flops 3221225472 | bytes 8912896 | tf_op jit(solution)/shard_map/pallas_call | solution.py:179
  265.1 3.7 %all-to-all-start = ((bf16[8,128,768]{2,1,0:T(8,128)(2,1)}), bf16[8,128,768]{2,1,0:T(8,128)(2,1)S(1)}, u32[]{:S(2)}, u32[]{:S(2)}) async-start(bf16[8,128,768]{2,1,0:T(8,128)(2,1)} %bitcast.8), calls=%async_computation.1 | async-start | bytes 3145728 | tf_op jit(solution)/shard_map/all_to_all | solution.py:269
  268.8 0.5 broadcast.63
  269.4 0.7 reduce.8
  270.0 0.1 reshape_squeeze.6
  270.1 0.1 select_reduce_fusion.2
  270.3 20.1 %all-to-all-done = bf16[8,128,768]{2,1,0:T(8,128)(2,1)S(1)} async-done(((bf16[8,128,768]{2,1,0:T(8,128)(2,1)}), bf16[8,128,768]{2,1,0:T(8,128)(2,1)S(1)}, u32[]{:S(2)}, u32[]{:S(2)}) %all-to-all-start) | async-done | bytes 1572896 | tf_op jit(solution)/shard_map/all_to_all | solution.py:269
  290.3 0.2 copy.24
  290.5 0.1 slice_bitcast_fusion
  290.6 1.6 gather_fusion
  292.2 6.9 %all-to-all-start.1 = ((bf16[16,1,8,4096]{3,2,1,0:T(8,128)(2,1)}), bf16[16,1,8,4096]{3,2,1,0:T(8,128)(2,1)S(1)}, u32[]{:S(2)}, u32[]{:S(2)}) async-start(bf16[16,1,8,4096]{3,2,1,0:T(8,128)(2,1)} %bitcast.34), calls=%async_computation.2 | async-start | bytes 2097152 | tf_op jit(solution)/shard_map/all_to_all | solution.py:285
  299.2 0.7 reduce.9
  299.8 0.1 reshape_squeeze.7
  299.9 0.1 select_reduce_fusion.1
  300.0 0.1 select_reduce_fusion
  300.2 0.8 slice.28
  301.0 15.5 %all-to-all-done.1 = bf16[16,1,8,4096]{3,2,1,0:T(8,128)(2,1)S(1)} async-done(((bf16[16,1,8,4096]{3,2,1,0:T(8,128)(2,1)}), bf16[16,1,8,4096]{3,2,1,0:T(8,128)(2,1)S(1)}, u32[]{:S(2)}, u32[]{:S(2)}) %all-to-all-start.1) | async-done | bytes 1048608 | tf_op jit(solution)/shard_map/all_to_all | solution.py:285
  316.5 1.6 gather_fusion.1
  (25 shorter events, 0.2 us)
Async XLA Ops:
  7.2 2.4 copy-start.4
  7.2 117.5 %all-gather.4.cloned.1.call-start = ((), (), s32[]{:S(2)}) async-start(), calls=%async_computation.3 | async-start | bytes 17825792 | tf_op jit(solution)/shard_map/all_gather | solution.py:256
  9.5 161.4 %all-gather.6.cloned.1.call-start = ((), (), s32[]{:S(2)}) async-start(), calls=%async_computation.4 | async-start | bytes 4718592 | tf_op jit(solution)/shard_map/all_gather | solution.py:260
  124.7 46.2 %copy-start.1 = (bf16[2048,704]{0,1:T(8,128)(2,1)S(1)}, bf16[2048,704]{0,1:T(8,128)(2,1)}, u32[]{:S(2)}) copy-start(bf16[2048,704]{0,1:T(8,128)(2,1)} %param.23) | copy-start | bytes 8650756
  124.7 46.2 %copy-start.3 = (f32[2048]{0:T(1024)S(1)}, f32[2048]{0:T(1024)}, u32[]{:S(2)}) copy-start(f32[2048]{0:T(1024)} %param.22) | copy-start | bytes 24580
  139.0 86.3 %reduce-scatter.2.cloned.1.call-start = ((), (), s32[]{:S(2)}) async-start(), calls=%async_computation.5 | async-start | bytes 4718592 | tf_op jit(solution)/shard_map/reduce_scatter | solution.py:262
  170.9 1.8 copy-start.2
  187.2 71.5 %copy-start = (bf16[2048,768]{1,0:T(8,128)(2,1)S(1)}, bf16[2048,768]{1,0:T(8,128)(2,1)}, u32[]{:S(2)}) copy-start(bf16[2048,768]{1,0:T(8,128)(2,1)} %w_ref.3) | copy-start | bytes 9437188
  187.3 71.4 %all-gather.8.cloned.1.call-start = ((), (), s32[]{:S(2)}) async-start(), calls=%async_computation.6 | async-start | bytes 4718592 | tf_op jit(solution)/shard_map/all_gather | solution.py:265
  265.1 4.2 %copy-start.5 = (s32[1,256]{1,0:T(1,128)S(1)}, s32[1,256]{1,0:T(1,128)}, u32[]{:S(2)}) copy-start(s32[1,256]{1,0:T(1,128)} %param.28) | copy-start | bytes 3076
  265.1 25.2 %all-to-all-start = ((bf16[8,128,768]{2,1,0:T(8,128)(2,1)}), bf16[8,128,768]{2,1,0:T(8,128)(2,1)S(1)}, u32[]{:S(2)}, u32[]{:S(2)}) async-start(bf16[8,128,768]{2,1,0:T(8,128)(2,1)} %bitcast.8), calls=%async_computation.1 | async-start | bytes 3145728 | tf_op jit(solution)/shard_map/all_to_all | solution.py:269
  290.5 8.6 %copy-start.6 = (s32[1,256]{1,0:T(1,128)S(1)}, s32[1,256]{1,0:T(1,128)}, u32[]{:S(2)}) copy-start(s32[1,256]{1,0:T(1,128)} %param.29) | copy-start | bytes 3076
  292.2 24.3 %all-to-all-start.1 = ((bf16[16,1,8,4096]{3,2,1,0:T(8,128)(2,1)}), bf16[16,1,8,4096]{3,2,1,0:T(8,128)(2,1)S(1)}, u32[]{:S(2)}, u32[]{:S(2)}) async-start(bf16[16,1,8,4096]{3,2,1,0:T(8,128)(2,1)} %bitcast.34), calls=%async_computation.2 | async-start | bytes 2097152 | tf_op jit(solution)/shard_map/all_to_all | solution.py:285
Sparse Core Ops, SparseCore 0:
  10.7 113.9 all-gather.3
  139.1 31.6 all-gather.5
  187.4 37.8 reduce-scatter.1
  227.8 30.8 all-gather.7

commit v16 on v14

--- a/solution.py
+++ b/solution.py
@@ -127,12 +127,24 @@
     )
 
 
-def ffn_kernel(x_ref, gain_ref, gate_ref, up_ref, down_ref, out_ref):
+def ffn_kernel(x_ref, gain_ref, gate_ref, up_ref, down_hbm, out_ref, down_ref, down_sem):
+    step = pl.program_id(0)
+    fetch = pltpu.make_async_copy(down_hbm, down_ref, down_sem)
+
+    @pl.when(step == 0)
+    def _():
+        fetch.start()
+
     normed = (rms_rows(x_ref[...].astype(jnp.float32)) * gain_ref[...]).astype(jnp.bfloat16)
     contract = (((1,), (1,)), ((), ()))
     gate_proj = lax.dot_general(normed, gate_ref[...], contract, preferred_element_type=jnp.float32)
     up_proj = lax.dot_general(normed, up_ref[...], contract, preferred_element_type=jnp.float32)
     hidden = (gate_proj / (1.0 + jnp.exp(-gate_proj)) * up_proj).astype(jnp.bfloat16)
+
+    @pl.when(step == 0)
+    def _():
+        fetch.wait()
+
     out_ref[...] = jnp.dot(hidden, down_ref[...], preferred_element_type=jnp.float32).astype(
         out_ref.dtype
     )
@@ -153,9 +165,13 @@
             pl.BlockSpec((1, width), full),
             pl.BlockSpec((hidden_w, width), full),
             pl.BlockSpec((hidden_w, width), full),
-            pl.BlockSpec((hidden_w, width), full),
+            pl.BlockSpec(memory_space=pl.ANY),
         ],
         out_specs=pl.BlockSpec((tile, width), lambda i: (i, 0)),
+        scratch_shapes=[
+            pltpu.VMEM((hidden_w, width), down_weight.dtype),
+            pltpu.SemaphoreType.DMA(()),
+        ],
         compiler_params=pltpu.CompilerParams(
             dimension_semantics=("arbitrary",), vmem_limit_bytes=48 * 1024 * 1024
         ),

time: 325 us -> 325 us (level)
  no operation moved by 1% of the time
where the time goes in v16:
time: 325 us; the launch traced here: 324 us
  waiting for transfers between devices  248 us (76%)
  Pallas kernels  37 us (11%)
  between operations  15.3 us (5%)
  starting transfers between devices  10.8 us (3%)
  local copies, waits for them, and re-layouts  8.17 us (3%)
  other arithmetic  5.21 us (2%)
    all_gather x1, waiting for transfers between devices, body(): all_kv = lax.all_gather(own_kv, 'tok', axis=0, tiled=True)  111 us
    reduce_scatter x1, waiting for transfers between devices, body(): ffn_own = lax.psum_scatter(partial, 'req', scatter_dimension=0, tiled=True)  37.9 us
    all_gather x1, waiting for transfers between devices, body(): gathered = lax.all_gather(residual_mid, 'req', axis=0, tiled=True)  31.8 us
    all_gather x1, waiting for transfers between devices, body(): lax.all_gather(next_normed, 'req', axis=0, tiled=True)  31.3 us
    all_to_all x1, waiting for transfers between devices, body(): lax.all_to_all(projected_cols.reshape(n_req, row_count, col_w), 'req', 0,...  20.1 us
    all_to_all x1, waiting for transfers between devices, body(): lax.all_to_all(outgoing, 'tok', split_axis=0, concat_axis=0, tiled=True)  15.5 us
    pallas_call x1, Pallas kernels, ffn_partial(): pl.pallas_call(ffn_kernel, out_shape=jax.ShapeDtypeStruct((count, width),...  14.3 us
    pallas_call x1, Pallas kernels, window_attention(): pl.pallas_call(functools.partial(attention_kernel, back, head_w // 2), ou...  14 us
  transfers between devices with their start and end apart: 6, of which 6 were waited for; matrix products, arithmetic and copies ran while one was open for 2% of the time, Pallas kernels for 0%

profile of v16, /device:TPU:0, one launch (start us, length us, event | category | flops | bytes accessed | tf_op | source)
XLA Modules:
  0.0 324.3 jit_solution(14718054632717326355)
XLA Ops:
  7.2 2.3 pad_maximum_fusion
  9.5 0.0 all-gather.6.cloned.1.call-start
  9.6 0.6 multiply_reduce_fusion
  11.6 0.7 dynamic-slice_bitcast_fusion.1
  12.2 0.7 copy.22.qseg_ref
  13.0 0.6 pad_add_fusion.scalars_ref
  13.6 111.1 %all-gather.4.cloned.1.call-done.k_ref.v_ref = bf16[2048,4096]{1,0:T(8,128)(2,1)} async-done(((bf16[128,4096]{1,0:T(8,128)(2,1)}), bf16[2048,4096]{1,0:T(8,128)(2,1)}) %all-gather.4.cloned.1.call-update) | async-done | bytes 16777232 | tf_op jit(solution)/shard_map/all_gather | solution.py:272
  124.7 14.0 %shard_map.166.mid_ref = bf16[128,2048]{1,0:T(8,128)(2,1)} custom-call(s32[2]{0:T(128)} %pad_add_fusion.scalars_ref, f32[1]{0:T(128)} %bitcast.2.lam_ref, bf16[128,2048]{1,0:T(8,128)(2,1)} %q_ref.1, bf16[2048,4096]{1,0:T(8,128)(2,1)} %all-gather.4.cloned.1.call-done.k_ref.v_ref, bf16[2048,4096]{1,0:T(8,128)(2,1)} %all-gather.4.cloned.1.call-done.k_ref.v_ref, ...), custom_call_target="tpu_custom_call" | custom-call | flops 2885681152 | bytes 26738688 | tf_op jit(solution)/shard_map/pallas_call | solution.py:94
  138.7 31.8 %all-gather.6.cloned.1.call-done.x_ref = bf16[1024,2048]{1,0:T(8,128)(2,1)} async-done(((bf16[128,2048]{1,0:T(8,128)(2,1)}), bf16[1024,2048]{1,0:T(8,128)(2,1)}) %all-gather.6.cloned.1.call-update) | async-done | bytes 4194320 | tf_op jit(solution)/shard_map/all_gather | solution.py:276
  170.6 1.8 copy-done.2
  172.4 14.3 %shard_map.167 = bf16[1024,2048]{1,0:T(8,128)(2,1)} custom-call(bf16[1024,2048]{1,0:T(8,128)(2,1)} %all-gather.6.cloned.1.call-done.x_ref, f32[1,2048]{1,0:T(1,128)S(1)} %bitcast.29, bf16[704,2048]{1,0:T(8,128)(2,1)S(1)} %bitcast.27, bf16[704,2048]{1,0:T(8,128)(2,1)S(1)} %bitcast.28, bf16[704,2048]{1,0:T(8,128)(2,1)} %down_hbm.1), custom_call_target="tpu_custom_call" | custom-call | flops 8858370048 | bytes 17039360 | tf_op jit(solution)/shard_map/pallas_call | solution.py:159
  186.8 37.9 %reduce-scatter.2.cloned.1.call-done.ffn_ref = bf16[128,2048]{1,0:T(8,128)(2,1)} async-done(((bf16[1024,2048]{1,0:T(8,128)(2,1)}), bf16[128,2048]{1,0:T(8,128)(2,1)}) %reduce-scatter.2.cloned.1.call-update) | async-done | bytes 524304 | tf_op jit(solution)/shard_map/reduce_scatter | solution.py:278
  224.7 2.3 shard_map.168
  227.0 31.3 %all-gather.8.cloned.1.call-done.x_ref = bf16[1024,2048]{1,0:T(8,128)(2,1)} async-done(((bf16[128,2048]{1,0:T(8,128)(2,1)}), bf16[1024,2048]{1,0:T(8,128)(2,1)}) %all-gather.8.cloned.1.call-update) | async-done | bytes 4194320 | tf_op jit(solution)/shard_map/all_gather | solution.py:281
  258.3 6.4 %shard_map.169 = bf16[1024,768]{1,0:T(8,128)(2,1)} custom-call(bf16[1024,2048]{1,0:T(8,128)(2,1)} %all-gather.8.cloned.1.call-done.x_ref, bf16[2048,768]{1,0:T(8,128)(2,1)S(1)} %copy-done), custom_call_target="tpu_custom_call" | custom-call | flops 3221225472 | bytes 8912896 | tf_op jit(solution)/shard_map/pallas_call | solution.py:195
  264.7 3.7 %all-to-all-start = ((bf16[8,128,768]{2,1,0:T(8,128)(2,1)}), bf16[8,128,768]{2,1,0:T(8,128)(2,1)S(1)}, u32[]{:S(2)}, u32[]{:S(2)}) async-start(bf16[8,128,768]{2,1,0:T(8,128)(2,1)} %bitcast.8), calls=%async_computation.1 | async-start | bytes 3145728 | tf_op jit(solution)/shard_map/all_to_all | solution.py:285
  268.5 0.5 broadcast.63
  269.0 0.7 reduce.8
  269.6 0.1 reshape_squeeze.6
  269.7 0.1 select_reduce_fusion.2
  269.9 20.1 %all-to-all-done = bf16[8,128,768]{2,1,0:T(8,128)(2,1)S(1)} async-done(((bf16[8,128,768]{2,1,0:T(8,128)(2,1)}), bf16[8,128,768]{2,1,0:T(8,128)(2,1)S(1)}, u32[]{:S(2)}, u32[]{:S(2)}) %all-to-all-start) | async-done | bytes 1572896 | tf_op jit(solution)/shard_map/all_to_all | solution.py:285
  290.0 0.2 copy.24
  290.1 0.1 slice_bitcast_fusion
  290.2 1.6 gather_fusion
  291.8 6.9 %all-to-all-start.1 = ((bf16[16,1,8,4096]{3,2,1,0:T(8,128)(2,1)}), bf16[16,1,8,4096]{3,2,1,0:T(8,128)(2,1)S(1)}, u32[]{:S(2)}, u32[]{:S(2)}) async-start(bf16[16,1,8,4096]{3,2,1,0:T(8,128)(2,1)} %bitcast.34), calls=%async_computation.2 | async-start | bytes 2097152 | tf_op jit(solution)/shard_map/all_to_all | solution.py:301
  298.8 0.7 reduce.9
  299.5 0.1 reshape_squeeze.7
  299.5 0.1 select_reduce_fusion.1
  299.6 0.1 select_reduce_fusion
  299.8 0.8 slice.28
  300.6 15.5 %all-to-all-done.1 = bf16[16,1,8,4096]{3,2,1,0:T(8,128)(2,1)S(1)} async-done(((bf16[16,1,8,4096]{3,2,1,0:T(8,128)(2,1)}), bf16[16,1,8,4096]{3,2,1,0:T(8,128)(2,1)S(1)}, u32[]{:S(2)}, u32[]{:S(2)}) %all-to-all-start.1) | async-done | bytes 1048608 | tf_op jit(solution)/shard_map/all_to_all | solution.py:301
  316.2 1.6 gather_fusion.1
  (25 shorter events, 0.2 us)
Async XLA Ops:
  7.2 2.4 copy-start.4
  7.2 117.5 %all-gather.4.cloned.1.call-start = ((), (), s32[]{:S(2)}) async-start(), calls=%async_computation.3 | async-start | bytes 17825792 | tf_op jit(solution)/shard_map/all_gather | solution.py:272
  9.5 161.0 %all-gather.6.cloned.1.call-start = ((), (), s32[]{:S(2)}) async-start(), calls=%async_computation.4 | async-start | bytes 4718592 | tf_op jit(solution)/shard_map/all_gather | solution.py:276
  124.7 45.9 %copy-start.1 = (bf16[2048,704]{0,1:T(8,128)(2,1)S(1)}, bf16[2048,704]{0,1:T(8,128)(2,1)}, u32[]{:S(2)}) copy-start(bf16[2048,704]{0,1:T(8,128)(2,1)} %param.23) | copy-start | bytes 8650756
  124.7 45.9 %copy-start.3 = (f32[2048]{0:T(1024)S(1)}, f32[2048]{0:T(1024)}, u32[]{:S(2)}) copy-start(f32[2048]{0:T(1024)} %param.22) | copy-start | bytes 24580
  138.7 86.0 %reduce-scatter.2.cloned.1.call-start = ((), (), s32[]{:S(2)}) async-start(), calls=%async_computation.5 | async-start | bytes 4718592 | tf_op jit(solution)/shard_map/reduce_scatter | solution.py:278
  170.6 1.8 copy-start.2
  186.7 71.6 %copy-start = (bf16[2048,768]{1,0:T(8,128)(2,1)S(1)}, bf16[2048,768]{1,0:T(8,128)(2,1)}, u32[]{:S(2)}) copy-start(bf16[2048,768]{1,0:T(8,128)(2,1)} %w_ref.3) | copy-start | bytes 9437188
  186.7 71.6 %all-gather.8.cloned.1.call-start = ((), (), s32[]{:S(2)}) async-start(), calls=%async_computation.6 | async-start | bytes 4718592 | tf_op jit(solution)/shard_map/all_gather | solution.py:281
  264.7 4.2 %copy-start.5 = (s32[1,256]{1,0:T(1,128)S(1)}, s32[1,256]{1,0:T(1,128)}, u32[]{:S(2)}) copy-start(s32[1,256]{1,0:T(1,128)} %param.28) | copy-start | bytes 3076
  264.7 25.2 %all-to-all-start = ((bf16[8,128,768]{2,1,0:T(8,128)(2,1)}), bf16[8,128,768]{2,1,0:T(8,128)(2,1)S(1)}, u32[]{:S(2)}, u32[]{:S(2)}) async-start(bf16[8,128,768]{2,1,0:T(8,128)(2,1)} %bitcast.8), calls=%async_computation.1 | async-start | bytes 3145728 | tf_op jit(solution)/shard_map/all_to_all | solution.py:285
  290.1 8.6 %copy-start.6 = (s32[1,256]{1,0:T(1,128)S(1)}, s32[1,256]{1,0:T(1,128)}, u32[]{:S(2)}) copy-start(s32[1,256]{1,0:T(1,128)} %param.29) | copy-start | bytes 3076
  291.8 24.3 %all-to-all-start.1 = ((bf16[16,1,8,4096]{3,2,1,0:T(8,128)(2,1)}), bf16[16,1,8,4096]{3,2,1,0:T(8,128)(2,1)S(1)}, u32[]{:S(2)}, u32[]{:S(2)}) async-start(bf16[16,1,8,4096]{3,2,1,0:T(8,128)(2,1)} %bitcast.34), calls=%async_computation.2 | async-start | bytes 2097152 | tf_op jit(solution)/shard_map/all_to_all | solution.py:301
Sparse Core Ops, SparseCore 0:
  10.7 113.9 all-gather.3
  138.8 31.6 all-gather.5
  186.9 37.7 reduce-scatter.1
  227.2 31.1 all-gather.7

commit v17 on v16

--- a/solution.py
+++ b/solution.py
@@ -274,7 +274,7 @@
         q_in, all_kv, query_segs, seg_row, first_row, lambda_mix, back, out_weight, layer_input
     )
     gathered = lax.all_gather(residual_mid, "req", axis=0, tiled=True)
-    partial = ffn_partial(gathered, ffn_gain, gate_weight, up_weight, down_weight, 256)
+    partial = ffn_partial(gathered, ffn_gain, gate_weight, up_weight, down_weight, 512)
     ffn_own = lax.psum_scatter(partial, "req", scatter_dimension=0, tiled=True)
     layer_output, next_normed = finish_rows(residual_mid, ffn_own, next_gain)
     projected_cols = project_rows(

time: 325 us -> 325 us (level)
  no operation moved by 1% of the time
where the time goes in v17:
time: 325 us; the launch traced here: 324 us
  waiting for transfers between devices  248 us (76%)
  Pallas kernels  36.9 us (11%)
  between operations  15.3 us (5%)
  starting transfers between devices  10.8 us (3%)
  local copies, waits for them, and re-layouts  8.17 us (3%)
  other arithmetic  5.21 us (2%)
    all_gather x1, waiting for transfers between devices, body(): all_kv = lax.all_gather(own_kv, 'tok', axis=0, tiled=True)  111 us
    reduce_scatter x1, waiting for transfers between devices, body(): ffn_own = lax.psum_scatter(partial, 'req', scatter_dimension=0, tiled=True)  38 us
    all_gather x1, waiting for transfers between devices, body(): gathered = lax.all_gather(residual_mid, 'req', axis=0, tiled=True)  31.8 us
    all_gather x1, waiting for transfers between devices, body(): lax.all_gather(next_normed, 'req', axis=0, tiled=True)  31 us
    all_to_all x1, waiting for transfers between devices, body(): lax.all_to_all(projected_cols.reshape(n_req, row_count, col_w), 'req', 0,...  20.1 us
    all_to_all x1, waiting for transfers between devices, body(): lax.all_to_all(outgoing, 'tok', split_axis=0, concat_axis=0, tiled=True)  15.5 us
    pallas_call x1, Pallas kernels, ffn_partial(): pl.pallas_call(ffn_kernel, out_shape=jax.ShapeDtypeStruct((count, width),...  14.2 us
    pallas_call x1, Pallas kernels, window_attention(): pl.pallas_call(functools.partial(attention_kernel, back, head_w // 2), ou...  14 us
  transfers between devices with their start and end apart: 6, of which 6 were waited for; matrix products, arithmetic and copies ran while one was open for 2% of the time, Pallas kernels for 0%

profile of v17, /device:TPU:0, one launch (start us, length us, event | category | flops | bytes accessed | tf_op | source)
XLA Modules:
  0.0 324.0 jit_solution(2250604420824604383)
XLA Ops:
  7.2 2.3 pad_maximum_fusion
  9.6 0.6 multiply_reduce_fusion
  11.6 0.7 dynamic-slice_bitcast_fusion.1
  12.2 0.7 copy.22.qseg_ref
  13.0 0.6 pad_add_fusion.scalars_ref
  13.6 111.1 %all-gather.4.cloned.1.call-done.k_ref.v_ref = bf16[2048,4096]{1,0:T(8,128)(2,1)} async-done(((bf16[128,4096]{1,0:T(8,128)(2,1)}), bf16[2048,4096]{1,0:T(8,128)(2,1)}) %all-gather.4.cloned.1.call-update) | async-done | bytes 16777232 | tf_op jit(solution)/shard_map/all_gather | solution.py:272
  124.7 14.0 %shard_map.166.mid_ref = bf16[128,2048]{1,0:T(8,128)(2,1)} custom-call(s32[2]{0:T(128)} %pad_add_fusion.scalars_ref, f32[1]{0:T(128)} %bitcast.2.lam_ref, bf16[128,2048]{1,0:T(8,128)(2,1)} %q_ref.1, bf16[2048,4096]{1,0:T(8,128)(2,1)} %all-gather.4.cloned.1.call-done.k_ref.v_ref, bf16[2048,4096]{1,0:T(8,128)(2,1)} %all-gather.4.cloned.1.call-done.k_ref.v_ref, ...), custom_call_target="tpu_custom_call" | custom-call | flops 2885681152 | bytes 26738688 | tf_op jit(solution)/shard_map/pallas_call | solution.py:94
  138.7 31.8 %all-gather.6.cloned.1.call-done.x_ref = bf16[1024,2048]{1,0:T(8,128)(2,1)} async-done(((bf16[128,2048]{1,0:T(8,128)(2,1)}), bf16[1024,2048]{1,0:T(8,128)(2,1)}) %all-gather.6.cloned.1.call-update) | async-done | bytes 4194320 | tf_op jit(solution)/shard_map/all_gather | solution.py:276
  170.6 1.8 copy-done.2
  172.4 14.2 %shard_map.167 = bf16[1024,2048]{1,0:T(8,128)(2,1)} custom-call(bf16[1024,2048]{1,0:T(8,128)(2,1)} %all-gather.6.cloned.1.call-done.x_ref, f32[1,2048]{1,0:T(1,128)S(1)} %bitcast.29, bf16[704,2048]{1,0:T(8,128)(2,1)S(1)} %bitcast.27, bf16[704,2048]{1,0:T(8,128)(2,1)S(1)} %bitcast.28, bf16[704,2048]{1,0:T(8,128)(2,1)} %down_hbm.1), custom_call_target="tpu_custom_call" | custom-call | flops 8858370048 | bytes 17039360 | tf_op jit(solution)/shard_map/pallas_call | solution.py:159
  186.6 0.0 all-gather.8.cloned.1.call-start
  186.7 38.0 %reduce-scatter.2.cloned.1.call-done.ffn_ref = bf16[128,2048]{1,0:T(8,128)(2,1)} async-done(((bf16[1024,2048]{1,0:T(8,128)(2,1)}), bf16[128,2048]{1,0:T(8,128)(2,1)}) %reduce-scatter.2.cloned.1.call-update) | async-done | bytes 524304 | tf_op jit(solution)/shard_map/reduce_scatter | solution.py:278
  224.7 2.3 shard_map.168
  227.1 31.0 %all-gather.8.cloned.1.call-done.x_ref = bf16[1024,2048]{1,0:T(8,128)(2,1)} async-done(((bf16[128,2048]{1,0:T(8,128)(2,1)}), bf16[1024,2048]{1,0:T(8,128)(2,1)}) %all-gather.8.cloned.1.call-update) | async-done | bytes 4194320 | tf_op jit(solution)/shard_map/all_gather | solution.py:281
  258.1 6.4 %shard_map.169 = bf16[1024,768]{1,0:T(8,128)(2,1)} custom-call(bf16[1024,2048]{1,0:T(8,128)(2,1)} %all-gather.8.cloned.1.call-done.x_ref, bf16[2048,768]{1,0:T(8,128)(2,1)S(1)} %copy-done), custom_call_target="tpu_custom_call" | custom-call | flops 3221225472 | bytes 8912896 | tf_op jit(solution)/shard_map/pallas_call | solution.py:195
  264.5 3.7 %all-to-all-start = ((bf16[8,128,768]{2,1,0:T(8,128)(2,1)}), bf16[8,128,768]{2,1,0:T(8,128)(2,1)S(1)}, u32[]{:S(2)}, u32[]{:S(2)}) async-start(bf16[8,128,768]{2,1,0:T(8,128)(2,1)} %bitcast.8), calls=%async_computation.1 | async-start | bytes 3145728 | tf_op jit(solution)/shard_map/all_to_all | solution.py:285
  268.2 0.5 broadcast.63
  268.7 0.7 reduce.8
  269.4 0.1 reshape_squeeze.6
  269.5 0.1 select_reduce_fusion.2
  269.6 20.1 %all-to-all-done = bf16[8,128,768]{2,1,0:T(8,128)(2,1)S(1)} async-done(((bf16[8,128,768]{2,1,0:T(8,128)(2,1)}), bf16[8,128,768]{2,1,0:T(8,128)(2,1)S(1)}, u32[]{:S(2)}, u32[]{:S(2)}) %all-to-all-start) | async-done | bytes 1572896 | tf_op jit(solution)/shard_map/all_to_all | solution.py:285
  289.7 0.2 copy.24
  289.9 0.1 slice_bitcast_fusion
  290.0 1.6 gather_fusion
  291.6 6.9 %all-to-all-start.1 = ((bf16[16,1,8,4096]{3,2,1,0:T(8,128)(2,1)}), bf16[16,1,8,4096]{3,2,1,0:T(8,128)(2,1)S(1)}, u32[]{:S(2)}, u32[]{:S(2)}) async-start(bf16[16,1,8,4096]{3,2,1,0:T(8,128)(2,1)} %bitcast.34), calls=%async_computation.2 | async-start | bytes 2097152 | tf_op jit(solution)/shard_map/all_to_all | solution.py:301
  298.5 0.7 reduce.9
  299.2 0.1 reshape_squeeze.7
  299.3 0.1 select_reduce_fusion.1
  299.4 0.1 select_reduce_fusion
  299.6 0.8 slice.28
  300.4 15.5 %all-to-all-done.1 = bf16[16,1,8,4096]{3,2,1,0:T(8,128)(2,1)S(1)} async-done(((bf16[16,1,8,4096]{3,2,1,0:T(8,128)(2,1)}), bf16[16,1,8,4096]{3,2,1,0:T(8,128)(2,1)S(1)}, u32[]{:S(2)}, u32[]{:S(2)}) %all-to-all-start.1) | async-done | bytes 1048608 | tf_op jit(solution)/shard_map/all_to_all | solution.py:301
  315.9 1.6 gather_fusion.1
  (25 shorter events, 0.2 us)
Async XLA Ops:
  7.2 2.4 copy-start.4
  7.2 117.5 %all-gather.4.cloned.1.call-start = ((), (), s32[]{:S(2)}) async-start(), calls=%async_computation.3 | async-start | bytes 17825792 | tf_op jit(solution)/shard_map/all_gather | solution.py:272
  9.5 161.0 %all-gather.6.cloned.1.call-start = ((), (), s32[]{:S(2)}) async-start(), calls=%async_computation.4 | async-start | bytes 4718592 | tf_op jit(solution)/shard_map/all_gather | solution.py:276
  124.7 45.9 %copy-start.1 = (bf16[2048,704]{0,1:T(8,128)(2,1)S(1)}, bf16[2048,704]{0,1:T(8,128)(2,1)}, u32[]{:S(2)}) copy-start(bf16[2048,704]{0,1:T(8,128)(2,1)} %param.23) | copy-start | bytes 8650756
  124.7 45.9 %copy-start.3 = (f32[2048]{0:T(1024)S(1)}, f32[2048]{0:T(1024)}, u32[]{:S(2)}) copy-start(f32[2048]{0:T(1024)} %param.22) | copy-start | bytes 24580
  138.7 86.0 %reduce-scatter.2.cloned.1.call-start = ((), (), s32[]{:S(2)}) async-start(), calls=%async_computation.5 | async-start | bytes 4718592 | tf_op jit(solution)/shard_map/reduce_scatter | solution.py:278
  170.6 1.8 copy-start.2
  186.6 71.5 %copy-start = (bf16[2048,768]{1,0:T(8,128)(2,1)S(1)}, bf16[2048,768]{1,0:T(8,128)(2,1)}, u32[]{:S(2)}) copy-start(bf16[2048,768]{1,0:T(8,128)(2,1)} %w_ref.3) | copy-start | bytes 9437188
  186.6 71.5 %all-gather.8.cloned.1.call-start = ((), (), s32[]{:S(2)}) async-start(), calls=%async_computation.6 | async-start | bytes 4718592 | tf_op jit(solution)/shard_map/all_gather | solution.py:281
  264.5 4.2 %copy-start.5 = (s32[1,256]{1,0:T(1,128)S(1)}, s32[1,256]{1,0:T(1,128)}, u32[]{:S(2)}) copy-start(s32[1,256]{1,0:T(1,128)} %param.28) | copy-start | bytes 3076
  264.5 25.2 %all-to-all-start = ((bf16[8,128,768]{2,1,0:T(8,128)(2,1)}), bf16[8,128,768]{2,1,0:T(8,128)(2,1)S(1)}, u32[]{:S(2)}, u32[]{:S(2)}) async-start(bf16[8,128,768]{2,1,0:T(8,128)(2,1)} %bitcast.8), calls=%async_computation.1 | async-start | bytes 3145728 | tf_op jit(solution)/shard_map/all_to_all | solution.py:285
  289.9 8.6 %copy-start.6 = (s32[1,256]{1,0:T(1,128)S(1)}, s32[1,256]{1,0:T(1,128)}, u32[]{:S(2)}) copy-start(s32[1,256]{1,0:T(1,128)} %param.29) | copy-start | bytes 3076
  291.6 24.3 %all-to-all-start.1 = ((bf16[16,1,8,4096]{3,2,1,0:T(8,128)(2,1)}), bf16[16,1,8,4096]{3,2,1,0:T(8,128)(2,1)S(1)}, u32[]{:S(2)}, u32[]{:S(2)}) async-start(bf16[16,1,8,4096]{3,2,1,0:T(8,128)(2,1)} %bitcast.34), calls=%async_computation.2 | async-start | bytes 2097152 | tf_op jit(solution)/shard_map/all_to_all | solution.py:301
Sparse Core Ops, SparseCore 0:
  10.7 113.9 all-gather.3
  138.8 31.6 all-gather.5
  186.8 37.9 reduce-scatter.1
  227.2 30.8 all-gather.7

commit v18 on v17

--- a/solution.py
+++ b/solution.py
@@ -278,7 +278,7 @@
     ffn_own = lax.psum_scatter(partial, "req", scatter_dimension=0, tiled=True)
     layer_output, next_normed = finish_rows(residual_mid, ffn_own, next_gain)
     projected_cols = project_rows(
-        lax.all_gather(next_normed, "req", axis=0, tiled=True), qkv_weight, 256
+        lax.all_gather(next_normed, "req", axis=0, tiled=True), qkv_weight, 512
     )
     n_req = lax.axis_size("req")
     col_w = projected_cols.shape[1]

time: 325 us -> 324 us (level)
  no operation moved by 1% of the time
where the time goes in v18:
time: 324 us
  waiting for transfers between devices  248 us (77%)
  Pallas kernels  36.6 us (11%)
  between operations  15.3 us (5%)
  starting transfers between devices  10.8 us (3%)
  local copies, waits for them, and re-layouts  8.17 us (3%)
  other arithmetic  5.21 us (2%)
    all_gather x1, waiting for transfers between devices, body(): all_kv = lax.all_gather(own_kv, 'tok', axis=0, tiled=True)  111 us
    reduce_scatter x1, waiting for transfers between devices, body(): ffn_own = lax.psum_scatter(partial, 'req', scatter_dimension=0, tiled=True)  38 us
    all_gather x1, waiting for transfers between devices, body(): gathered = lax.all_gather(residual_mid, 'req', axis=0, tiled=True)  31.8 us
    all_gather x1, waiting for transfers between devices, body(): lax.all_gather(next_normed, 'req', axis=0, tiled=True)  31 us
    all_to_all x1, waiting for transfers between devices, body(): lax.all_to_all(projected_cols.reshape(n_req, row_count, col_w), 'req', 0,...  20.1 us
    all_to_all x1, waiting for transfers between devices, body(): lax.all_to_all(outgoing, 'tok', split_axis=0, concat_axis=0, tiled=True)  15.5 us
    pallas_call x1, Pallas kernels, ffn_partial(): pl.pallas_call(ffn_kernel, out_shape=jax.ShapeDtypeStruct((count, width),...  14.2 us
    pallas_call x1, Pallas kernels, window_attention(): pl.pallas_call(functools.partial(attention_kernel, back, head_w // 2), ou...  14 us
  transfers between devices with their start and end apart: 6, of which 6 were waited for; matrix products, arithmetic and copies ran while one was open for 2% of the time, Pallas kernels for 0%

profile of v18, /device:TPU:0, one launch (start us, length us, event | category | flops | bytes accessed | tf_op | source)
XLA Modules:
  0.0 323.7 jit_solution(379050497787871768)
XLA Ops:
  7.2 2.3 pad_maximum_fusion
  9.6 0.6 multiply_reduce_fusion
  11.6 0.7 dynamic-slice_bitcast_fusion.1
  12.2 0.7 copy.22.qseg_ref
  13.0 0.6 pad_add_fusion.scalars_ref
  13.6 111.1 %all-gather.4.cloned.1.call-done.k_ref.v_ref = bf16[2048,4096]{1,0:T(8,128)(2,1)} async-done(((bf16[128,4096]{1,0:T(8,128)(2,1)}), bf16[2048,4096]{1,0:T(8,128)(2,1)}) %all-gather.4.cloned.1.call-update) | async-done | bytes 16777232 | tf_op jit(solution)/shard_map/all_gather | solution.py:272
  124.7 14.0 %shard_map.166.mid_ref = bf16[128,2048]{1,0:T(8,128)(2,1)} custom-call(s32[2]{0:T(128)} %pad_add_fusion.scalars_ref, f32[1]{0:T(128)} %bitcast.2.lam_ref, bf16[128,2048]{1,0:T(8,128)(2,1)} %q_ref.1, bf16[2048,4096]{1,0:T(8,128)(2,1)} %all-gather.4.cloned.1.call-done.k_ref.v_ref, bf16[2048,4096]{1,0:T(8,128)(2,1)} %all-gather.4.cloned.1.call-done.k_ref.v_ref, ...), custom_call_target="tpu_custom_call" | custom-call | flops 2885681152 | bytes 26738688 | tf_op jit(solution)/shard_map/pallas_call | solution.py:94
  138.7 31.8 %all-gather.6.cloned.1.call-done.x_ref = bf16[1024,2048]{1,0:T(8,128)(2,1)} async-done(((bf16[128,2048]{1,0:T(8,128)(2,1)}), bf16[1024,2048]{1,0:T(8,128)(2,1)}) %all-gather.6.cloned.1.call-update) | async-done | bytes 4194320 | tf_op jit(solution)/shard_map/all_gather | solution.py:276
  170.6 1.8 copy-done.2
  172.4 14.2 %shard_map.167 = bf16[1024,2048]{1,0:T(8,128)(2,1)} custom-call(bf16[1024,2048]{1,0:T(8,128)(2,1)} %all-gather.6.cloned.1.call-done.x_ref, f32[1,2048]{1,0:T(1,128)S(1)} %bitcast.29, bf16[704,2048]{1,0:T(8,128)(2,1)S(1)} %bitcast.27, bf16[704,2048]{1,0:T(8,128)(2,1)S(1)} %bitcast.28, bf16[704,2048]{1,0:T(8,128)(2,1)} %down_hbm.1), custom_call_target="tpu_custom_call" | custom-call | flops 8858370048 | bytes 17039360 | tf_op jit(solution)/shard_map/pallas_call | solution.py:159
  186.6 0.0 all-gather.8.cloned.1.call-start
  186.7 38.0 %reduce-scatter.2.cloned.1.call-done.ffn_ref = bf16[128,2048]{1,0:T(8,128)(2,1)} async-done(((bf16[1024,2048]{1,0:T(8,128)(2,1)}), bf16[128,2048]{1,0:T(8,128)(2,1)}) %reduce-scatter.2.cloned.1.call-update) | async-done | bytes 524304 | tf_op jit(solution)/shard_map/reduce_scatter | solution.py:278
  224.7 2.3 shard_map.168
  227.1 31.0 %all-gather.8.cloned.1.call-done.x_ref = bf16[1024,2048]{1,0:T(8,128)(2,1)} async-done(((bf16[128,2048]{1,0:T(8,128)(2,1)}), bf16[1024,2048]{1,0:T(8,128)(2,1)}) %all-gather.8.cloned.1.call-update) | async-done | bytes 4194320 | tf_op jit(solution)/shard_map/all_gather | solution.py:281
  258.1 6.1 %shard_map.169 = bf16[1024,768]{1,0:T(8,128)(2,1)} custom-call(bf16[1024,2048]{1,0:T(8,128)(2,1)} %all-gather.8.cloned.1.call-done.x_ref, bf16[2048,768]{1,0:T(8,128)(2,1)S(1)} %copy-done), custom_call_target="tpu_custom_call" | custom-call | flops 3221225472 | bytes 8912896 | tf_op jit(solution)/shard_map/pallas_call | solution.py:195
  264.2 3.7 %all-to-all-start = ((bf16[8,128,768]{2,1,0:T(8,128)(2,1)}), bf16[8,128,768]{2,1,0:T(8,128)(2,1)S(1)}, u32[]{:S(2)}, u32[]{:S(2)}) async-start(bf16[8,128,768]{2,1,0:T(8,128)(2,1)} %bitcast.8), calls=%async_computation.1 | async-start | bytes 3145728 | tf_op jit(solution)/shard_map/all_to_all | solution.py:285
  267.9 0.5 broadcast.63
  268.4 0.7 reduce.8
  269.1 0.1 reshape_squeeze.6
  269.2 0.1 select_reduce_fusion.2
  269.3 20.1 %all-to-all-done = bf16[8,128,768]{2,1,0:T(8,128)(2,1)S(1)} async-done(((bf16[8,128,768]{2,1,0:T(8,128)(2,1)}), bf16[8,128,768]{2,1,0:T(8,128)(2,1)S(1)}, u32[]{:S(2)}, u32[]{:S(2)}) %all-to-all-start) | async-done | bytes 1572896 | tf_op jit(solution)/shard_map/all_to_all | solution.py:285
  289.4 0.2 copy.24
  289.6 0.1 slice_bitcast_fusion
  289.7 1.6 gather_fusion
  291.3 6.9 %all-to-all-start.1 = ((bf16[16,1,8,4096]{3,2,1,0:T(8,128)(2,1)}), bf16[16,1,8,4096]{3,2,1,0:T(8,128)(2,1)S(1)}, u32[]{:S(2)}, u32[]{:S(2)}) async-start(bf16[16,1,8,4096]{3,2,1,0:T(8,128)(2,1)} %bitcast.34), calls=%async_computation.2 | async-start | bytes 2097152 | tf_op jit(solution)/shard_map/all_to_all | solution.py:301
  298.2 0.7 reduce.9
  298.9 0.1 reshape_squeeze.7
  299.0 0.1 select_reduce_fusion.1
  299.1 0.1 select_reduce_fusion
  299.2 0.8 slice.28
  300.1 15.5 %all-to-all-done.1 = bf16[16,1,8,4096]{3,2,1,0:T(8,128)(2,1)S(1)} async-done(((bf16[16,1,8,4096]{3,2,1,0:T(8,128)(2,1)}), bf16[16,1,8,4096]{3,2,1,0:T(8,128)(2,1)S(1)}, u32[]{:S(2)}, u32[]{:S(2)}) %all-to-all-start.1) | async-done | bytes 1048608 | tf_op jit(solution)/shard_map/all_to_all | solution.py:301
  315.6 1.6 gather_fusion.1
  (25 shorter events, 0.2 us)
Async XLA Ops:
  7.2 2.4 copy-start.4
  7.2 117.5 %all-gather.4.cloned.1.call-start = ((), (), s32[]{:S(2)}) async-start(), calls=%async_computation.3 | async-start | bytes 17825792 | tf_op jit(solution)/shard_map/all_gather | solution.py:272
  9.5 161.0 %all-gather.6.cloned.1.call-start = ((), (), s32[]{:S(2)}) async-start(), calls=%async_computation.4 | async-start | bytes 4718592 | tf_op jit(solution)/shard_map/all_gather | solution.py:276
  124.7 45.9 %copy-start.1 = (bf16[2048,704]{0,1:T(8,128)(2,1)S(1)}, bf16[2048,704]{0,1:T(8,128)(2,1)}, u32[]{:S(2)}) copy-start(bf16[2048,704]{0,1:T(8,128)(2,1)} %param.23) | copy-start | bytes 8650756
  124.7 45.9 %copy-start.3 = (f32[2048]{0:T(1024)S(1)}, f32[2048]{0:T(1024)}, u32[]{:S(2)}) copy-start(f32[2048]{0:T(1024)} %param.22) | copy-start | bytes 24580
  138.7 86.0 %reduce-scatter.2.cloned.1.call-start = ((), (), s32[]{:S(2)}) async-start(), calls=%async_computation.5 | async-start | bytes 4718592 | tf_op jit(solution)/shard_map/reduce_scatter | solution.py:278
  170.6 1.8 copy-start.2
  186.6 71.5 %copy-start = (bf16[2048,768]{1,0:T(8,128)(2,1)S(1)}, bf16[2048,768]{1,0:T(8,128)(2,1)}, u32[]{:S(2)}) copy-start(bf16[2048,768]{1,0:T(8,128)(2,1)} %w_ref.3) | copy-start | bytes 9437188
  186.6 71.5 %all-gather.8.cloned.1.call-start = ((), (), s32[]{:S(2)}) async-start(), calls=%async_computation.6 | async-start | bytes 4718592 | tf_op jit(solution)/shard_map/all_gather | solution.py:281
  264.2 4.2 %copy-start.5 = (s32[1,256]{1,0:T(1,128)S(1)}, s32[1,256]{1,0:T(1,128)}, u32[]{:S(2)}) copy-start(s32[1,256]{1,0:T(1,128)} %param.28) | copy-start | bytes 3076
  264.2 25.2 %all-to-all-start = ((bf16[8,128,768]{2,1,0:T(8,128)(2,1)}), bf16[8,128,768]{2,1,0:T(8,128)(2,1)S(1)}, u32[]{:S(2)}, u32[]{:S(2)}) async-start(bf16[8,128,768]{2,1,0:T(8,128)(2,1)} %bitcast.8), calls=%async_computation.1 | async-start | bytes 3145728 | tf_op jit(solution)/shard_map/all_to_all | solution.py:285
  289.6 8.6 %copy-start.6 = (s32[1,256]{1,0:T(1,128)S(1)}, s32[1,256]{1,0:T(1,128)}, u32[]{:S(2)}) copy-start(s32[1,256]{1,0:T(1,128)} %param.29) | copy-start | bytes 3076
  291.3 24.3 %all-to-all-start.1 = ((bf16[16,1,8,4096]{3,2,1,0:T(8,128)(2,1)}), bf16[16,1,8,4096]{3,2,1,0:T(8,128)(2,1)S(1)}, u32[]{:S(2)}, u32[]{:S(2)}) async-start(bf16[16,1,8,4096]{3,2,1,0:T(8,128)(2,1)} %bitcast.34), calls=%async_computation.2 | async-start | bytes 2097152 | tf_op jit(solution)/shard_map/all_to_all | solution.py:301
Sparse Core Ops, SparseCore 0:
  10.7 113.9 all-gather.3
  138.8 31.6 all-gather.5
  186.8 37.9 reduce-scatter.1
  227.2 30.8 all-gather.7

commit v19 on v17

--- a/solution.py
+++ b/solution.py
@@ -274,7 +274,7 @@
         q_in, all_kv, query_segs, seg_row, first_row, lambda_mix, back, out_weight, layer_input
     )
     gathered = lax.all_gather(residual_mid, "req", axis=0, tiled=True)
-    partial = ffn_partial(gathered, ffn_gain, gate_weight, up_weight, down_weight, 512)
+    partial = ffn_partial(gathered, ffn_gain, gate_weight, up_weight, down_weight, 1024)
     ffn_own = lax.psum_scatter(partial, "req", scatter_dimension=0, tiled=True)
     layer_output, next_normed = finish_rows(residual_mid, ffn_own, next_gain)
     projected_cols = project_rows(

time: 325 us -> 327 us (level)
  no operation moved by 1% of the time
where the time goes in v19:
time: 327 us; the launch traced here: 326 us
  waiting for transfers between devices  248 us (76%)
  Pallas kernels  39 us (12%)
  between operations  15.3 us (5%)
  starting transfers between devices  10.8 us (3%)
  local copies, waits for them, and re-layouts  8.17 us (2%)
  other arithmetic  5.21 us (2%)
    all_gather x1, waiting for transfers between devices, body(): all_kv = lax.all_gather(own_kv, 'tok', axis=0, tiled=True)  111 us
    reduce_scatter x1, waiting for transfers between devices, body(): ffn_own = lax.psum_scatter(partial, 'req', scatter_dimension=0, tiled=True)  37.9 us
    all_gather x1, waiting for transfers between devices, body(): gathered = lax.all_gather(residual_mid, 'req', axis=0, tiled=True)  31.8 us
    all_gather x1, waiting for transfers between devices, body(): lax.all_gather(next_normed, 'req', axis=0, tiled=True)  31.2 us
    all_to_all x1, waiting for transfers between devices, body(): lax.all_to_all(projected_cols.reshape(n_req, row_count, col_w), 'req', 0,...  20.1 us
    pallas_call x1, Pallas kernels, ffn_partial(): pl.pallas_call(ffn_kernel, out_shape=jax.ShapeDtypeStruct((count, width),...  16.3 us
    all_to_all x1, waiting for transfers between devices, body(): lax.all_to_all(outgoing, 'tok', split_axis=0, concat_axis=0, tiled=True)  15.5 us
    pallas_call x1, Pallas kernels, window_attention(): pl.pallas_call(functools.partial(attention_kernel, back, head_w // 2), ou...  14 us
  transfers between devices with their start and end apart: 6, of which 6 were waited for; matrix products, arithmetic and copies ran while one was open for 2% of the time, Pallas kernels for 0%

profile of v19, /device:TPU:0, one launch (start us, length us, event | category | flops | bytes accessed | tf_op | source)
XLA Modules:
  0.0 326.1 jit_solution(2931296609396104507)
XLA Ops:
  7.2 2.3 pad_maximum_fusion
  9.5 0.0 all-gather.6.cloned.1.call-start
  9.6 0.6 multiply_reduce_fusion
  11.6 0.7 dynamic-slice_bitcast_fusion.1
  12.2 0.7 copy.22.qseg_ref
  13.0 0.6 pad_add_fusion.scalars_ref
  13.6 111.1 %all-gather.4.cloned.1.call-done.k_ref.v_ref = bf16[2048,4096]{1,0:T(8,128)(2,1)} async-done(((bf16[128,4096]{1,0:T(8,128)(2,1)}), bf16[2048,4096]{1,0:T(8,128)(2,1)}) %all-gather.4.cloned.1.call-update) | async-done | bytes 16777232 | tf_op jit(solution)/shard_map/all_gather | solution.py:272
  124.7 14.0 %shard_map.166.mid_ref = bf16[128,2048]{1,0:T(8,128)(2,1)} custom-call(s32[2]{0:T(128)} %pad_add_fusion.scalars_ref, f32[1]{0:T(128)} %bitcast.2.lam_ref, bf16[128,2048]{1,0:T(8,128)(2,1)} %q_ref.1, bf16[2048,4096]{1,0:T(8,128)(2,1)} %all-gather.4.cloned.1.call-done.k_ref.v_ref, bf16[2048,4096]{1,0:T(8,128)(2,1)} %all-gather.4.cloned.1.call-done.k_ref.v_ref, ...), custom_call_target="tpu_custom_call" | custom-call | flops 2885681152 | bytes 26738688 | tf_op jit(solution)/shard_map/pallas_call | solution.py:94
  138.7 31.8 %all-gather.6.cloned.1.call-done.x_ref = bf16[1024,2048]{1,0:T(8,128)(2,1)} async-done(((bf16[128,2048]{1,0:T(8,128)(2,1)}), bf16[1024,2048]{1,0:T(8,128)(2,1)}) %all-gather.6.cloned.1.call-update) | async-done | bytes 4194320 | tf_op jit(solution)/shard_map/all_gather | solution.py:276
  170.6 1.8 copy-done.2
  172.4 16.3 %shard_map.167 = bf16[1024,2048]{1,0:T(8,128)(2,1)} custom-call(bf16[1024,2048]{1,0:T(8,128)(2,1)} %all-gather.6.cloned.1.call-done.x_ref, f32[1,2048]{1,0:T(1,128)S(1)} %bitcast.29, bf16[704,2048]{1,0:T(8,128)(2,1)S(1)} %bitcast.27, bf16[704,2048]{1,0:T(8,128)(2,1)S(1)} %bitcast.28, bf16[704,2048]{1,0:T(8,128)(2,1)} %down_hbm.1), custom_call_target="tpu_custom_call" | custom-call | flops 8858370048 | bytes 17039360 | tf_op jit(solution)/shard_map/pallas_call | solution.py:159
  188.8 37.9 %reduce-scatter.2.cloned.1.call-done.ffn_ref = bf16[128,2048]{1,0:T(8,128)(2,1)} async-done(((bf16[1024,2048]{1,0:T(8,128)(2,1)}), bf16[128,2048]{1,0:T(8,128)(2,1)}) %reduce-scatter.2.cloned.1.call-update) | async-done | bytes 524304 | tf_op jit(solution)/shard_map/reduce_scatter | solution.py:278
  226.7 2.3 shard_map.168
  229.0 31.2 %all-gather.8.cloned.1.call-done.x_ref = bf16[1024,2048]{1,0:T(8,128)(2,1)} async-done(((bf16[128,2048]{1,0:T(8,128)(2,1)}), bf16[1024,2048]{1,0:T(8,128)(2,1)}) %all-gather.8.cloned.1.call-update) | async-done | bytes 4194320 | tf_op jit(solution)/shard_map/all_gather | solution.py:281
  260.2 6.4 %shard_map.169 = bf16[1024,768]{1,0:T(8,128)(2,1)} custom-call(bf16[1024,2048]{1,0:T(8,128)(2,1)} %all-gather.8.cloned.1.call-done.x_ref, bf16[2048,768]{1,0:T(8,128)(2,1)S(1)} %copy-done), custom_call_target="tpu_custom_call" | custom-call | flops 3221225472 | bytes 8912896 | tf_op jit(solution)/shard_map/pallas_call | solution.py:195
  266.6 3.7 %all-to-all-start = ((bf16[8,128,768]{2,1,0:T(8,128)(2,1)}), bf16[8,128,768]{2,1,0:T(8,128)(2,1)S(1)}, u32[]{:S(2)}, u32[]{:S(2)}) async-start(bf16[8,128,768]{2,1,0:T(8,128)(2,1)} %bitcast.8), calls=%async_computation.1 | async-start | bytes 3145728 | tf_op jit(solution)/shard_map/all_to_all | solution.py:285
  270.3 0.5 broadcast.63
  270.8 0.7 reduce.8
  271.5 0.1 reshape_squeeze.6
  271.6 0.1 select_reduce_fusion.2
  271.7 20.1 %all-to-all-done = bf16[8,128,768]{2,1,0:T(8,128)(2,1)S(1)} async-done(((bf16[8,128,768]{2,1,0:T(8,128)(2,1)}), bf16[8,128,768]{2,1,0:T(8,128)(2,1)S(1)}, u32[]{:S(2)}, u32[]{:S(2)}) %all-to-all-start) | async-done | bytes 1572896 | tf_op jit(solution)/shard_map/all_to_all | solution.py:285
  291.8 0.2 copy.24
  292.0 0.1 slice_bitcast_fusion
  292.1 1.6 gather_fusion
  293.7 6.9 %all-to-all-start.1 = ((bf16[16,1,8,4096]{3,2,1,0:T(8,128)(2,1)}), bf16[16,1,8,4096]{3,2,1,0:T(8,128)(2,1)S(1)}, u32[]{:S(2)}, u32[]{:S(2)}) async-start(bf16[16,1,8,4096]{3,2,1,0:T(8,128)(2,1)} %bitcast.34), calls=%async_computation.2 | async-start | bytes 2097152 | tf_op jit(solution)/shard_map/all_to_all | solution.py:301
  300.6 0.7 reduce.9
  301.3 0.1 reshape_squeeze.7
  301.4 0.1 select_reduce_fusion.1
  301.5 0.1 select_reduce_fusion
  301.7 0.8 slice.28
  302.5 15.5 %all-to-all-done.1 = bf16[16,1,8,4096]{3,2,1,0:T(8,128)(2,1)S(1)} async-done(((bf16[16,1,8,4096]{3,2,1,0:T(8,128)(2,1)}), bf16[16,1,8,4096]{3,2,1,0:T(8,128)(2,1)S(1)}, u32[]{:S(2)}, u32[]{:S(2)}) %all-to-all-start.1) | async-done | bytes 1048608 | tf_op jit(solution)/shard_map/all_to_all | solution.py:301
  318.0 1.6 gather_fusion.1
  (25 shorter events, 0.2 us)
Async XLA Ops:
  7.2 2.4 copy-start.4
  7.2 117.5 %all-gather.4.cloned.1.call-start = ((), (), s32[]{:S(2)}) async-start(), calls=%async_computation.3 | async-start | bytes 17825792 | tf_op jit(solution)/shard_map/all_gather | solution.py:272
  9.5 161.0 %all-gather.6.cloned.1.call-start = ((), (), s32[]{:S(2)}) async-start(), calls=%async_computation.4 | async-start | bytes 4718592 | tf_op jit(solution)/shard_map/all_gather | solution.py:276
  124.7 45.9 %copy-start.1 = (bf16[2048,704]{0,1:T(8,128)(2,1)S(1)}, bf16[2048,704]{0,1:T(8,128)(2,1)}, u32[]{:S(2)}) copy-start(bf16[2048,704]{0,1:T(8,128)(2,1)} %param.23) | copy-start | bytes 8650756
  124.7 45.9 %copy-start.3 = (f32[2048]{0:T(1024)S(1)}, f32[2048]{0:T(1024)}, u32[]{:S(2)}) copy-start(f32[2048]{0:T(1024)} %param.22) | copy-start | bytes 24580
  138.7 88.0 %reduce-scatter.2.cloned.1.call-start = ((), (), s32[]{:S(2)}) async-start(), calls=%async_computation.5 | async-start | bytes 4718592 | tf_op jit(solution)/shard_map/reduce_scatter | solution.py:278
  170.6 1.8 copy-start.2
  188.7 71.5 %copy-start = (bf16[2048,768]{1,0:T(8,128)(2,1)S(1)}, bf16[2048,768]{1,0:T(8,128)(2,1)}, u32[]{:S(2)}) copy-start(bf16[2048,768]{1,0:T(8,128)(2,1)} %w_ref.3) | copy-start | bytes 9437188
  188.7 71.5 %all-gather.8.cloned.1.call-start = ((), (), s32[]{:S(2)}) async-start(), calls=%async_computation.6 | async-start | bytes 4718592 | tf_op jit(solution)/shard_map/all_gather | solution.py:281
  266.6 4.2 %copy-start.5 = (s32[1,256]{1,0:T(1,128)S(1)}, s32[1,256]{1,0:T(1,128)}, u32[]{:S(2)}) copy-start(s32[1,256]{1,0:T(1,128)} %param.28) | copy-start | bytes 3076
  266.6 25.2 %all-to-all-start = ((bf16[8,128,768]{2,1,0:T(8,128)(2,1)}), bf16[8,128,768]{2,1,0:T(8,128)(2,1)S(1)}, u32[]{:S(2)}, u32[]{:S(2)}) async-start(bf16[8,128,768]{2,1,0:T(8,128)(2,1)} %bitcast.8), calls=%async_computation.1 | async-start | bytes 3145728 | tf_op jit(solution)/shard_map/all_to_all | solution.py:285
  292.0 8.6 %copy-start.6 = (s32[1,256]{1,0:T(1,128)S(1)}, s32[1,256]{1,0:T(1,128)}, u32[]{:S(2)}) copy-start(s32[1,256]{1,0:T(1,128)} %param.29) | copy-start | bytes 3076
  293.7 24.3 %all-to-all-start.1 = ((bf16[16,1,8,4096]{3,2,1,0:T(8,128)(2,1)}), bf16[16,1,8,4096]{3,2,1,0:T(8,128)(2,1)S(1)}, u32[]{:S(2)}, u32[]{:S(2)}) async-start(bf16[16,1,8,4096]{3,2,1,0:T(8,128)(2,1)} %bitcast.34), calls=%async_computation.2 | async-start | bytes 2097152 | tf_op jit(solution)/shard_map/all_to_all | solution.py:301
Sparse Core Ops, SparseCore 0:
  10.7 113.9 all-gather.3
  138.8 31.6 all-gather.5
  188.8 37.7 reduce-scatter.1
  229.1 31.0 all-gather.7
